TPU v7x, 32 devices: a whole 2x2x4 slice. The times are simulated.
32 devices in a mesh: dp: 2 (over x), fsdp: 16 (over z, y, core).
Axes of the slice: x: 2, y: 2, z: 4, core: 2. Of those that a mesh axis runs over, the one named last changes fastest.
Arguments:
- tokens: bfloat16 [18432, 768], P(('dp', 'fsdp')), may hold values from -6 to 6
- gain_attn: bfloat16 [768], P(('dp', 'fsdp')), may hold values from 0.25 to 1.75
- w_qkv: bfloat16 [768, 2304], P(('dp', 'fsdp')), may hold values from -0.21875 to 0.21875
- w_proj: bfloat16 [768, 768], P(('dp', 'fsdp')), may hold values from -2.5 to 2.5
- gain_moe: bfloat16 [768], P(('dp', 'fsdp')), may hold values from 0.25 to 1.75
- w_router: bfloat16 [768, 8], P(('dp', 'fsdp')), may hold values from -0.15625 to 0.15625
- w_in: bfloat16 [8, 768, 3072], P('dp', 'fsdp'), may hold values from -0.21875 to 0.21875
- w_out: bfloat16 [8, 3072, 768], P('dp', 'fsdp'), may hold values from -0.875 to 0.875
- routes: int32 [18432, 2], P(('dp', 'fsdp')), may hold values from 0 to 7, as said below
- slot_ids: int32 [18432, 2], P(('dp', 'fsdp')), may hold values from 0 to 152, as said below
- cotangent: bfloat16 [18432, 768], P(('dp', 'fsdp')), may hold values from -6 to 6
Outputs:
- output: bfloat16 [18432, 768], P(('dp', 'fsdp'))
- grad_tokens: float32 [18432, 768], P(('dp', 'fsdp'))
- d_gain_attn: float32 [768], P(('dp', 'fsdp'))
- d_qkv: float32 [768, 2304], P(('dp', 'fsdp'))
- d_proj: float32 [768, 768], P(('dp', 'fsdp'))
- d_gain_moe: float32 [768], P(('dp', 'fsdp'))
- d_router: float32 [768, 8], P(('dp', 'fsdp'))
- d_in: float32 [8, 768, 3072], P('dp', 'fsdp')
- d_out: float32 [8, 3072, 768], P('dp', 'fsdp')
Inputs may be any that keep to these rules, and one draw needn't show every extreme that they name: `routes`: each row names two different experts. `slot_ids`: among the 576 patches of one device, the pairs routed to one expert hold the distinct slots 0, 1, 2, ... in some priority order; a pair beyond the 152 slots holds 152 and is dropped. On every device some expert gets more than 152 pairs.
All inputs are finite; a program needn't handle non-finite values.
Results may differ from a plain program's by a relative error of at most 0.017.
Values may be sent and summed in bfloat16 or wider, within the bound.
No kernel may reach another device: no remote copies, remote signals or barrier semaphores. Data moves between devices by JAX's collectives and lax.ppermute only.
A program may use at most 320 MiB of HBM per device.

v0:
```python
import jax
import jax.numpy as jnp
from jax import lax
from jax.sharding import PartitionSpec as P

HEADS = 12
HEAD_DIM = 64
EXPERTS = 8
SEQ = 576
CAP = 152


norm_epsilon = 1e-06


def norm_parts(values):
    centre = values - jnp.mean(values, axis=-1, keepdims=True)
    inverse = lax.rsqrt(jnp.mean(centre * centre, axis=-1, keepdims=True) + norm_epsilon)
    return (centre * inverse, inverse)


def norm_back(grad_normed, normed, inverse):
    mean_grad = jnp.mean(grad_normed, axis=-1, keepdims=True)
    mean_cross = jnp.mean(grad_normed * normed, axis=-1, keepdims=True)
    return (grad_normed - mean_grad - normed * mean_cross) * inverse


def gelu_tanh(values):
    return jax.nn.gelu(values, approximate=True)


def head_forward(operands):
    queries, keys_head, values_head = operands
    scores = jnp.einsum(
        "isd,itd->ist", queries, keys_head, preferred_element_type=jnp.float32
    ) * HEAD_DIM ** (-0.5)
    largest = jnp.max(scores, axis=-1, keepdims=True)
    powers = jnp.exp(scores - largest)
    totals = jnp.sum(powers, axis=-1, keepdims=True)
    attn_probs = (powers / totals).astype(jnp.bfloat16)
    head_out = jnp.einsum(
        "ist,itd->isd", attn_probs, values_head, preferred_element_type=jnp.float32
    )
    return (head_out.astype(jnp.bfloat16), (largest + jnp.log(totals))[..., 0])


def head_backward(operands):
    queries, keys_head, values_head, grad_head, log_total = operands
    scores = jnp.einsum(
        "isd,itd->ist", queries, keys_head, preferred_element_type=jnp.float32
    ) * HEAD_DIM ** (-0.5)
    attn_probs = jnp.exp(scores - log_total[..., None])
    grad_probs = jnp.einsum(
        "isd,itd->ist", grad_head, values_head, preferred_element_type=jnp.float32
    )
    row_terms = jnp.sum(attn_probs * grad_probs, axis=-1, keepdims=True)
    grad_scores = (attn_probs * (grad_probs - row_terms)).astype(jnp.bfloat16)
    grad_query = jnp.einsum(
        "ist,itd->isd", grad_scores, keys_head, preferred_element_type=jnp.float32
    ) * HEAD_DIM ** (-0.5)
    grad_key = jnp.einsum(
        "ist,isd->itd", grad_scores, queries, preferred_element_type=jnp.float32
    ) * HEAD_DIM ** (-0.5)
    grad_value = jnp.einsum(
        "ist,isd->itd",
        attn_probs.astype(jnp.bfloat16),
        grad_head,
        preferred_element_type=jnp.float32,
    )
    return (grad_query, grad_key, grad_value)


def expert_forward(expert_rows, w_up, w_down):
    pre_act = jnp.einsum("ecd,edf->ecf", expert_rows, w_up, preferred_element_type=jnp.float32)
    hidden = gelu_tanh(pre_act).astype(jnp.bfloat16)
    result = jnp.einsum("ecf,efd->ecd", hidden, w_down, preferred_element_type=jnp.float32).astype(
        jnp.bfloat16
    )
    return (pre_act, hidden, result)


def expert_backward(expert_rows, pre_act, hidden, grad_result, w_up, w_down):
    grad_hidden = jnp.einsum(
        "ecd,efd->ecf", grad_result, w_down, preferred_element_type=jnp.float32
    )
    ignored, pull_back = jax.vjp(gelu_tanh, pre_act)
    grad_pre = pull_back(grad_hidden)[0].astype(jnp.bfloat16)
    grad_down = jnp.einsum("ecf,ecd->efd", hidden, grad_result, preferred_element_type=jnp.float32)
    grad_up = jnp.einsum("ecd,ecf->edf", expert_rows, grad_pre, preferred_element_type=jnp.float32)
    grad_rows = jnp.einsum(
        "ecf,edf->ecd", grad_pre, w_up, preferred_element_type=jnp.float32
    ).astype(jnp.bfloat16)
    return (grad_up, grad_down, grad_rows)


def gather_dense(gain_attn, w_qkv, w_proj, gain_moe, w_router):
    return (
        lax.all_gather(gain_attn, ("dp", "fsdp"), axis=0, tiled=True),
        lax.all_gather(w_qkv, ("dp", "fsdp"), axis=0, tiled=True),
        lax.all_gather(w_proj, ("dp", "fsdp"), axis=0, tiled=True),
        lax.all_gather(gain_moe, ("dp", "fsdp"), axis=0, tiled=True),
        lax.all_gather(w_router, ("dp", "fsdp"), axis=0, tiled=True),
    )


def gather_experts(w_in, w_out):
    local_pair = (w_in, w_out)
    return (
        lax.all_gather(local_pair[0], "fsdp", axis=1, tiled=True),
        lax.all_gather(local_pair[1], "fsdp", axis=1, tiled=True),
    )


def reduce_experts(grad_up, grad_down):
    reduced = (
        lax.psum_scatter(
            grad_up.astype(jnp.bfloat16), "fsdp", scatter_dimension=1, tiled=True
        ).astype(jnp.float32),
        lax.psum_scatter(
            grad_down.astype(jnp.bfloat16), "fsdp", scatter_dimension=1, tiled=True
        ).astype(jnp.float32),
    )
    return reduced


def per_device(
    tokens, gain_attn, w_qkv, w_proj, gain_moe, w_router, w_in, w_out, routes, slot_ids, cotangent
):
    dense_full = gather_dense(gain_attn, w_qkv, w_proj, gain_moe, w_router)
    expert_weights = gather_experts(w_in, w_out)
    rows_here = tokens.shape[0]
    images = rows_here // SEQ
    residual = tokens.astype(jnp.float32)
    normed_one, inverse_one = norm_parts(residual)
    gain_one = dense_full[0].astype(jnp.float32)
    act_one = (normed_one * gain_one).astype(jnp.bfloat16)
    qkv = jnp.dot(act_one, dense_full[1], preferred_element_type=jnp.float32).astype(jnp.bfloat16)
    split_qkv = qkv.reshape(images, SEQ, 3, HEADS, HEAD_DIM).transpose(2, 3, 0, 1, 4)
    head_out, head_lse = lax.map(head_forward, (split_qkv[0], split_qkv[1], split_qkv[2]))
    attended = head_out.transpose(1, 2, 0, 3).reshape(rows_here, -1)
    resid_mid = residual + jnp.dot(attended, dense_full[2], preferred_element_type=jnp.float32)
    normed_two, inverse_two = norm_parts(resid_mid)
    gain_two = dense_full[3].astype(jnp.float32)
    act_two = (normed_two * gain_two).astype(jnp.bfloat16)
    logits = jnp.dot(act_two, dense_full[4], preferred_element_type=jnp.float32)
    router = jax.nn.softmax(logits, axis=-1)
    expert_ids = lax.broadcasted_iota(jnp.int32, (1, 1, EXPERTS), 2)
    chosen = routes[:, :, None] == expert_ids
    gate_values = jnp.sum(jnp.where(chosen, router[:, None, :], 0.0), axis=-1)
    gates_low = gate_values.astype(jnp.bfloat16)
    slot_count = EXPERTS * CAP
    columns = lax.broadcasted_iota(jnp.int32, (1, 1, slot_count), 2)
    live_pair = slot_ids < CAP
    targets = routes * CAP + slot_ids
    matches = (targets[:, :, None] == columns) & live_pair[:, :, None]
    dispatch = jnp.sum(matches.astype(jnp.bfloat16), axis=1)
    combine = jnp.sum(
        jnp.where(matches, gates_low[:, :, None], jnp.zeros((), jnp.bfloat16)), axis=1
    )
    slot_rows = (
        jnp.einsum("tx,td->xd", dispatch, act_two, preferred_element_type=jnp.float32)
        .astype(jnp.bfloat16)
        .reshape(EXPERTS, CAP, -1)
    )
    expert_rows = lax.all_to_all(slot_rows, "dp", split_axis=0, concat_axis=1, tiled=True)
    pre_act, hidden, result = expert_forward(expert_rows, expert_weights[0], expert_weights[1])
    slot_result = lax.all_to_all(result, "dp", split_axis=1, concat_axis=0, tiled=True)
    flat_result = slot_result.reshape(slot_count, -1)
    moe_sum = jnp.einsum("tx,xd->td", combine, flat_result, preferred_element_type=jnp.float32)
    output = (resid_mid + moe_sum).astype(jnp.bfloat16)
    dense_full = gather_dense(gain_attn, w_qkv, w_proj, gain_moe, w_router)
    expert_weights = gather_experts(w_in, w_out)
    grad_slots = (
        jnp.einsum("tx,td->xd", combine, cotangent, preferred_element_type=jnp.float32)
        .astype(jnp.bfloat16)
        .reshape(EXPERTS, CAP, -1)
    )
    picked = flat_result[jnp.clip(targets, 0, slot_count - 1)]
    grad_gates = jnp.where(
        live_pair,
        jnp.einsum("tkd,td->tk", picked, cotangent, preferred_element_type=jnp.float32),
        0.0,
    )
    grad_router = jnp.sum(jnp.where(chosen, grad_gates[:, :, None], 0.0), axis=1)
    grad_logits = (
        router * (grad_router - jnp.sum(router * grad_router, axis=-1, keepdims=True))
    ).astype(jnp.bfloat16)
    d_router = jnp.einsum("td,te->de", act_two, grad_logits, preferred_element_type=jnp.float32)
    grad_act_two = jnp.einsum(
        "te,de->td", grad_logits, dense_full[4], preferred_element_type=jnp.float32
    )
    grad_expert = lax.all_to_all(grad_slots, "dp", split_axis=0, concat_axis=1, tiled=True)
    grad_up, grad_down, grad_rows = expert_backward(
        expert_rows, pre_act, hidden, grad_expert, expert_weights[0], expert_weights[1]
    )
    grad_rows = lax.all_to_all(grad_rows, "dp", split_axis=1, concat_axis=0, tiled=True)
    grad_act_two = grad_act_two + jnp.einsum(
        "tx,xd->td", dispatch, grad_rows.reshape(slot_count, -1), preferred_element_type=jnp.float32
    )
    d_gain_moe = jnp.sum(grad_act_two * normed_two, axis=0)
    grad_mid = cotangent.astype(jnp.float32) + norm_back(
        grad_act_two * gain_two, normed_two, inverse_two
    )
    grad_mid_low = grad_mid.astype(jnp.bfloat16)
    d_proj = jnp.einsum("td,te->de", attended, grad_mid_low, preferred_element_type=jnp.float32)
    grad_attended = jnp.einsum(
        "te,de->td", grad_mid_low, dense_full[2], preferred_element_type=jnp.float32
    ).astype(jnp.bfloat16)
    grad_heads = grad_attended.reshape(images, SEQ, HEADS, HEAD_DIM).transpose(2, 0, 1, 3)
    grad_query, grad_key, grad_value = lax.map(
        head_backward, (split_qkv[0], split_qkv[1], split_qkv[2], grad_heads, head_lse)
    )
    grad_qkv = (
        jnp.stack([grad_query, grad_key, grad_value])
        .transpose(2, 3, 0, 1, 4)
        .reshape(rows_here, -1)
        .astype(jnp.bfloat16)
    )
    d_qkv = jnp.einsum("td,te->de", act_one, grad_qkv, preferred_element_type=jnp.float32)
    grad_act_one = jnp.einsum(
        "te,de->td", grad_qkv, dense_full[1], preferred_element_type=jnp.float32
    )
    d_gain_attn = jnp.sum(grad_act_one * normed_one, axis=0)
    grad_tokens = grad_mid + norm_back(grad_act_one * gain_one, normed_one, inverse_one)
    dense_grads = (
        lax.psum_scatter(d_gain_attn, ("dp", "fsdp"), scatter_dimension=0, tiled=True),
        lax.psum_scatter(d_qkv, ("dp", "fsdp"), scatter_dimension=0, tiled=True),
        lax.psum_scatter(d_proj, ("dp", "fsdp"), scatter_dimension=0, tiled=True),
        lax.psum_scatter(d_gain_moe, ("dp", "fsdp"), scatter_dimension=0, tiled=True),
        lax.psum_scatter(d_router, ("dp", "fsdp"), scatter_dimension=0, tiled=True),
    )
    expert_grads = reduce_experts(grad_up, grad_down)
    return (
        output,
        grad_tokens,
        dense_grads[0],
        dense_grads[1],
        dense_grads[2],
        dense_grads[3],
        dense_grads[4],
        expert_grads[0],
        expert_grads[1],
    )


def solution(mesh):
    in_specs = (
        P(("dp", "fsdp"), None),
        P(("dp", "fsdp")),
        P(("dp", "fsdp"), None),
        P(("dp", "fsdp"), None),
        P(("dp", "fsdp")),
        P(("dp", "fsdp"), None),
        P("dp", "fsdp", None),
        P("dp", "fsdp", None),
        P(("dp", "fsdp"), None),
        P(("dp", "fsdp"), None),
        P(("dp", "fsdp"), None),
    )
    out_specs = (
        P(("dp", "fsdp"), None),
        P(("dp", "fsdp"), None),
        P(("dp", "fsdp")),
        P(("dp", "fsdp"), None),
        P(("dp", "fsdp"), None),
        P(("dp", "fsdp")),
        P(("dp", "fsdp"), None),
        P("dp", "fsdp", None),
        P("dp", "fsdp", None),
    )
    return jax.shard_map(
        per_device, mesh=mesh, in_specs=in_specs, out_specs=out_specs, check_vma=False
    )
```

profile of v0, /device:TPU:0, one launch (start us, length us, event | category | flops | bytes accessed | tf_op | source)
XLA Modules:
  0.0 1001.7 jit_solution(7998535637937780949)
XLA Ops:
  10.6 42.0 %all-reduce.6 = (bf16[768]{0:T(1024)(128)(2,1)S(1)}, bf16[768]{0:T(1024)(128)(2,1)S(1)}) all-reduce(bf16[768]{0:T(1024)(128)(2,1)S(1)} %dynamic-update-slice, bf16[768]{0:T(1024)(128)(2,1)S(1)} %dynamic-update-slice.1), channel_id=1, replica_groups=mesh['dp'=2,'fsdp'=16] {'dp','fsdp'}, use_global_device_ids=true, to_apply=%add | all-reduce | flops 1536 | bytes 6144
  52.6 40.8 %all-gather = bf16[32,24,8]{1,2,0:T(8,128)(2,1)S(1)} all-gather(bf16[1,24,8]{1,2,0:T(8,128)(2,1)S(1)} %bitcast.199), channel_id=1, replica_groups=mesh['dp'=2,'fsdp'=16] {'dp','fsdp'}, dimensions={0}, use_global_device_ids=true | all-gather | bytes 12672 | tf_op jit(solution)/shard_map/all_gather | solution.py:102
  95.4 5.9 convolution_convert_fusion.3
  113.4 37.9 %while.26 = (s32[]{:T(128)}, bf16[12,1,576,64]{2,3,1,0:T(8,128)(2,1)}, f32[12,1,576]{2,1,0:T(1,128)}, bf16[12,1,576,64]{3,2,1,0:T(8,128)(2,1)S(1)}, bf16[12,1,57...) while((s32[]{:T(128)}, bf16[12,1,576,64]{2,3,1,0:T(8,128)(2,1)}, ...), condition=%wide.region_5.6_spmd, body=%wide.region_2.5_spmd.sunk | while | flops 87293376 | bytes 4531033 | solution.py:139
  171.9 18.5 %all-to-all-done.2 = bf16[8,152,768]{2,1,0:T(8,128)(2,1)S(1)} async-done(((bf16[8,152,768]{2,1,0:T(8,128)(2,1)}), bf16[8,152,768]{2,1,0:T(8,128)(2,1)S(1)}, u32[]{:S(2)}, u32[]{:S(2)}) %all-to-all-start.2) | async-done | bytes 1867808 | tf_op jit(solution)/shard_map/all_to_all | solution.py:192
  198.6 20.2 %all-to-all-done = bf16[8,152,768]{2,1,0:T(8,128)(2,1)} async-done(((bf16[8,152,768]{2,1,0:T(8,128)(2,1)}), bf16[8,152,768]{2,1,0:T(8,128)(2,1)}, u32[]{:S(2)}, u32[]{:S(2)}) %all-to-all-start) | async-done | bytes 1867808 | tf_op jit(solution)/shard_map/all_to_all | solution.py:165
  221.7 7.1 all-gather.12.cloned.1.call-done
  228.8 12.9 %fusion.77 = f32[4,304,3072]{2,1,0:T(8,128)} fusion(bf16[4,304,768]{2,1,0:T(8,128)(2,1)S(1)} %bitcast.182, bf16[4,3072,768]{2,1,0:T(8,128)(2,1)} %all-gather.12.cloned.1.call-done), kind=kOutput, calls=%fused_computation.141 | convolution fusion | flops 5737807872 | bytes 35684352 | tf_op jit(solution)/shard_map/ecd,efd->ecf/dot_general | solution.py:83
  241.7 87.4 %all-gather.10.cloned.1.call-done = bf16[4,768,3072]{2,1,0:T(8,128)(2,1)} async-done(((bf16[4,48,3072]{2,1,0:T(8,128)(2,1)}), bf16[4,768,3072]{2,1,0:T(8,128)(2,1)}) %all-gather.10.cloned.1.call-update) | async-done | bytes 18874384 | tf_op jit(solution)/shard_map/all_gather | solution.py:109
  329.1 26.9 %fusion.43 = (bf16[4,304,3072]{2,1,0:T(8,128)(2,1)}, f32[4,304,3072]{2,1,0:T(8,128)}) fusion(f32[4,304,3072]{2,1,0:T(8,128)} %fusion.77, bf16[4,304,768]{2,1,0:T(8,128)(2,1)} %bitcast.192, bf16[4,768,3072]{2,1,0:T(8,128)(2,1)} %all-gather.10.cloned.1.call-done), kind=kOutput, calls=%fused_computation.59 | convolution fusion | flops 5812518912 | bytes 58097664 | tf_op jit(solution)/shard_map/ecd,edf->ecf/dot_general | solution.py:74
  356.0 16.5 %convolution_convert_fusion.2 = bf16[4,768,3072]{2,1,0:T(8,128)(2,1)} fusion(bf16[4,304,768]{2,1,0:T(8,128)(2,1)} %bitcast.193, bf16[4,304,3072]{2,1,0:T(8,128)(2,1)} %get-tuple-element.212), kind=kOutput, calls=%fused_computation.62 | convolution fusion | flops 5747245056 | bytes 28213248 | tf_op jit(solution)/shard_map/ecd,ecf->edf/dot_general | solution.py:89
  372.8 20.0 %convolution_convert_fusion.1 = bf16[4,3072,768]{2,1,0:T(8,128)(2,1)} fusion(bf16[4,304,768]{2,1,0:T(8,128)(2,1)S(1)} %bitcast.183, f32[4,304,3072]{2,1,0:T(8,128)} %get-tuple-element.213), kind=kOutput, calls=%fused_computation.61 | convolution fusion | flops 5780865024 | bytes 35684352 | tf_op jit(solution)/shard_map/ecf,ecd->efd/dot_general | solution.py:88
  392.9 19.3 %convolution_convert_fusion.7 = bf16[4,304,768]{2,1,0:T(8,128)(2,1)S(1)} fusion(bf16[4,3072,768]{2,1,0:T(8,128)(2,1)} %all-gather.12.cloned.1.call-done, f32[4,304,3072]{2,1,0:T(8,128)} %get-tuple-element.213), kind=kOutput, calls=%fused_computation.85 | convolution fusion | flops 5772361728 | bytes 35684352 | tf_op jit(solution)/shard_map/ecf,efd->ecd/dot_general | solution.py:76
  418.4 13.2 %convolution_convert_fusion.6 = bf16[4,304,768]{2,1,0:T(8,128)(2,1)} fusion(bf16[4,304,3072]{2,1,0:T(8,128)(2,1)} %get-tuple-element.212, bf16[4,768,3072]{2,1,0:T(8,128)(2,1)} %all-gather.10.cloned.1.call-done), kind=kOutput, calls=%fused_computation.84 | convolution fusion | flops 5738741760 | bytes 28213248 | tf_op jit(solution)/shard_map/ecf,edf->ecd/dot_general | solution.py:90
  435.3 6.1 all-to-all-done.1
  449.7 20.1 %all-to-all-done.3 = bf16[4,304,768]{2,0,1:T(4,128)(2,1)} async-done(((bf16[4,304,768]{2,0,1:T(4,128)(2,1)}), bf16[4,304,768]{2,0,1:T(4,128)(2,1)}, u32[]{:S(2)}, u32[]{:S(2)}) %all-to-all-start.3) | async-done | bytes 1867808 | tf_op jit(solution)/shard_map/all_to_all | solution.py:196
  482.4 6.0 fusion.62
  503.7 100.7 %while.27 = (s32[]{:T(128)}, bf16[12,1,576,64]{2,3,1,0:T(8,128)(2,1)}, bf16[12,1,576,64]{2,3,1,0:T(8,128)(2,1)}, bf16[12,1,576,64]{2,3,1,0:T(8,128)(2,1)}, bf16[...) while((s32[]{:T(128)}, ...), condition=%wide.region_19.20_spmd, body=%wide.region_17.19_spmd.sunk | while | flops 215064000 | bytes 11510129 | solution.py:210
  608.4 5.5 fusion.71
  615.2 7.2 fusion.60
  622.4 43.2 %all-reduce.5 = (f32[768]{0:T(1024)S(1)}, f32[768]{0:T(1024)S(1)}, f32[768,8]{0,1:T(8,128)S(1)}) all-reduce(f32[768]{0:T(1024)S(1)} %get-tuple-element.158, f32[768]{0:T(1024)S(1)} %get-tuple-element.156, f32[768,8]{0,1:T(8,128)S(1)} %fusion.79), channel_id=2, replica_groups=mesh['dp'=2,'fsdp'=16] {'dp','fsdp'}, use_global_device_ids=true, to_apply=%region_23.24.clone | all-reduce | flops 7680 | bytes 61440
  676.7 88.2 %reduce-scatter.12.cloned.1.call-done = bf16[4,192,768]{2,1,0:T(8,128)(2,1)} async-done(((bf16[4,3072,768]{2,1,0:T(8,128)(2,1)}), bf16[4,192,768]{2,1,0:T(8,128)(2,1)}) %reduce-scatter.12.cloned.1.call-update) | async-done | bytes 1179664 | tf_op jit(solution)/shard_map/reduce_scatter | solution.py:119
  767.8 101.8 %reduce-scatter.8.cloned.1.call-done = f32[24,768]{1,0:T(8,128)} async-done(((f32[768,768]{1,0:T(8,128)}), f32[24,768]{1,0:T(8,128)}) %reduce-scatter.8.cloned.1.call-update) | async-done | bytes 73744 | tf_op jit(solution)/shard_map/reduce_scatter | solution.py:228
  869.6 124.8 %reduce-scatter.6.cloned.1.call-done = f32[24,2304]{1,0:T(8,128)} async-done(((f32[768,2304]{1,0:T(8,128)}), f32[24,2304]{1,0:T(8,128)}) %reduce-scatter.6.cloned.1.call-update) | async-done | bytes 221200 | tf_op jit(solution)/shard_map/reduce_scatter | solution.py:227
  (316 shorter events, 252.4 us)
Async XLA Ops:
  7.2 45.4 %copy-start.34 = (bf16[24,8]{0,1:T(8,128)(2,1)S(1)}, bf16[24,8]{0,1:T(8,128)(2,1)}, u32[]{:S(2)}) copy-start(bf16[24,8]{0,1:T(8,128)(2,1)} %param.20) | copy-start | bytes 1156
  7.2 86.3 %copy-start.8 = (bf16[576,768]{1,0:T(8,128)(2,1)S(1)}, bf16[576,768]{1,0:T(8,128)(2,1)}, u32[]{:S(2)}) copy-start(bf16[576,768]{1,0:T(8,128)(2,1)} %param.15) | copy-start | bytes 2654212
  7.2 88.2 %all-gather.6.cloned.1.call-start = ((), (), s32[]{:S(2)}) async-start(), calls=%async_computation.8 | async-start | bytes 3649536 | tf_op jit(solution)/shard_map/all_gather | solution.py:99
  8.0 143.4 %all-gather.8.cloned.1.call-start = ((), (), s32[]{:S(2)}) async-start(), calls=%async_computation.9 | async-start | bytes 1216512 | tf_op jit(solution)/shard_map/all_gather | solution.py:100
  8.7 220.1 %all-gather.12.cloned.1.call-start = ((), (), s32[]{:S(2)}) async-start(), calls=%async_computation.11 | async-start | bytes 20054016 | tf_op jit(solution)/shard_map/all_gather | solution.py:110
  9.4 84.7 %copy-start.21 = (s32[576,2]{0,1:T(2,128)S(1)}, s32[576,2]{0,1:T(2,128)}, u32[]{:S(2)}) copy-start(s32[576,2]{0,1:T(2,128)} %param.24) | copy-start | bytes 13828
  9.4 85.3 %copy-start.23 = (s32[576,2]{0,1:T(2,128)S(1)}, s32[576,2]{0,1:T(2,128)}, u32[]{:S(2)}) copy-start(s32[576,2]{0,1:T(2,128)} %param.23) | copy-start | bytes 13828
  9.5 319.6 %all-gather.10.cloned.1.call-start = ((), (), s32[]{:S(2)}) async-start(), calls=%async_computation.10 | async-start | bytes 20054016 | tf_op jit(solution)/shard_map/all_gather | solution.py:109
  52.6 42.8 %copy-start.29 = (f32[768]{0:T(1024)}, f32[768]{0:T(1024)S(1)}, u32[]{:S(2)}) copy-start(f32[768]{0:T(1024)S(1)} %convert_element_type.101) | copy-start | bytes 9220
  151.3 4.2 copy-start.5
  156.7 10.9 %copy-start.6 = (bf16[576,768]{1,0:T(8,128)(2,1)}, bf16[576,768]{1,0:T(8,128)(2,1)S(1)}, u32[]{:S(2)}) copy-start(bf16[576,768]{1,0:T(8,128)(2,1)S(1)} %multiply_convert_fusion.2) | copy-start | bytes 2654212
  156.7 4.2 copy-start.19
  163.8 26.7 %all-to-all-start.2 = ((bf16[8,152,768]{2,1,0:T(8,128)(2,1)}), bf16[8,152,768]{2,1,0:T(8,128)(2,1)S(1)}, u32[]{:S(2)}, u32[]{:S(2)}) async-start(bf16[8,152,768]{2,1,0:T(8,128)(2,1)} %bitcast.194), calls=%async_computation.2 | async-start | bytes 3735552 | tf_op jit(solution)/shard_map/all_to_all | solution.py:192
  191.7 27.1 %all-to-all-start = ((bf16[8,152,768]{2,1,0:T(8,128)(2,1)}), bf16[8,152,768]{2,1,0:T(8,128)(2,1)}, u32[]{:S(2)}, u32[]{:S(2)}) async-start(bf16[8,152,768]{2,1,0:T(8,128)(2,1)} %bitcast.191), calls=%async_computation | async-start | bytes 3735552 | tf_op jit(solution)/shard_map/all_to_all | solution.py:165
  196.5 477.2 %reduce-scatter.10.cloned.1.call-start = ((), (), s32[]{:S(2)}) async-start(), calls=%async_computation.14 | async-start | bytes 20054016 | tf_op jit(solution)/shard_map/reduce_scatter | solution.py:116
  372.6 392.4 %reduce-scatter.12.cloned.1.call-start = ((), (), s32[]{:S(2)}) async-start(), calls=%async_computation.15 | async-start | bytes 20054016 | tf_op jit(solution)/shard_map/reduce_scatter | solution.py:119
  414.4 27.0 %all-to-all-start.1 = ((bf16[4,304,768]{2,0,1:T(4,128)(2,1)}), bf16[4,304,768]{2,0,1:T(4,128)(2,1)S(1)}, u32[]{:S(2)}, u32[]{:S(2)}) async-start(bf16[4,304,768]{2,0,1:T(4,128)(2,1)} %copy.108), calls=%async_computation.1 | async-start | bytes 3735552 | tf_op jit(solution)/shard_map/all_to_all | solution.py:167
  435.3 12.2 %copy-start.28 = (s32[576,2]{0,1:T(2,128)S(1)}, s32[576,2]{0,1:T(2,128)}, u32[]{:S(2)}) copy-start(s32[576,2]{0,1:T(2,128)} %get-tuple-element.199) | copy-start | bytes 13828
  442.6 27.1 %all-to-all-start.3 = ((bf16[4,304,768]{2,0,1:T(4,128)(2,1)}), bf16[4,304,768]{2,0,1:T(4,128)(2,1)}, u32[]{:S(2)}, u32[]{:S(2)}) async-start(bf16[4,304,768]{2,0,1:T(4,128)(2,1)} %copy.112), calls=%async_computation.3 | async-start | bytes 3735552 | tf_op jit(solution)/shard_map/all_to_all | solution.py:196
  447.4 422.2 %reduce-scatter.8.cloned.1.call-start = ((), (), s32[]{:S(2)}) async-start(), calls=%async_computation.13 | async-start | bytes 2433024 | tf_op jit(solution)/shard_map/reduce_scatter | solution.py:228
  482.4 7.1 copy-start.22
  482.4 7.3 copy-start.16
  503.4 491.0 %reduce-scatter.6.cloned.1.call-start = ((), (), s32[]{:S(2)}) async-start(), calls=%async_computation.12 | async-start | bytes 7299072 | tf_op jit(solution)/shard_map/reduce_scatter | solution.py:227
  615.2 52.2 %copy-start.10 = (bf16[576,768]{1,0:T(8,128)(2,1)S(1)}, bf16[576,768]{1,0:T(8,128)(2,1)}, u32[]{:S(2)}) copy-start(bf16[576,768]{1,0:T(8,128)(2,1)} %param.15) | copy-start | bytes 2654212
  (26 other events, 53.1 us)
Sparse Core Ops, SparseCore 0:
  10.9 62.6 all-gather.5
  76.6 52.6 all-gather.7
  130.9 97.8 all-gather.11
  230.2 98.8 all-gather.9
  372.7 194.0 reduce-scatter.9
  570.7 194.1 reduce-scatter.11
  770.8 98.7 reduce-scatter.7
  875.8 118.5 reduce-scatter.5
where the time goes:
time: 1010 us; the launch traced here: 1000 us
  waiting for transfers between devices  477 us (47%)
  matrix products  276 us (27%)
  blocking collectives  126 us (12%)
  local copies, waits for them, and re-layouts  66.9 us (7%)
  other arithmetic  22.4 us (2%)
  starting transfers between devices  18.3 us (2%)
  between operations  15.1 us (1%)
    reduce_scatter x1, waiting for transfers between devices, per_device(): lax.psum_scatter(d_qkv, ('dp', 'fsdp'), scatter_dimension=0, tiled=True)  125 us
    reduce_scatter x1, waiting for transfers between devices, per_device(): lax.psum_scatter(d_proj, ('dp', 'fsdp'), scatter_dimension=0, tiled=True)  102 us
    reduce_scatter x1, waiting for transfers between devices, reduce_experts(): lax.psum_scatter(grad_down.astype(jnp.bfloat16), 'fsdp', scatter_dimensio...  88.2 us
    all_gather x1, waiting for transfers between devices, gather_experts(): lax.all_gather(local_pair[0], 'fsdp', axis=1, tiled=True)  87.4 us
    unnamed x2, blocking collectives  85.2 us
    all_gather x1, blocking collectives, gather_dense(): lax.all_gather(w_router, ('dp', 'fsdp'), axis=0, tiled=True)  40.8 us
    dot_general x1, matrix products, expert_forward(): jnp.einsum('ecd,edf->ecf', expert_rows, w_up, preferred_element_type=jnp....  26.9 us
    dot_general x12, matrix products, head_forward(): jnp.einsum('ist,itd->isd', attn_probs, values_head, preferred_element_typ...  23.4 us
  transfers between devices with their start and end apart: 12, of which 9 were waited for; matrix products, arithmetic and copies ran while one was open for 31% of the time, Pallas kernels for 0%

commit v1 on v0

v1 whole, which is shorter than its diff:
```python
import jax
import jax.numpy as jnp
from jax import lax
from jax.sharding import Mesh, PartitionSpec as P

HEADS = 12
HEAD_DIM = 64
EXPERTS = 8
SEQ = 576
CAP = 152
NORM_EPSILON = 1e-06
SCALE = HEAD_DIM ** (-0.5)
F32 = jnp.float32
BF16 = jnp.bfloat16


def norm_parts(values):
    centre = values - jnp.mean(values, axis=-1, keepdims=True)
    inverse = lax.rsqrt(jnp.mean(centre * centre, axis=-1, keepdims=True) + NORM_EPSILON)
    return centre * inverse, inverse


def norm_back(grad_normed, normed, inverse):
    mean_grad = jnp.mean(grad_normed, axis=-1, keepdims=True)
    mean_cross = jnp.mean(grad_normed * normed, axis=-1, keepdims=True)
    return (grad_normed - mean_grad - normed * mean_cross) * inverse


def gelu_tanh(values):
    return jax.nn.gelu(values, approximate=True)


def head_forward(operands):
    queries, keys_head, values_head = operands
    scores = jnp.einsum("isd,itd->ist", queries, keys_head, preferred_element_type=F32) * SCALE
    largest = jnp.max(scores, axis=-1, keepdims=True)
    powers = jnp.exp(scores - largest)
    totals = jnp.sum(powers, axis=-1, keepdims=True)
    attn_probs = (powers / totals).astype(BF16)
    head_out = jnp.einsum("ist,itd->isd", attn_probs, values_head, preferred_element_type=F32)
    return head_out.astype(BF16), (largest + jnp.log(totals))[..., 0]


def head_backward(operands):
    queries, keys_head, values_head, grad_head, log_total = operands
    scores = jnp.einsum("isd,itd->ist", queries, keys_head, preferred_element_type=F32) * SCALE
    attn_probs = jnp.exp(scores - log_total[..., None])
    grad_probs = jnp.einsum("isd,itd->ist", grad_head, values_head, preferred_element_type=F32)
    row_terms = jnp.sum(attn_probs * grad_probs, axis=-1, keepdims=True)
    grad_scores = (attn_probs * (grad_probs - row_terms)).astype(BF16)
    grad_query = jnp.einsum("ist,itd->isd", grad_scores, keys_head, preferred_element_type=F32) * SCALE
    grad_key = jnp.einsum("ist,isd->itd", grad_scores, queries, preferred_element_type=F32) * SCALE
    grad_value = jnp.einsum(
        "ist,isd->itd", attn_probs.astype(BF16), grad_head, preferred_element_type=F32
    )
    return grad_query, grad_key, grad_value


def attention_forward(qkv):
    rows = qkv.shape[0]
    split_qkv = qkv.reshape(rows // SEQ, SEQ, 3, HEADS, HEAD_DIM).transpose(2, 3, 0, 1, 4)
    head_out, head_lse = lax.map(head_forward, (split_qkv[0], split_qkv[1], split_qkv[2]))
    return head_out.transpose(1, 2, 0, 3).reshape(rows, -1), (split_qkv, head_lse)


def attention_backward(saved, grad_attended):
    split_qkv, head_lse = saved
    rows = grad_attended.shape[0]
    grad_heads = grad_attended.reshape(rows // SEQ, SEQ, HEADS, HEAD_DIM).transpose(2, 0, 1, 3)
    parts = lax.map(
        head_backward, (split_qkv[0], split_qkv[1], split_qkv[2], grad_heads, head_lse)
    )
    return jnp.stack(parts).transpose(2, 3, 0, 1, 4).reshape(rows, -1).astype(BF16)


class PairwiseLinks:
    def __init__(self, mesh):
        self.mesh = Mesh(mesh.devices.reshape(2, 2, 2, 2, 2), ("x", "zh", "zl", "y", "c"))
        self.data = ("x", "zh", "zl", "y", "c")
        self.fsdp = ("zh", "zl", "y", "c")
        self.dp = "x"
        self.hosts = ("x", "zl", "y")

    def swap(self, value, axis):
        return lax.ppermute(value, axis, [(0, 1), (1, 0)])

    def join(self, value, axis, at):
        other = self.swap(value, axis)
        first = lax.axis_index(axis) == 0
        return jnp.stack([jnp.where(first, value, other), jnp.where(first, other, value)], axis=at)

    def add_halves(self, value, axis, at):
        me = lax.axis_index(axis)
        mine = lax.dynamic_index_in_dim(value, me, at, keepdims=False)
        theirs = lax.dynamic_index_in_dim(value, 1 - me, at, keepdims=False)
        got = self.swap(theirs, axis)
        return (mine.astype(F32) + got.astype(F32)).astype(value.dtype)

    def gather_rows(self, shard):
        rows, columns = shard.shape
        copies = jnp.broadcast_to(shard[None], (4, rows, columns))
        over_z = lax.all_to_all(copies, ("zh", "zl"), 0, 0, tiled=True)
        over_y = self.join(over_z, "y", 1)
        over_x = self.join(over_y, "x", 0)
        whole = self.join(over_x, "c", 3)
        return whole.reshape(32 * rows, columns)

    def scatter_rows(self, value):
        rows, columns = value.shape
        part = value.reshape(2, 4, 2, 2, rows // 32, columns)
        part = self.add_halves(part, "c", 3)
        part = self.add_halves(part, "x", 0)
        part = self.add_halves(part, "y", 1)
        got = lax.all_to_all(part, ("zh", "zl"), 0, 0, tiled=True)
        return jnp.sum(got.astype(F32), axis=0)

    def send_slots(self, slots):
        return lax.all_to_all(slots, self.hosts, 0, 0, tiled=True)

    def return_slots(self, slots):
        return lax.all_to_all(slots, self.hosts, 0, 0, tiled=True)

    def gather_expert(self, shard):
        mine = lax.all_to_all(shard, ("zl", "y"), 0, 0, tiled=True)
        halves = self.join(mine, "zh", 0)
        whole = self.join(halves, "c", 2)
        return whole.reshape(1, -1, shard.shape[-1])

    def scatter_expert(self, grad):
        _, rows, columns = grad.shape
        part = grad.astype(BF16).reshape(2, 4, 2, rows // 16, columns)
        part = self.add_halves(part, "c", 2)
        part = self.add_halves(part, "zh", 0)
        return lax.all_to_all(part, ("zl", "y"), 0, 0, tiled=True).astype(F32)


class AxisLinks:
    def __init__(self, mesh):
        self.mesh = mesh
        self.data = ("dp", "fsdp")
        self.fsdp = "fsdp"
        self.dp = "dp"

    def gather_rows(self, shard):
        return lax.all_gather(shard, self.data, axis=0, tiled=True)

    def scatter_rows(self, value):
        return lax.psum_scatter(value.astype(F32), self.data, scatter_dimension=0, tiled=True)

    def send_slots(self, slots):
        return lax.all_to_all(slots, "dp", 0, 1, tiled=True)

    def return_slots(self, slots):
        return lax.all_to_all(slots, "dp", 1, 0, tiled=True)

    def gather_expert(self, shard):
        return lax.all_gather(shard, "fsdp", axis=1, tiled=True)

    def scatter_expert(self, grad):
        return lax.psum_scatter(
            grad.astype(BF16), "fsdp", scatter_dimension=1, tiled=True
        ).astype(F32)


def per_device(
    links, tokens, gain_attn, w_qkv, w_proj, gain_moe, w_router, w_in, w_out, routes, slot_ids, cotangent
):
    width = tokens.shape[1]
    small = jnp.concatenate(
        [w_router, gain_attn[:, None], gain_moe[:, None]], axis=1
    )
    small = jnp.pad(small, ((0, 0), (0, 128 - small.shape[1])))
    dense = links.gather_rows(jnp.concatenate([w_qkv, w_proj, small], axis=1))
    full_qkv = dense[:, : 3 * width]
    full_proj = dense[:, 3 * width : 4 * width]
    full_router = dense[:, 4 * width : 4 * width + EXPERTS]
    gain_one = dense[:, 4 * width + EXPERTS].astype(F32)
    gain_two = dense[:, 4 * width + EXPERTS + 1].astype(F32)
    expert_in = links.gather_expert(w_in)
    expert_out = links.gather_expert(w_out)

    residual = tokens.astype(F32)
    normed_one, inverse_one = norm_parts(residual)
    act_one = (normed_one * gain_one).astype(BF16)
    qkv = jnp.dot(act_one, full_qkv, preferred_element_type=F32).astype(BF16)
    attended, saved = attention_forward(qkv)
    resid_mid = residual + jnp.dot(attended, full_proj, preferred_element_type=F32)
    normed_two, inverse_two = norm_parts(resid_mid)
    act_two = (normed_two * gain_two).astype(BF16)
    logits = jnp.dot(act_two, full_router, preferred_element_type=F32)
    router = jax.nn.softmax(logits, axis=-1)
    expert_ids = lax.broadcasted_iota(jnp.int32, (1, 1, EXPERTS), 2)
    chosen = routes[:, :, None] == expert_ids
    gates_low = jnp.sum(jnp.where(chosen, router[:, None, :], 0.0), axis=-1).astype(BF16)
    slot_count = EXPERTS * CAP
    columns = lax.broadcasted_iota(jnp.int32, (1, slot_count), 1)
    live_pair = slot_ids < CAP
    targets = jnp.where(live_pair, routes * CAP + slot_ids, -1)
    match_a = targets[:, 0:1] == columns
    match_b = targets[:, 1:2] == columns
    dispatch = (match_a | match_b).astype(BF16)
    zero = jnp.zeros((), BF16)
    combine = jnp.where(match_a, gates_low[:, 0:1], jnp.where(match_b, gates_low[:, 1:2], zero))

    def to_slots(weights, values):
        rows = jnp.einsum("tx,td->xd", weights, values, preferred_element_type=F32)
        return rows.astype(BF16).reshape(EXPERTS, CAP, -1)

    slot_rows = links.send_slots(to_slots(dispatch, act_two))
    grad_slots = links.send_slots(to_slots(combine, cotangent))
    held = slot_rows.shape
    hosted = expert_in.shape[0]
    expert_rows = slot_rows.reshape(hosted, -1, width)
    grad_result = grad_slots.reshape(hosted, -1, width)

    pre_act = jnp.einsum("ecd,edf->ecf", expert_rows, expert_in, preferred_element_type=F32)
    hidden = gelu_tanh(pre_act).astype(BF16)
    result = jnp.einsum("ecf,efd->ecd", hidden, expert_out, preferred_element_type=F32)
    flat_result = links.return_slots(result.astype(BF16).reshape(held)).reshape(slot_count, -1)

    grad_down = jnp.einsum("ecf,ecd->efd", hidden, grad_result, preferred_element_type=F32)
    d_out = links.scatter_expert(grad_down)
    grad_hidden = jnp.einsum("ecd,efd->ecf", grad_result, expert_out, preferred_element_type=F32)
    grad_pre = jax.vjp(gelu_tanh, pre_act)[1](grad_hidden)[0].astype(BF16)
    grad_rows = jnp.einsum("ecf,edf->ecd", grad_pre, expert_in, preferred_element_type=F32)
    grad_rows = links.return_slots(grad_rows.astype(BF16).reshape(held)).reshape(slot_count, -1)
    grad_up = jnp.einsum("ecd,ecf->edf", expert_rows, grad_pre, preferred_element_type=F32)
    d_in = links.scatter_expert(grad_up)

    moe_sum = jnp.einsum("tx,xd->td", combine, flat_result, preferred_element_type=F32)
    output = (resid_mid + moe_sum).astype(BF16)
    crossed = jnp.einsum("td,xd->tx", cotangent, flat_result, preferred_element_type=F32)
    grad_gates = jnp.stack(
        [
            jnp.sum(jnp.where(match_a, crossed, 0.0), axis=1),
            jnp.sum(jnp.where(match_b, crossed, 0.0), axis=1),
        ],
        axis=1,
    )
    grad_router = jnp.sum(jnp.where(chosen, grad_gates[:, :, None], 0.0), axis=1)
    grad_logits = (
        router * (grad_router - jnp.sum(router * grad_router, axis=-1, keepdims=True))
    ).astype(BF16)
    d_router = jnp.einsum("td,te->de", act_two, grad_logits, preferred_element_type=F32)
    grad_act_two = jnp.einsum("te,de->td", grad_logits, full_router, preferred_element_type=F32)
    grad_act_two = grad_act_two + jnp.einsum(
        "tx,xd->td", dispatch, grad_rows, preferred_element_type=F32
    )
    d_gain_moe = jnp.sum(grad_act_two * normed_two, axis=0)
    grad_mid = cotangent.astype(F32) + norm_back(grad_act_two * gain_two, normed_two, inverse_two)
    grad_mid_low = grad_mid.astype(BF16)
    d_proj = jnp.einsum("td,te->de", attended, grad_mid_low, preferred_element_type=F32)
    grad_attended = jnp.einsum(
        "te,de->td", grad_mid_low, full_proj, preferred_element_type=F32
    ).astype(BF16)
    grad_qkv = attention_backward(saved, grad_attended)
    d_qkv = jnp.einsum("td,te->de", act_one, grad_qkv, preferred_element_type=F32)
    grad_act_one = jnp.einsum("te,de->td", grad_qkv, full_qkv, preferred_element_type=F32)
    d_gain_attn = jnp.sum(grad_act_one * normed_one, axis=0)
    grad_tokens = grad_mid + norm_back(grad_act_one * gain_one, normed_one, inverse_one)
    small_grads = jnp.concatenate([d_router, d_gain_attn[:, None], d_gain_moe[:, None]], axis=1)
    small_grads = jnp.pad(small_grads, ((0, 0), (0, 128 - small_grads.shape[1])))
    dense_grads = links.scatter_rows(
        jnp.concatenate([d_qkv, d_proj, small_grads], axis=1).astype(BF16)
    )
    return (
        output,
        grad_tokens,
        dense_grads[:, 4 * width + EXPERTS],
        dense_grads[:, : 3 * width],
        dense_grads[:, 3 * width : 4 * width],
        dense_grads[:, 4 * width + EXPERTS + 1],
        dense_grads[:, 4 * width : 4 * width + EXPERTS],
        d_in,
        d_out,
    )


def solution(mesh):
    pairwise = mesh.shape["dp"] == 2 and mesh.shape["fsdp"] == 16
    links = PairwiseLinks(mesh) if pairwise else AxisLinks(mesh)
    rows = P(links.data, None)
    flat = P(links.data)
    expert = P(links.dp, links.fsdp, None)
    return jax.shard_map(
        lambda *arrays: per_device(links, *arrays),
        mesh=links.mesh,
        in_specs=(rows, flat, rows, rows, flat, rows, expert, expert, rows, rows, rows),
        out_specs=(rows, rows, flat, rows, rows, flat, rows, expert, expert),
        check_vma=False,
    )
```

time: 1010 us -> 765 us (0.76)
  waiting for transfers between devices: 477 us -> 301 us
  blocking collectives: 126 us -> 22.6 us
  other arithmetic: 22.4 us -> 64.3 us
  starting transfers between devices: 18.3 us -> 50.1 us
  matrix products: 276 us -> 251 us
  between operations: 15.1 us -> 2.19 us
    reduce_scatter x4 -> x0, waiting for transfers between devices: 315 us -> none  [the longest x1 125 us: per_device(): lax.psum_scatter(d_qkv, ('dp', 'fsdp'), scatter_dimension=0, tiled=True)]
    ppermute x0 -> x14, waiting for transfers between devices: none -> 216 us  [swap(): return lax.ppermute(value, axis, [(0, 1), (1, 0)])]
    all_gather x4 -> x0, waiting for transfers between devices: 94.5 us -> none  [the longest x1 87.4 us: gather_experts(): lax.all_gather(local_pair[0], 'fsdp', axis=1, tiled=True)]
    unnamed x2 -> x0, blocking collectives: 85.2 us -> none
    all_gather x1 -> x0, blocking collectives: 40.8 us -> none  [gather_dense(): lax.all_gather(w_router, ('dp', 'fsdp'), axis=0, tiled=True)]
    dot_general x68, matrix products: 215 us -> 191 us  [the longest x12 22.8 us: head_backward(): jnp.einsum('ist,isd->itd', grad_scores, queries, preferred_element_type=F32)]
    all_to_all x0 -> x1, blocking collectives: none -> 22.6 us  [gather_rows(): over_z = lax.all_to_all(copies, ('zh', 'zl'), 0, 0, tiled=True)]
    another operation x4 -> x18, other arithmetic: 0.52 us -> 22.6 us  [the longest x14 22.6 us: join(): jnp.stack([jnp.where(first, value, other), jnp.where(first, other, value)...]
  transfers between devices with their start and end apart: 12 -> 23, of which waited for: 9 -> 14; matrix products, arithmetic and copies ran while one was open for 31% -> 39% of each run, Pallas kernels for 0% -> 0%
where the time goes in v1:
time: 765 us; the launch traced here: 752 us
  waiting for transfers between devices  301 us (39%)
  matrix products  251 us (33%)
  other arithmetic  64.3 us (8%)
  local copies, waits for them, and re-layouts  60.1 us (8%)
  starting transfers between devices  50.1 us (7%)
  blocking collectives  22.6 us (3%)
    ppermute x14, waiting for transfers between devices, swap(): return lax.ppermute(value, axis, [(0, 1), (1, 0)])  216 us
    all_to_all x2, waiting for transfers between devices, send_slots(): return lax.all_to_all(slots, self.hosts, 0, 0, tiled=True)  41.8 us
    all_to_all x2, waiting for transfers between devices, return_slots(): return lax.all_to_all(slots, self.hosts, 0, 0, tiled=True)  24.4 us
    dot_general x12, matrix products, head_forward(): jnp.einsum('ist,itd->isd', attn_probs, values_head, preferred_element_typ...  23.2 us
    dot_general x12, matrix products, head_backward(): jnp.einsum('ist,isd->itd', grad_scores, queries, preferred_element_type=F32)  22.8 us
    another operation x14, other arithmetic, join(): jnp.stack([jnp.where(first, value, other), jnp.where(first, other, value)...  22.6 us
    all_to_all x1, blocking collectives, gather_rows(): over_z = lax.all_to_all(copies, ('zh', 'zl'), 0, 0, tiled=True)  22.6 us
    dot_general x12, matrix products, head_backward(): jnp.einsum('ist,itd->isd', grad_scores, keys_head, preferred_element_type...  22.1 us
  transfers between devices with their start and end apart: 23, of which 14 were waited for; matrix products, arithmetic and copies ran while one was open for 39% of the time, Pallas kernels for 0%

profile of v1, /device:TPU:0, one launch (start us, length us, event | category | flops | bytes accessed | tf_op | source)
XLA Modules:
  0.0 752.2 jit_solution(684831136403379420)
XLA Ops:
  2.5 22.6 %all_to_all.50 = bf16[4,24,3200]{2,1,0:T(8,128)(2,1)S(1)} all-to-all(bf16[4,24,3200]{2,1,0:T(8,128)(2,1)S(1)} %broadcast_in_dim.123), channel_id=1, replica_groups=mesh['x'=2,'zh'=2,'zl'=2,'y'=2,'c'=2] {'zh','zl'}, dimensions={0} | all-to-all | bytes 1228800 | tf_op jit(solution)/shard_map/all_to_all | solution.py:102
  30.8 17.2 %collective-permute-done = bf16[4,24,3200]{2,1,0:T(8,128)(2,1)S(1)} collective-permute-done((bf16[4,24,3200]{2,1,0:T(8,128)(2,1)S(1)}, bf16[4,24,3200]{2,1,0:T(8,128)(2,1)S(1)}, u32[]{:S(2)}, u32[]{:S(2)}) %collective-permute-start) | collective-permute-done | bytes 614432 | tf_op jit(solution)/shard_map/ppermute | solution.py:85
  57.4 15.9 %collective-permute-done.1 = bf16[4,2,24,3200]{3,2,1,0:T(8,128)(2,1)} collective-permute-done((bf16[4,2,24,3200]{3,2,1,0:T(8,128)(2,1)S(1)}, bf16[4,2,24,3200]{3,2,1,0:T(8,128)(2,1)}, u32[]{:S(2)}, u32[]{:S(2)}) %collective-permute-start.1) | collective-permute-done | bytes 1228832 | tf_op jit(solution)/shard_map/ppermute | solution.py:85
  76.9 5.8 all-to-all-done.2
  83.3 54.1 %collective-permute-done.5 = bf16[4,192,768]{2,1,0:T(8,128)(2,1)} collective-permute-done((bf16[4,192,768]{2,1,0:T(8,128)(2,1)}, bf16[4,192,768]{2,1,0:T(8,128)(2,1)}, u32[]{:S(2)}, u32[]{:S(2)}) %collective-permute-start.5) | collective-permute-done | bytes 1179680 | tf_op jit(solution)/shard_map/ppermute | solution.py:85
  141.4 18.3 %collective-permute-done.3 = bf16[4,48,3072]{2,1,0:T(8,128)(2,1)} collective-permute-done((bf16[4,48,3072]{2,1,0:T(8,128)(2,1)}, bf16[4,48,3072]{2,1,0:T(8,128)(2,1)}, u32[]{:S(2)}, u32[]{:S(2)}) %collective-permute-start.3) | collective-permute-done | bytes 1179680 | tf_op jit(solution)/shard_map/ppermute | solution.py:85
  187.6 48.6 %while.26 = (s32[]{:T(128)}, bf16[12,1,576,64]{2,3,1,0:T(8,128)(2,1)}, f32[12,1,576]{2,1,0:T(1,128)}, bf16[12,1,576,64]{3,2,1,0:T(8,128)(2,1)S(1)}, bf16[12,1,57...) while((s32[]{:T(128)}, bf16[12,1,576,64]{2,3,1,0:T(8,128)(2,1)}, ...), condition=%wide.region_5.6_spmd, body=%wide.region_2.5_spmd.sunk | while | flops 87293376 | bytes 4531033 | solution.py:62
  258.2 18.7 %all-to-all-done.1 = bf16[8,152,768]{2,1,0:T(8,128)(2,1)} async-done(((bf16[8,152,768]{2,1,0:T(8,128)(2,1)}), bf16[8,152,768]{2,1,0:T(8,128)(2,1)}, u32[]{:S(2)}, u32[]{:S(2)}) %all-to-all-start.1) | async-done | bytes 1867808 | tf_op jit(solution)/shard_map/all_to_all | solution.py:118
  276.8 8.4 %fusion.111 = f32[1216,3072]{1,0:T(8,128)S(1)} fusion(bf16[1216,768]{1,0:T(8,128)(2,1)} %bitcast.31, bf16[768,3072]{1,0:T(8,128)(2,1)} %bitcast.256), kind=kOutput, calls=%fused_computation.217 | convolution fusion | flops 5737807872 | bytes 21528576 | tf_op jit(solution)/shard_map/ecd,edf->ecf/dot_general | solution.py:216
  285.3 15.7 %convolution_convert_fusion.6 = bf16[1216,768]{1,0:T(8,128)(2,1)} fusion(bf16[3072,768]{1,0:T(8,128)(2,1)} %bitcast.254, f32[1216,3072]{1,0:T(8,128)S(1)} %fusion.111), kind=kOutput, calls=%fused_computation.76 | convolution fusion | flops 5772361728 | bytes 21528576 | tf_op jit(solution)/shard_map/ecf,efd->ecd/dot_general | solution.py:218
  308.0 24.4 %all-to-all-done.4 = bf16[8,152,768]{2,1,0:T(8,128)(2,1)} async-done(((bf16[8,152,768]{2,1,0:T(8,128)(2,1)}), bf16[8,152,768]{2,1,0:T(8,128)(2,1)}, u32[]{:S(2)}, u32[]{:S(2)}) %all-to-all-start.4) | async-done | bytes 1867808 | tf_op jit(solution)/shard_map/all_to_all | solution.py:121
  339.9 4.7 all-to-all-start.5
  347.7 23.1 %all-to-all-done.5 = bf16[8,152,768]{2,1,0:T(8,128)(2,1)} async-done(((bf16[8,152,768]{2,1,0:T(8,128)(2,1)}), bf16[8,152,768]{2,1,0:T(8,128)(2,1)}, u32[]{:S(2)}, u32[]{:S(2)}) %all-to-all-start.5) | async-done | bytes 1867808 | tf_op jit(solution)/shard_map/all_to_all | solution.py:118
  370.8 18.1 %fusion.43 = bf16[1216,3072]{1,0:T(8,128)(2,1)S(1)} fusion(f32[1216,3072]{1,0:T(8,128)} %copy-done.61, bf16[1216,768]{1,0:T(8,128)(2,1)} %bitcast.48, bf16[3072,768]{1,0:T(8,128)(2,1)} %bitcast.255), kind=kOutput, calls=%fused_computation.58 | convolution fusion | flops 5812518912 | bytes 28999680 | tf_op jit(solution)/shard_map/ecd,efd->ecf/dot_general | solution.py:223
  388.9 12.1 %convolution_convert_fusion.5 = bf16[1216,768]{1,0:T(8,128)(2,1)} fusion(bf16[1216,3072]{1,0:T(8,128)(2,1)S(1)} %fusion.43, bf16[768,3072]{1,0:T(8,128)(2,1)} %bitcast.257), kind=kOutput, calls=%fused_computation.75 | convolution fusion | flops 5738741760 | bytes 14057472 | tf_op jit(solution)/shard_map/ecf,edf->ecd/dot_general | solution.py:225
  405.6 9.2 %convolution_convert_fusion.2 = bf16[768,3072]{1,0:T(8,128)(2,1)S(1)} fusion(bf16[1216,768]{1,0:T(8,128)(2,1)} %bitcast.31, bf16[1216,3072]{1,0:T(8,128)(2,1)} %copy-done.60), kind=kOutput, calls=%fused_computation.62 | convolution fusion | flops 5740167168 | bytes 14057472 | tf_op jit(solution)/shard_map/ecd,ecf->edf/dot_general | solution.py:227
  417.6 12.1 %convolution_convert_fusion.1 = bf16[3072,768]{1,0:T(8,128)(2,1)S(1)} fusion(bf16[1216,768]{1,0:T(8,128)(2,1)} %bitcast.48, f32[1216,3072]{1,0:T(8,128)} %copy-done.61), kind=kOutput, calls=%fused_computation.61 | convolution fusion | flops 5773787136 | bytes 21528576 | tf_op jit(solution)/shard_map/ecf,ecd->efd/dot_general | solution.py:221
  445.4 100.1 %while.27 = (s32[]{:T(128)}, bf16[12,1,576,64]{2,3,1,0:T(8,128)(2,1)}, bf16[12,1,576,64]{2,3,1,0:T(8,128)(2,1)}, bf16[12,1,576,64]{2,3,1,0:T(8,128)(2,1)}, bf16[...) while((s32[]{:T(128)}, ...), condition=%wide.region_19.20_spmd, body=%wide.region_17.19_spmd.sunk | while | flops 215064000 | bytes 11510129 | solution.py:70
  547.9 5.7 fusion.47
  558.9 6.9 convolution_convert_fusion.3
  590.1 66.3 %collective-permute-done.11 = bf16[4,48,3072]{2,1,0:T(8,128)(2,1)S(1)} collective-permute-done((bf16[4,48,3072]{2,1,0:T(8,128)(2,1)S(1)}, bf16[4,48,3072]{2,1,0:T(8,128)(2,1)S(1)}, u32[]{:S(2)}, u32[]{:S(2)}) %collective-permute-start.11) | collective-permute-done | bytes 1179680 | tf_op jit(solution)/shard_map/ppermute | solution.py:85
  662.3 19.2 %collective-permute-done.13 = bf16[4,192,768]{2,1,0:T(8,128)(2,1)} collective-permute-done((bf16[4,192,768]{2,1,0:T(8,128)(2,1)}, bf16[4,192,768]{2,1,0:T(8,128)(2,1)}, u32[]{:S(2)}, u32[]{:S(2)}) %collective-permute-start.13) | collective-permute-done | bytes 1179680 | tf_op jit(solution)/shard_map/ppermute | solution.py:85
  687.0 7.0 all-to-all-done.8
  702.2 24.9 %collective-permute-done.9 = bf16[4,24,3200]{2,1,0:T(8,128)(2,1)S(1)} collective-permute-done((bf16[4,24,3200]{2,1,0:T(8,128)(2,1)}, bf16[4,24,3200]{2,1,0:T(8,128)(2,1)S(1)}, u32[]{:S(2)}, u32[]{:S(2)}) %collective-permute-start.9) | collective-permute-done | bytes 614432 | tf_op jit(solution)/shard_map/ppermute | solution.py:85
  (403 shorter events, 339.0 us)
Async XLA Ops:
  25.0 23.0 %collective-permute-start = (bf16[4,24,3200]{2,1,0:T(8,128)(2,1)S(1)}, bf16[4,24,3200]{2,1,0:T(8,128)(2,1)S(1)}, u32[]{:S(2)}, u32[]{:S(2)}) collective-permute-start(bf16[4,24,3200]{2,1,0:T(8,128)(2,1)S(1)} %all_to_all.50), channel_id=1, source_target_pairs={{0,2},{2,0},{1,3},{3,1},{4,6},{6,4},{5,7},{7,5},{8,10},{10,8},{9,1... | collective-permute-start | bytes 1843208 | tf_op jit(solution)/shard_map/ppermute | solution.py:85
  26.5 25.8 %all-to-all-start.3 = ((bf16[4,192,768]{2,1,0:T(8,128)(2,1)}), bf16[4,192,768]{2,1,0:T(8,128)(2,1)}, u32[]{:S(2)}, u32[]{:S(2)}) async-start(bf16[4,192,768]{2,1,0:T(8,128)(2,1)} %param.22), calls=%async_computation.3 | async-start | bytes 2359296 | tf_op jit(solution)/shard_map/all_to_all | solution.py:124
  48.3 25.0 %collective-permute-start.1 = (bf16[4,2,24,3200]{3,2,1,0:T(8,128)(2,1)S(1)}, bf16[4,2,24,3200]{3,2,1,0:T(8,128)(2,1)}, u32[]{:S(2)}, u32[]{:S(2)}) collective-permute-start(bf16[4,2,24,3200]{3,2,1,0:T(8,128)(2,1)S(1)} %pad_maximum_fusion.7), channel_id=1, source_target_pairs={{0,16},{16,0},{1,17},{17,1},{2,18},{18,2},{3,19},{19,3},{4,20},{20... | collective-permute-start | bytes 3686408 | tf_op jit(solution)/shard_map/ppermute | solution.py:85
  52.3 30.4 %all-to-all-start.2 = ((bf16[4,48,3072]{2,1,0:T(8,128)(2,1)}), bf16[4,48,3072]{2,1,0:T(8,128)(2,1)}, u32[]{:S(2)}, u32[]{:S(2)}) async-start(bf16[4,48,3072]{2,1,0:T(8,128)(2,1)} %param.21), calls=%async_computation.2 | async-start | bytes 2359296 | tf_op jit(solution)/shard_map/all_to_all | solution.py:124
  56.7 80.7 %collective-permute-start.5 = (bf16[4,192,768]{2,1,0:T(8,128)(2,1)}, bf16[4,192,768]{2,1,0:T(8,128)(2,1)}, u32[]{:S(2)}, u32[]{:S(2)}) collective-permute-start(bf16[4,192,768]{2,1,0:T(8,128)(2,1)} %all-to-all-done.3), channel_id=1, source_target_pairs={{0,8},{8,0},{1,9},{9,1},{2,10},{10,2},{3,11},{11,3},{4,12},{12,4},... | collective-permute-start | bytes 3538952 | tf_op jit(solution)/shard_map/ppermute | solution.py:85
  76.7 86.9 %collective-permute-start.2 = (bf16[2,4,2,24,3200]{4,3,2,1,0:T(8,128)(2,1)}, bf16[2,4,2,24,3200]{4,3,2,1,0:T(8,128)(2,1)}, u32[]{:S(2)}, u32[]{:S(2)}) collective-permute-start(bf16[2,4,2,24,3200]{4,3,2,1,0:T(8,128)(2,1)} %pad_maximum_fusion.4), channel_id=1, source_target_pairs={{0,1},{1,0},{2,3},{3,2},{4,5},{5,4},{6,7},{7,6},{8,9},{9,8},{10,11... | collective-permute-start | bytes 7372808 | tf_op jit(solution)/shard_map/ppermute | solution.py:85
  82.8 76.9 %collective-permute-start.3 = (bf16[4,48,3072]{2,1,0:T(8,128)(2,1)}, bf16[4,48,3072]{2,1,0:T(8,128)(2,1)}, u32[]{:S(2)}, u32[]{:S(2)}) collective-permute-start(bf16[4,48,3072]{2,1,0:T(8,128)(2,1)} %all-to-all-done.2), channel_id=1, source_target_pairs={{0,8},{8,0},{1,9},{9,1},{2,10},{10,2},{3,11},{11,3},{4,12},{12,4},... | collective-permute-start | bytes 3538952 | tf_op jit(solution)/shard_map/ppermute | solution.py:85
  82.8 157.9 %copy-start.48 = (s32[576]{0:T(1024)}, s32[576]{0:T(1024)S(1)}, u32[]{:S(2)}) copy-start(s32[576]{0:T(1024)S(1)} %get-tuple-element.215) | copy-start | bytes 6916
  141.4 107.3 %collective-permute-start.6 = (bf16[2,4,192,768]{3,2,1,0:T(8,128)(2,1)}, bf16[2,4,192,768]{3,2,1,0:T(8,128)(2,1)}, u32[]{:S(2)}, u32[]{:S(2)}) collective-permute-start(bf16[2,4,192,768]{3,2,1,0:T(8,128)(2,1)} %pad_maximum_fusion.6), channel_id=1, source_target_pairs={{0,1},{1,0},{2,3},{3,2},{4,5},{5,4},{6,7},{7,6},{8,9},{9,8},{10,11... | collective-permute-start | bytes 7077896 | tf_op jit(solution)/shard_map/ppermute | solution.py:85
  163.6 89.9 %collective-permute-start.4 = (bf16[2,4,48,3072]{3,2,1,0:T(8,128)(2,1)}, bf16[2,4,48,3072]{3,2,1,0:T(8,128)(2,1)}, u32[]{:S(2)}, u32[]{:S(2)}) collective-permute-start(bf16[2,4,48,3072]{3,2,1,0:T(8,128)(2,1)} %pad_maximum_fusion.5), channel_id=1, source_target_pairs={{0,1},{1,0},{2,3},{3,2},{4,5},{5,4},{6,7},{7,6},{8,9},{9,8},{10,11... | collective-permute-start | bytes 7077896 | tf_op jit(solution)/shard_map/ppermute | solution.py:85
  244.0 32.8 %all-to-all-start.1 = ((bf16[8,152,768]{2,1,0:T(8,128)(2,1)}), bf16[8,152,768]{2,1,0:T(8,128)(2,1)}, u32[]{:S(2)}, u32[]{:S(2)}) async-start(bf16[8,152,768]{2,1,0:T(8,128)(2,1)} %bitcast.261), calls=%async_computation.1 | async-start | bytes 3735552 | tf_op jit(solution)/shard_map/all_to_all | solution.py:118
  301.0 31.4 %all-to-all-start.4 = ((bf16[8,152,768]{2,1,0:T(8,128)(2,1)}), bf16[8,152,768]{2,1,0:T(8,128)(2,1)}, u32[]{:S(2)}, u32[]{:S(2)}) async-start(bf16[8,152,768]{2,1,0:T(8,128)(2,1)} %bitcast.264), calls=%async_computation.4 | async-start | bytes 3735552 | tf_op jit(solution)/shard_map/all_to_all | solution.py:121
  339.9 30.9 %all-to-all-start.5 = ((bf16[8,152,768]{2,1,0:T(8,128)(2,1)}), bf16[8,152,768]{2,1,0:T(8,128)(2,1)}, u32[]{:S(2)}, u32[]{:S(2)}) async-start(bf16[8,152,768]{2,1,0:T(8,128)(2,1)} %bitcast.262), calls=%async_computation.5 | async-start | bytes 3735552 | tf_op jit(solution)/shard_map/all_to_all | solution.py:118
  401.1 32.0 %all-to-all-start.6 = ((bf16[8,152,768]{2,1,0:T(8,128)(2,1)}), bf16[8,152,768]{2,1,0:T(8,128)(2,1)}, u32[]{:S(2)}, u32[]{:S(2)}) async-start(bf16[8,152,768]{2,1,0:T(8,128)(2,1)} %bitcast.263), calls=%async_computation.6 | async-start | bytes 3735552 | tf_op jit(solution)/shard_map/all_to_all | solution.py:121
  417.6 155.1 %collective-permute-start.10 = (bf16[2,4,48,3072]{3,2,1,0:T(8,128)(2,1)}, bf16[2,4,48,3072]{3,2,1,0:T(8,128)(2,1)}, u32[]{:S(2)}, u32[]{:S(2)}) collective-permute-start(bf16[2,4,48,3072]{3,2,1,0:T(8,128)(2,1)} %dynamic-slice_bitcast_fusion.2), channel_id=1, source_target_pairs={{0,1},{1,0},{2,3},{3,2},{4,5},{5,4},{6,7},{7,6},{8,9},{9,8},{10,11... | collective-permute-start | bytes 7077896 | tf_op jit(solution)/shard_map/ppermute | solution.py:85
  432.6 144.7 %collective-permute-start.12 = (bf16[2,4,192,768]{3,2,1,0:T(8,128)(2,1)}, bf16[2,4,192,768]{3,2,1,0:T(8,128)(2,1)}, u32[]{:S(2)}, u32[]{:S(2)}) collective-permute-start(bf16[2,4,192,768]{3,2,1,0:T(8,128)(2,1)} %dynamic-slice_bitcast_fusion.1), channel_id=1, source_target_pairs={{0,1},{1,0},{2,3},{3,2},{4,5},{5,4},{6,7},{7,6},{8,9},{9,8},{10,11... | collective-permute-start | bytes 7077896 | tf_op jit(solution)/shard_map/ppermute | solution.py:85
  572.6 10.6 %collective-permute-start.7 = (bf16[2,4,2,24,3200]{4,3,2,1,0:T(8,128)(2,1)}, bf16[2,4,2,24,3200]{4,3,2,1,0:T(8,128)(2,1)}, u32[]{:S(2)}, u32[]{:S(2)}) collective-permute-start(bf16[2,4,2,24,3200]{4,3,2,1,0:T(8,128)(2,1)} %dynamic-slice_bitcast_fusion), channel_id=1, source_target_pairs={{0,1},{1,0},{2,3},{3,2},{4,5},{5,4},{6,7},{7,6},{8,9},{9,8},{10,11... | collective-permute-start | bytes 7372808 | tf_op jit(solution)/shard_map/ppermute | solution.py:85
  576.1 80.4 %collective-permute-start.11 = (bf16[4,48,3072]{2,1,0:T(8,128)(2,1)S(1)}, bf16[4,48,3072]{2,1,0:T(8,128)(2,1)S(1)}, u32[]{:S(2)}, u32[]{:S(2)}) collective-permute-start(bf16[4,48,3072]{2,1,0:T(8,128)(2,1)S(1)} %dynamic-slice_bitcast_fusion.5), channel_id=1, source_target_pairs={{0,8},{8,0},{1,9},{9,1},{2,10},{10,2},{3,11},{11,3},{4,12},{12,4},... | collective-permute-start | bytes 3538952 | tf_op jit(solution)/shard_map/ppermute | solution.py:85
  581.6 99.8 %collective-permute-start.13 = (bf16[4,192,768]{2,1,0:T(8,128)(2,1)}, bf16[4,192,768]{2,1,0:T(8,128)(2,1)}, u32[]{:S(2)}, u32[]{:S(2)}) collective-permute-start(bf16[4,192,768]{2,1,0:T(8,128)(2,1)} %dynamic-slice_bitcast_fusion.4), channel_id=1, source_target_pairs={{0,8},{8,0},{1,9},{9,1},{2,10},{10,2},{3,11},{11,3},{4,12},{12,4},... | collective-permute-start | bytes 3538952 | tf_op jit(solution)/shard_map/ppermute | solution.py:85
  588.1 96.2 %collective-permute-start.8 = (bf16[4,2,24,3200]{3,2,1,0:T(8,128)(2,1)}, bf16[4,2,24,3200]{3,2,1,0:T(8,128)(2,1)}, u32[]{:S(2)}, u32[]{:S(2)}) collective-permute-start(bf16[4,2,24,3200]{3,2,1,0:T(8,128)(2,1)} %dynamic-slice_bitcast_fusion.3), channel_id=1, source_target_pairs={{0,16},{16,0},{1,17},{17,1},{2,18},{18,2},{3,19},{19,3},{4,20},{20... | collective-permute-start | bytes 3686408 | tf_op jit(solution)/shard_map/ppermute | solution.py:85
  658.0 36.0 %all-to-all-start.8 = ((bf16[4,48,3072]{2,1,0:T(8,128)(2,1)}), bf16[4,48,3072]{2,1,0:T(8,128)(2,1)}, u32[]{:S(2)}, u32[]{:S(2)}) async-start(bf16[4,48,3072]{2,1,0:T(8,128)(2,1)} %fusion.55), calls=%async_computation.8 | async-start | bytes 2359296 | tf_op jit(solution)/shard_map/all_to_all | solution.py:134
  694.0 35.2 %all-to-all-start.9 = ((bf16[4,192,768]{2,1,0:T(8,128)(2,1)}), bf16[4,192,768]{2,1,0:T(8,128)(2,1)}, u32[]{:S(2)}, u32[]{:S(2)}) async-start(bf16[4,192,768]{2,1,0:T(8,128)(2,1)} %fusion.54), calls=%async_computation.9 | async-start | bytes 2359296 | tf_op jit(solution)/shard_map/all_to_all | solution.py:134
  700.2 26.8 %collective-permute-start.9 = (bf16[4,24,3200]{2,1,0:T(8,128)(2,1)}, bf16[4,24,3200]{2,1,0:T(8,128)(2,1)S(1)}, u32[]{:S(2)}, u32[]{:S(2)}) collective-permute-start(bf16[4,24,3200]{2,1,0:T(8,128)(2,1)} %dynamic-slice_bitcast_fusion.6), channel_id=1, source_target_pairs={{0,2},{2,0},{1,3},{3,1},{4,6},{6,4},{5,7},{7,5},{8,10},{10,8},{9,1... | collective-permute-start | bytes 1843208 | tf_op jit(solution)/shard_map/ppermute | solution.py:85
  729.2 19.8 %all-to-all-start.7 = ((bf16[4,24,3200]{2,1,0:T(8,128)(2,1)}), bf16[4,24,3200]{2,1,0:T(8,128)(2,1)S(1)}, u32[]{:S(2)}, u32[]{:S(2)}) async-start(bf16[4,24,3200]{2,1,0:T(8,128)(2,1)} %fusion.85), calls=%async_computation.7 | async-start | bytes 1228800 | tf_op jit(solution)/shard_map/all_to_all | solution.py:114
  (63 other events, 744.0 us)

commit v2 on v1

v2 whole, which is shorter than its diff:
```python
import math

import jax
import jax.numpy as jnp
from jax import lax
from jax.experimental import pallas as pl
from jax.experimental.pallas import tpu as pltpu
from jax.sharding import Mesh, PartitionSpec as P

HEADS = 12
HEAD_DIM = 64
EXPERTS = 8
SEQ = 576
CAP = 152
SLOTS = EXPERTS * CAP
NORM_EPSILON = 1e-06
SCALE = HEAD_DIM ** (-0.5)
PAIR = 2 * HEAD_DIM
PAIRS = HEADS // 2
WIDTH = HEADS * HEAD_DIM
LANES = 128
GAIN_ONE = EXPERTS
GAIN_TWO = EXPERTS + 1
TOKEN_BLOCK = 192
ROW_BLOCK = 304
F_BLOCK = 512
F32 = jnp.float32
BF16 = jnp.bfloat16
QUICK = pl.CostEstimate(flops=1, bytes_accessed=1, transcendentals=0)


def dot_nn(left, right):
    return jnp.dot(left, right, preferred_element_type=F32)


def dot_nt(left, right):
    return lax.dot_general(left, right, (((1,), (1,)), ((), ())), preferred_element_type=F32)


def dot_tn(left, right):
    return lax.dot_general(left, right, (((0,), (0,)), ((), ())), preferred_element_type=F32)


def scaled(values):
    return values * jnp.asarray(SCALE, BF16)


def norm_parts(values):
    centre = values - jnp.mean(values, axis=-1, keepdims=True)
    inverse = lax.rsqrt(jnp.mean(centre * centre, axis=-1, keepdims=True) + NORM_EPSILON)
    return centre * inverse, inverse


def norm_back(grad_normed, normed, inverse):
    mean_grad = jnp.mean(grad_normed, axis=-1, keepdims=True)
    mean_cross = jnp.mean(grad_normed * normed, axis=-1, keepdims=True)
    return (grad_normed - mean_grad - normed * mean_cross) * inverse


def whole(*shape):
    return pl.BlockSpec(shape, lambda *at: (0,) * len(shape))


def call(name, kernel, grid, in_specs, out_specs, out_shape, scratch=(), scalars=0):
    return pl.pallas_call(
        kernel,
        grid_spec=pltpu.PrefetchScalarGridSpec(
            num_scalar_prefetch=scalars,
            grid=grid,
            in_specs=in_specs,
            out_specs=out_specs,
            scratch_shapes=scratch,
        ),
        out_shape=out_shape,
        cost_estimate=QUICK,
        name=name,
    )


def struct(shape, dtype):
    return jax.ShapeDtypeStruct(shape, dtype)


def attention_kernel(qkv_ref, out_ref, log_ref):
    values_t = qkv_ref[:, 2 * PAIR :].T
    outs = []
    for head in range(2):
        at = head * HEAD_DIM
        queries = scaled(qkv_ref[:, at : at + HEAD_DIM])
        keys = qkv_ref[:, PAIR + at : PAIR + at + HEAD_DIM]
        scores = dot_nt(keys, queries)
        largest = jnp.max(scores, axis=0, keepdims=True)
        powers = jnp.exp(scores - largest)
        totals = jnp.sum(powers, axis=0, keepdims=True)
        mixed = dot_nn(values_t[at : at + HEAD_DIM], powers.astype(BF16))
        outs.append((mixed / totals).astype(BF16))
        log_ref[0, 0, head : head + 1, :] = largest + jnp.log(totals)
    out_ref[...] = jnp.concatenate(outs, axis=0).T


def attention_back_kernel(qkv_ref, out_ref, log_ref, grad_ref, result_ref):
    products = out_ref[...].T.astype(F32) * grad_ref[...].T.astype(F32)
    keys_t = scaled(qkv_ref[:, PAIR : 2 * PAIR]).T
    grad_queries = []
    for head in range(2):
        at = head * HEAD_DIM
        span = slice(at, at + HEAD_DIM)
        queries = scaled(qkv_ref[:, span])
        keys = qkv_ref[:, PAIR + at : PAIR + at + HEAD_DIM]
        values = qkv_ref[:, 2 * PAIR + at : 2 * PAIR + at + HEAD_DIM]
        grads = grad_ref[:, span]
        row_terms = jnp.sum(products[span], axis=0, keepdims=True)
        probs = jnp.exp(dot_nt(keys, queries) - log_ref[0, 0, head : head + 1, :])
        grad_scores = (probs * (dot_nt(values, grads) - row_terms)).astype(BF16)
        grad_values = dot_nn(probs.astype(BF16), grads)
        grad_keys = dot_nn(grad_scores, queries)
        result_ref[:, 2 * PAIR + at : 2 * PAIR + at + HEAD_DIM] = grad_values.astype(BF16)
        result_ref[:, PAIR + at : PAIR + at + HEAD_DIM] = grad_keys.astype(BF16)
        grad_queries.append(dot_nn(keys_t[span], grad_scores).astype(BF16))
    result_ref[:, :PAIR] = jnp.concatenate(grad_queries, axis=0).T


def attention_specs():
    return (
        pl.BlockSpec((SEQ, 3 * PAIR), lambda image, pair: (image, pair)),
        pl.BlockSpec((SEQ, PAIR), lambda image, pair: (image, pair)),
        pl.BlockSpec((1, 1, 2, SEQ), lambda image, pair: (image, pair, 0, 0)),
    )


def attention_forward(qkv):
    rows = qkv.shape[0]
    images = rows // SEQ
    wide, narrow, logs = attention_specs()
    return call(
        "attention_forward",
        attention_kernel,
        (images, PAIRS),
        [wide],
        [narrow, logs],
        [struct((rows, WIDTH), BF16), struct((images, PAIRS, 2, SEQ), F32)],
    )(qkv)


def attention_backward(qkv, attended, logs_saved, grad_attended):
    wide, narrow, logs = attention_specs()
    return call(
        "attention_backward",
        attention_back_kernel,
        (qkv.shape[0] // SEQ, PAIRS),
        [wide, narrow, logs, narrow],
        wide,
        struct(qkv.shape, BF16),
    )(qkv, attended, logs_saved, grad_attended)


QKV_SPEC = pl.BlockSpec((WIDTH, 3 * WIDTH), lambda *at: (0, 0))
PROJ_SPEC = pl.BlockSpec((WIDTH, WIDTH), lambda *at: (0, 3))
SMALL_SPEC = pl.BlockSpec((WIDTH, LANES), lambda *at: (0, 4 * WIDTH // LANES))


def project_kernel(tokens_ref, weight_ref, small_ref, qkv_ref, act_ref, table_ref):
    @pl.when(pl.program_id(0) == 0)
    def _():
        table = small_ref[...].T
        table_ref[...] = table
        gain = table[GAIN_ONE : GAIN_ONE + 1].astype(F32)
        normed, _ = norm_parts(tokens_ref[...].astype(F32))
        act_ref[...] = (normed * gain).astype(BF16)

    qkv_ref[...] = dot_nn(act_ref[...], weight_ref[...]).astype(BF16)


def project(tokens, dense):
    rows = tokens.shape[0]
    return call(
        "project",
        project_kernel,
        (PAIRS,),
        [
            whole(rows, WIDTH),
            pl.BlockSpec((WIDTH, 3 * PAIR), lambda pair: (0, pair)),
            SMALL_SPEC,
        ],
        [
            pl.BlockSpec((rows, 3 * PAIR), lambda pair: (0, pair)),
            whole(rows, WIDTH),
            whole(LANES, WIDTH),
        ],
        [
            struct((rows, 3 * WIDTH), BF16),
            struct((rows, WIDTH), BF16),
            struct((LANES, WIDTH), BF16),
        ],
    )(tokens, dense, dense)


def slot_hits(routes_ref, slots_ref):
    rows = routes_ref.shape[1]
    places = lax.broadcasted_iota(jnp.int32, (CAP, rows), 0)
    expert = pl.program_id(0)
    return [
        (routes_ref[k : k + 1, :] == expert) & (slots_ref[k : k + 1, :] == places)
        for k in range(2)
    ]


def middle_kernel(
    routes_ref, slots_ref, tokens_ref, attended_ref, proj_ref, table_ref,
    mid_ref, act_ref, columns_ref, gates_ref, slot_rows_ref,
):
    @pl.when(pl.program_id(0) == 0)
    def _():
        mid = tokens_ref[...].astype(F32) + dot_nn(attended_ref[...], proj_ref[...])
        mid_ref[...] = mid
        normed, _ = norm_parts(mid)
        gain = table_ref[GAIN_TWO : GAIN_TWO + 1, :].astype(F32)
        act = (normed * gain).astype(BF16)
        act_ref[...] = act
        logits = dot_nt(table_ref[:16, :], act)[:EXPERTS]
        powers = jnp.exp(logits - jnp.max(logits, axis=0, keepdims=True))
        router = powers / jnp.sum(powers, axis=0, keepdims=True)
        names = lax.broadcasted_iota(jnp.int32, router.shape, 0)
        gates = [
            jnp.sum(jnp.where(names == routes_ref[k : k + 1, :], router, 0.0), axis=0, keepdims=True)
            .astype(BF16)
            .astype(F32)
            for k in range(2)
        ]
        rows = router.shape[1]
        gates = jnp.concatenate(gates + [jnp.zeros((EXPERTS - 2, rows), F32)], axis=0)
        gates_ref[...] = gates
        spare = jnp.zeros((LANES - 2 * EXPERTS, rows), F32)
        columns_ref[...] = jnp.concatenate([router, gates, spare], axis=0).T

    first, second = slot_hits(routes_ref, slots_ref)
    dispatch = jnp.where(first | second, 1.0, 0.0).astype(BF16)
    slot_rows_ref[0] = dot_nn(dispatch, act_ref[...]).astype(BF16)


def middle(routes_t, slots_t, tokens, attended, dense, table):
    rows = tokens.shape[0]
    return call(
        "middle",
        middle_kernel,
        (EXPERTS,),
        [
            whole(2, rows),
            whole(2, rows),
            whole(rows, WIDTH),
            whole(rows, WIDTH),
            PROJ_SPEC,
            whole(LANES, WIDTH),
        ],
        [
            whole(rows, WIDTH),
            whole(rows, WIDTH),
            whole(rows, LANES),
            whole(EXPERTS, rows),
            pl.BlockSpec((1, CAP, WIDTH), lambda expert: (expert, 0, 0)),
        ],
        [
            struct((rows, WIDTH), F32),
            struct((rows, WIDTH), BF16),
            struct((rows, LANES), F32),
            struct((EXPERTS, rows), F32),
            struct((EXPERTS, CAP, WIDTH), BF16),
        ],
    )(routes_t, slots_t, tokens, attended, dense, table)


def slot_grads_kernel(routes_ref, slots_ref, gates_ref, grad_ref, result_ref):
    first, second = slot_hits(routes_ref, slots_ref)
    combine = jnp.where(first, gates_ref[0:1, :], jnp.where(second, gates_ref[1:2, :], 0.0))
    result_ref[0] = dot_nn(combine.astype(BF16), grad_ref[...]).astype(BF16)


def slot_grads(routes_t, slots_t, gates, cotangent):
    rows = cotangent.shape[0]
    return call(
        "slot_grads",
        slot_grads_kernel,
        (EXPERTS,),
        [whole(2, rows), whole(2, rows), whole(EXPERTS, rows), whole(rows, WIDTH)],
        pl.BlockSpec((1, CAP, WIDTH), lambda expert: (expert, 0, 0)),
        struct((EXPERTS, CAP, WIDTH), BF16),
    )(routes_t, slots_t, gates, cotangent)


def expert_up_kernel(rows_ref, weight_ref, hidden_ref, slope_ref):
    root = math.sqrt(2.0 / math.pi)
    value = dot_nn(rows_ref[...], weight_ref[...])
    square = value * value
    curve = jnp.tanh(value * (root + (root * 0.044715) * square))
    upper = 0.5 + 0.5 * curve
    hidden_ref[...] = (value * upper).astype(BF16)
    inner = value * (root + (3.0 * root * 0.044715) * square)
    slope_ref[...] = (upper + (0.5 - 0.5 * curve * curve) * inner).astype(BF16)


def expert_up(rows, weight):
    count, depth = rows.shape[0], weight.shape[1]
    wide = pl.BlockSpec((count, F_BLOCK), lambda f: (0, f))
    return call(
        "expert_up",
        expert_up_kernel,
        (depth // F_BLOCK,),
        [whole(count, WIDTH), pl.BlockSpec((WIDTH, F_BLOCK), lambda f: (0, f))],
        [wide, wide],
        [struct((count, depth), BF16)] * 2,
    )(rows, weight)


def expert_down_kernel(hidden_ref, weight_ref, result_ref):
    result_ref[...] = dot_nn(hidden_ref[...], weight_ref[...]).astype(BF16)


def expert_down(hidden, weight):
    count, depth = hidden.shape
    return call(
        "expert_down",
        expert_down_kernel,
        (count // ROW_BLOCK,),
        [pl.BlockSpec((ROW_BLOCK, depth), lambda r: (r, 0)), whole(depth, WIDTH)],
        pl.BlockSpec((ROW_BLOCK, WIDTH), lambda r: (r, 0)),
        struct((count, WIDTH), BF16),
    )(hidden, weight)


def expert_back_kernel(grad_ref, slope_ref, out_ref, in_ref, grad_pre_ref, grad_rows_ref):
    grad_hidden = dot_nt(grad_ref[...], out_ref[...])
    grad_pre = (grad_hidden * slope_ref[...].astype(F32)).astype(BF16)
    grad_pre_ref[...] = grad_pre
    grad_rows_ref[...] = dot_nt(grad_pre, in_ref[...]).astype(BF16)


def expert_back(grad_result, slope, weight_out, weight_in):
    count, depth = slope.shape
    wide = pl.BlockSpec((ROW_BLOCK, depth), lambda r: (r, 0))
    narrow = pl.BlockSpec((ROW_BLOCK, WIDTH), lambda r: (r, 0))
    return call(
        "expert_back",
        expert_back_kernel,
        (count // ROW_BLOCK,),
        [narrow, wide, whole(depth, WIDTH), whole(WIDTH, depth)],
        [wide, narrow],
        [struct((count, depth), BF16), struct((count, WIDTH), BF16)],
    )(grad_result, slope, weight_out, weight_in)


def out_grad_kernel(me_ref, hidden_ref, grad_ref, mine_ref, theirs_ref):
    value = dot_tn(hidden_ref[...], grad_ref[...]).astype(BF16)
    half = value.shape[0] // 2
    first = me_ref[0] == 0
    mine_ref[0, 0] = jnp.where(first, value[:half], value[half:])
    theirs_ref[0, 0] = jnp.where(first, value[half:], value[:half])


def out_grad(me, hidden, grad_result):
    count, depth = hidden.shape
    rest = depth // 16
    half = pl.BlockSpec((1, 1, rest, WIDTH), lambda f, me: (f // 4, lax.rem(f, 4), 0, 0))
    return call(
        "out_grad",
        out_grad_kernel,
        (8,),
        [pl.BlockSpec((count, 2 * rest), lambda f, me: (0, f)), whole(count, WIDTH)],
        [half, half],
        [struct((2, 4, rest, WIDTH), BF16)] * 2,
        scalars=1,
    )(me, hidden, grad_result)


def in_grad_kernel(me_ref, rows_ref, grad_ref, mine_ref, theirs_ref, turned_ref):
    @pl.when(pl.program_id(0) == 0)
    def _():
        turned_ref[...] = rows_ref[...].T

    value = dot_nn(turned_ref[...], grad_ref[...]).astype(BF16)
    value = value.reshape(8, 2, WIDTH // 16, F_BLOCK)
    first = me_ref[0] == 0
    shape = mine_ref.shape
    mine_ref[...] = jnp.where(first, value[:, 0], value[:, 1]).reshape(shape)
    theirs_ref[...] = jnp.where(first, value[:, 1], value[:, 0]).reshape(shape)


def in_grad(me, rows, grad_pre):
    count, depth = grad_pre.shape
    rest = WIDTH // 16
    half = pl.BlockSpec((2, 4, rest, F_BLOCK), lambda f, me: (0, 0, 0, f))
    return call(
        "in_grad",
        in_grad_kernel,
        (depth // F_BLOCK,),
        [whole(count, WIDTH), pl.BlockSpec((count, F_BLOCK), lambda f, me: (0, f))],
        [half, half],
        [struct((2, 4, rest, depth), BF16)] * 2,
        scratch=[pltpu.VMEM((WIDTH, count), BF16)],
        scalars=1,
    )(me, rows, grad_pre)


def token_hits(targets_ref):
    columns = lax.broadcasted_iota(jnp.int32, (targets_ref.shape[0], SLOTS), 1)
    return [targets_ref[:, k : k + 1] == columns for k in range(2)]


def combine_kernel(
    routes_ref, targets_ref, columns_ref, mid_ref, grad_ref, result_ref, output_ref, logits_ref
):
    first, second = token_hits(targets_ref)
    gates = columns_ref[:, EXPERTS : EXPERTS + 2]
    combine = jnp.where(first, gates[:, 0:1], jnp.where(second, gates[:, 1:2], 0.0)).astype(BF16)
    output_ref[...] = (mid_ref[...] + dot_nn(combine, result_ref[...])).astype(BF16)
    crossed = dot_nt(grad_ref[...], result_ref[...])
    lanes = lax.broadcasted_iota(jnp.int32, columns_ref.shape, 1)
    grad_router = jnp.zeros(columns_ref.shape, F32)
    for k, hits in enumerate((first, second)):
        grad_gate = jnp.sum(jnp.where(hits, crossed, 0.0), axis=1, keepdims=True)
        grad_router += jnp.where(lanes == routes_ref[:, k : k + 1], grad_gate, 0.0)
    router = jnp.where(lanes < EXPERTS, columns_ref[...], 0.0)
    total = jnp.sum(router * grad_router, axis=1, keepdims=True)
    logits_ref[...] = (router * (grad_router - total)).astype(BF16)


def token_spec(columns):
    return pl.BlockSpec((TOKEN_BLOCK, columns), lambda t: (t, 0))


def combine_results(routes, targets, columns, mid, cotangent, result):
    rows = mid.shape[0]
    return call(
        "combine",
        combine_kernel,
        (rows // TOKEN_BLOCK,),
        [
            token_spec(2),
            token_spec(2),
            token_spec(LANES),
            token_spec(WIDTH),
            token_spec(WIDTH),
            whole(SLOTS, WIDTH),
        ],
        [token_spec(WIDTH), token_spec(LANES)],
        [struct((rows, WIDTH), BF16), struct((rows, LANES), BF16)],
    )(routes, targets, columns, mid, cotangent, result)


def middle_back_kernel(
    targets_ref, logits_ref, mid_ref, grad_ref, rows_ref, proj_ref, table_ref,
    grad_mid_ref, low_ref, attended_ref, gain_ref,
):
    first, second = token_hits(targets_ref)
    dispatch = jnp.where(first | second, 1.0, 0.0).astype(BF16)
    grad_act = dot_nn(dispatch, rows_ref[...]) + dot_nn(logits_ref[...], table_ref[...])
    normed, inverse = norm_parts(mid_ref[...])
    gain = table_ref[GAIN_TWO : GAIN_TWO + 1, :].astype(F32)
    part = jnp.sum(grad_act * normed, axis=0, keepdims=True)

    @pl.when(pl.program_id(0) == 0)
    def _():
        gain_ref[...] = jnp.zeros_like(gain_ref)

    gain_ref[0:1, :] += part
    grad_mid = grad_ref[...].astype(F32) + norm_back(grad_act * gain, normed, inverse)
    grad_mid_ref[...] = grad_mid
    low = grad_mid.astype(BF16)
    low_ref[...] = low
    attended_ref[...] = dot_nt(low, proj_ref[...]).astype(BF16)


def middle_back(targets, logits, mid, cotangent, grad_rows, dense, table):
    rows = mid.shape[0]
    return call(
        "middle_back",
        middle_back_kernel,
        (rows // TOKEN_BLOCK,),
        [
            token_spec(2),
            token_spec(LANES),
            token_spec(WIDTH),
            token_spec(WIDTH),
            whole(SLOTS, WIDTH),
            PROJ_SPEC,
            whole(LANES, WIDTH),
        ],
        [token_spec(WIDTH), token_spec(WIDTH), token_spec(WIDTH), whole(8, WIDTH)],
        [
            struct((rows, WIDTH), F32),
            struct((rows, WIDTH), BF16),
            struct((rows, WIDTH), BF16),
            struct((8, WIDTH), F32),
        ],
    )(targets, logits, mid, cotangent, grad_rows, dense, table)


def proj_grads_kernel(attended_ref, low_ref, act_ref, logits_ref, gain_ref, result_ref):
    result_ref[:, :WIDTH] = dot_tn(attended_ref[...], low_ref[...]).astype(BF16)
    small = dot_tn(act_ref[...], logits_ref[...])
    lanes = lax.broadcasted_iota(jnp.int32, small.shape, 1)
    gain = gain_ref[...].T[:, 0:1]
    result_ref[:, WIDTH:] = jnp.where(lanes == GAIN_TWO, gain, small).astype(BF16)


def proj_grads(attended, low, act_two, logits, gain):
    rows = low.shape[0]
    return call(
        "proj_grads",
        proj_grads_kernel,
        (1,),
        [whole(rows, WIDTH)] * 3 + [whole(rows, LANES), whole(8, WIDTH)],
        whole(WIDTH, WIDTH + LANES),
        struct((WIDTH, WIDTH + LANES), BF16),
    )(attended, low, act_two, logits, gain)


def qkv_grads_kernel(act_ref, grad_ref, result_ref, turned_ref):
    @pl.when(pl.program_id(0) == 0)
    def _():
        turned_ref[...] = act_ref[...].T

    result_ref[...] = dot_nn(turned_ref[...], grad_ref[...]).astype(BF16)


def qkv_grads(act_one, grad_qkv):
    rows = act_one.shape[0]
    return call(
        "qkv_grads",
        qkv_grads_kernel,
        (PAIRS,),
        [whole(rows, WIDTH), pl.BlockSpec((rows, 3 * PAIR), lambda pair: (0, pair))],
        pl.BlockSpec((WIDTH, 3 * PAIR), lambda pair: (0, pair)),
        struct((WIDTH, 3 * WIDTH), BF16),
        scratch=[pltpu.VMEM((WIDTH, rows), BF16)],
    )(act_one, grad_qkv)


def token_grads_kernel(grad_ref, weight_ref, tokens_ref, grad_mid_ref, table_ref, result_ref):
    grad_act = dot_nt(grad_ref[...], weight_ref[...])
    normed, inverse = norm_parts(tokens_ref[...].astype(F32))
    gain = table_ref[GAIN_ONE : GAIN_ONE + 1, :].astype(F32)
    result_ref[...] = grad_mid_ref[...] + norm_back(grad_act * gain, normed, inverse)


def token_grads(grad_qkv, dense, tokens, grad_mid, table):
    rows = tokens.shape[0]
    return call(
        "token_grads",
        token_grads_kernel,
        (rows // TOKEN_BLOCK,),
        [token_spec(3 * WIDTH), QKV_SPEC, token_spec(WIDTH), token_spec(WIDTH), whole(LANES, WIDTH)],
        token_spec(WIDTH),
        struct((rows, WIDTH), F32),
    )(grad_qkv, dense, tokens, grad_mid, table)


def by_pair(columns):
    rows = columns.shape[0]
    return columns.reshape(rows, 3, PAIRS, PAIR).transpose(0, 2, 1, 3).reshape(rows, -1)


def by_part(columns):
    rows = columns.shape[0]
    return columns.reshape(rows, PAIRS, 3, PAIR).transpose(0, 2, 1, 3).reshape(rows, -1)


def place_kernel(count, me_ref, *refs):
    pieces, result_ref = refs[:-1], refs[-1]
    at = 0
    for axis in range(count):
        at = 2 * at + lax.rem(pl.program_id(axis) + me_ref[axis], 2)
    for index, piece in enumerate(pieces):

        @pl.when(at == index)
        def _():
            result_ref[...] = piece[...].reshape(result_ref.shape)


def place(me, pieces, axes):
    count = len(axes)
    shape = list(pieces[0].shape)
    for axis in axes:
        shape.insert(axis, 2)
    block = [1 if axis in axes else size for axis, size in enumerate(shape)]

    def index(*at):
        return tuple(at[axes.index(a)] if a in axes else 0 for a in range(len(shape)))

    return call(
        "place",
        lambda *refs: place_kernel(count, *refs),
        (2,) * count,
        [whole(*piece.shape) for piece in pieces],
        pl.BlockSpec(tuple(block), index),
        struct(tuple(shape), pieces[0].dtype),
        scalars=1,
    )(me, *pieces)


def together(*values):
    return lax.optimization_barrier(values)


def add(mine, got):
    return (mine.astype(F32) + got.astype(F32)).astype(BF16)


class PairwiseLinks:
    def __init__(self, mesh):
        self.mesh = Mesh(mesh.devices.reshape(2, 2, 2, 2, 2), ("x", "zh", "zl", "y", "c"))
        self.data = ("x", "zh", "zl", "y", "c")
        self.fsdp = ("zh", "zl", "y", "c")
        self.dp = "x"

    def swap(self, value, axis):
        return lax.ppermute(value, axis, [(0, 1), (1, 0)])

    def trade(self, value, axes):
        return lax.all_to_all(value, axes, 0, 0, tiled=True)

    def place_of(self, *axes):
        return jnp.stack([lax.axis_index(axis) for axis in axes]).astype(jnp.int32)

    def half(self, value, axis, at, other):
        first = lax.axis_index(axis) == (1 if other else 0)
        low = lax.index_in_dim(value, 0, at, keepdims=False)
        high = lax.index_in_dim(value, 1, at, keepdims=False)
        return jnp.where(first, low, high)

    def add_halves(self, value, axis, at):
        got = self.swap(self.half(value, axis, at, True), axis)
        return add(self.half(value, axis, at, False), got)

    def gather_all(self, dense, w_in, w_out):
        rows, columns = dense.shape
        in_raw = self.swap(w_in, "zh")
        copies = jnp.broadcast_to(dense[None], (4, rows, columns))
        own = self.trade(copies, ("zh", "zl"))
        in_near = self.trade(w_in, ("zl", "y"))
        over_y = self.swap(own, "y")
        over_x = self.swap(own, "x")
        over_xy = self.swap(over_y, "x")
        pieces = [own, over_y, over_x, over_xy]
        pieces = [piece for near in pieces for piece in (near, self.swap(near, "c"))]
        full = place(self.place_of("x", "y", "c"), pieces, (0, 2, 3)).reshape(32 * rows, columns)

        def finish(near, far):
            pieces = [near, self.swap(near, "c"), far, self.swap(far, "c")]
            joined = place(self.place_of("zh", "c"), pieces, (0, 2))
            return joined.reshape(-1, near.shape[-1])

        def finish_in(signal):
            signal, raw = together(signal, in_raw)
            return signal, finish(in_near, self.trade(raw, ("zl", "y")))

        out_near = self.trade(w_out, ("zl", "y"))
        out_far = self.swap(out_near, "zh")

        def finish_out(signal):
            signal, far = together(signal, out_far)
            return signal, finish(out_near, far)

        return full, finish_in, finish_out

    def send_slots(self, slots):
        return self.trade(slots, ("x", "zl", "y"))

    def return_slots(self, slots):
        return self.trade(slots, ("x", "zl", "y"))

    def core(self):
        return self.place_of("c")

    def expert_cores(self, mine, theirs):
        return add(mine, self.swap(theirs, "c"))

    def expert_far(self, part):
        got = self.swap(self.half(part, "zh", 0, True), "zh")
        return self.half(part, "zh", 0, False), got

    def expert_end(self, mine, got):
        return self.trade(add(mine, got), ("zl", "y")).astype(F32)

    def scatter_rows(self, value):
        rows, columns = value.shape
        part = value.reshape(2, 4, 2, 2, rows // 32, columns)
        part = self.add_halves(part, "c", 3)
        part = self.add_halves(part, "x", 0)
        part = self.add_halves(part, "y", 1)
        return jnp.sum(self.trade(part, ("zh", "zl")).astype(F32), axis=0)


class AxisLinks:
    def __init__(self, mesh):
        self.mesh = mesh
        self.data = ("dp", "fsdp")
        self.fsdp = "fsdp"
        self.dp = "dp"

    def gather_all(self, dense, w_in, w_out):
        def finish(shard):
            return lambda signal: (
                signal,
                lax.all_gather(shard, "fsdp", axis=1, tiled=True).reshape(-1, shard.shape[-1]),
            )

        return lax.all_gather(dense, self.data, axis=0, tiled=True), finish(w_in), finish(w_out)

    def send_slots(self, slots):
        return lax.all_to_all(slots, "dp", 0, 0, tiled=True)

    def return_slots(self, slots):
        return lax.all_to_all(slots, "dp", 0, 0, tiled=True)

    def core(self):
        return jnp.zeros((1,), jnp.int32)

    def expert_cores(self, mine, theirs):
        return jnp.stack([mine, theirs], axis=2)

    def expert_far(self, part):
        return part, None

    def expert_end(self, part, got):
        grad = part.reshape(1, -1, part.shape[-1])
        return lax.psum_scatter(grad, "fsdp", scatter_dimension=1, tiled=True).astype(F32)

    def scatter_rows(self, value):
        return lax.psum_scatter(value.astype(F32), self.data, scatter_dimension=0, tiled=True)


def per_device(
    links, tokens, gain_attn, w_qkv, w_proj, gain_moe, w_router, w_in, w_out, routes, slot_ids, cotangent
):
    small = jnp.concatenate([w_router, gain_attn[:, None], gain_moe[:, None]], axis=1)
    small = jnp.pad(small, ((0, 0), (0, LANES - small.shape[1])))
    own_qkv = by_pair(w_qkv)
    dense, finish_in, finish_out = links.gather_all(
        jnp.concatenate([own_qkv, w_proj, small], axis=1), w_in, w_out
    )
    routes_t = routes.T
    slots_t = slot_ids.T
    targets = jnp.where(slot_ids < CAP, routes * CAP + slot_ids, -1)

    qkv, act_one, table = project(tokens, dense)
    attended, logs = attention_forward(qkv)
    mid, act_two, columns, gates, rows_sent = middle(
        routes_t, slots_t, tokens, attended, dense, table
    )
    rows_sent, expert_in = finish_in(rows_sent)
    slot_rows = links.send_slots(rows_sent)
    grads_sent, slot_rows = together(slot_grads(routes_t, slots_t, gates, cotangent), slot_rows)
    grad_slots = links.send_slots(grads_sent)
    held = slot_rows.shape
    expert_rows = slot_rows.reshape(-1, WIDTH)
    hidden, slope = expert_up(expert_rows, expert_in)
    hidden, expert_out = finish_out(hidden)
    result, grad_slots = together(expert_down(hidden, expert_out), grad_slots)
    flat_result = links.return_slots(result.reshape(held)).reshape(SLOTS, WIDTH)
    grad_result = grad_slots.reshape(-1, WIDTH)

    core = links.core()
    out_part = links.expert_cores(*out_grad(core, hidden, grad_result))
    grad_pre, grad_rows = expert_back(grad_result, slope, expert_out, expert_in)
    grad_rows, flat_result = together(grad_rows, flat_result)
    rows_back = links.return_slots(grad_rows.reshape(held)).reshape(SLOTS, WIDTH)
    out_mine, out_got = links.expert_far(out_part)
    in_part = links.expert_cores(*in_grad(core, expert_rows, grad_pre))
    in_mine, in_got = links.expert_far(in_part)

    output, grad_logits = combine_results(routes, targets, columns, mid, cotangent, flat_result)
    grad_mid, low, grad_attended, d_gain = middle_back(
        targets, grad_logits, mid, cotangent, rows_back, dense, table
    )
    grad_qkv = attention_backward(qkv, attended, logs, grad_attended)
    d_qkv = qkv_grads(act_one, grad_qkv)
    d_rest = proj_grads(attended, low, act_two, grad_logits, d_gain)
    grad_tokens = token_grads(grad_qkv, dense, tokens, grad_mid, table)
    d_out = links.expert_end(out_mine, out_got)
    d_in = links.expert_end(in_mine, in_got)
    d_rest = links.scatter_rows(d_rest)
    d_qkv = links.scatter_rows(d_qkv)
    d_gain_attn = jnp.sum(d_qkv * own_qkv.astype(F32), axis=1) / gain_attn.astype(F32)
    return (
        output,
        grad_tokens,
        d_gain_attn,
        by_part(d_qkv),
        d_rest[:, :WIDTH],
        d_rest[:, WIDTH + GAIN_TWO],
        d_rest[:, WIDTH : WIDTH + EXPERTS],
        d_in,
        d_out,
    )


def solution(mesh):
    pairwise = mesh.shape["dp"] == 2 and mesh.shape["fsdp"] == 16
    links = PairwiseLinks(mesh) if pairwise else AxisLinks(mesh)
    rows = P(links.data, None)
    flat = P(links.data)
    expert = P(links.dp, links.fsdp, None)
    return jax.shard_map(
        lambda *arrays: per_device(links, *arrays),
        mesh=links.mesh,
        in_specs=(rows, flat, rows, rows, flat, rows, expert, expert, rows, rows, rows),
        out_specs=(rows, rows, flat, rows, rows, flat, rows, expert, expert),
        check_vma=False,
    )
```

time: 765 us -> 482 us (0.63); the launches traced: 752 us -> 480 us
  matrix products: 251 us -> 0 us
  Pallas kernels: 0 us -> 170 us
  waiting for transfers between devices: 301 us -> 154 us
  local copies, waits for them, and re-layouts: 60.1 us -> 13.2 us
  other arithmetic: 64.3 us -> 35.1 us
  blocking collectives: 22.6 us -> 49.7 us
    dot_general x104 -> x0, matrix products: 251 us -> none  [the longest x12 23.2 us: head_forward(): jnp.einsum('ist,itd->isd', attn_probs, values_head, preferred_element_typ...]
    pallas_call x0 -> x18, Pallas kernels: none -> 170 us  [the longest x3 18.3 us: place(): call('place', lambda *refs: place_kernel(count, *refs), (2,) * count, [wh...]
    ppermute x14 -> x23, waiting for transfers between devices: 216 us -> 125 us  [swap(): return lax.ppermute(value, axis, [(0, 1), (1, 0)])]
    all_to_all x9 -> x10, waiting for transfers between devices: 85.6 us -> 28.5 us  [trade(): return lax.all_to_all(value, axes, 0, 0, tiled=True)]
    all_to_all x1 -> x2, blocking collectives: 22.6 us -> 49.7 us  [trade(): return lax.all_to_all(value, axes, 0, 0, tiled=True)]
    another operation x18 -> x2, other arithmetic: 22.6 us -> 1.22 us  [place_of(): return jnp.stack([lax.axis_index(axis) for axis in axes]).astype(jnp.int32)]
    squeeze x8 -> x0, local copies, waits for them, and re-layouts: 13.3 us -> none  [the longest x7 9.84 us: add_halves(): theirs = lax.dynamic_index_in_dim(value, 1 - me, at, keepdims=False)]
    select_n x1 -> x9, other arithmetic: 0.01 us -> 8.67 us  [the longest x8 7.92 us: half(): return jnp.where(first, low, high)]
  transfers between devices with their start and end apart: 23 -> 33, of which waited for: 14 -> 13; matrix products, arithmetic and copies ran while one was open for 39% -> 8% of each run, Pallas kernels for 0% -> 35%
where the time goes in v2:
time: 482 us; the launch traced here: 480 us
  Pallas kernels  170 us (35%)
  waiting for transfers between devices  154 us (32%)
  starting transfers between devices  57.6 us (12%)
  blocking collectives  49.7 us (10%)
  other arithmetic  35.1 us (7%)
  local copies, waits for them, and re-layouts  13.2 us (3%)
    ppermute x23, waiting for transfers between devices, swap(): return lax.ppermute(value, axis, [(0, 1), (1, 0)])  125 us
    all_to_all x2, blocking collectives, trade(): return lax.all_to_all(value, axes, 0, 0, tiled=True)  49.7 us
    all_to_all x10, starting transfers between devices, trade(): return lax.all_to_all(value, axes, 0, 0, tiled=True)  39.1 us
    all_to_all x10, waiting for transfers between devices, trade(): return lax.all_to_all(value, axes, 0, 0, tiled=True)  28.5 us
    ppermute x23, starting transfers between devices, swap(): return lax.ppermute(value, axis, [(0, 1), (1, 0)])  18.5 us
    pallas_call x3, Pallas kernels, place(): call('place', lambda *refs: place_kernel(count, *refs), (2,) * count, [wh...  18.3 us
    pallas_call x1, Pallas kernels, expert_back(): call('expert_back', expert_back_kernel, (count // ROW_BLOCK,), [narrow, w...  18.2 us
    convert_element_type x10, other arithmetic, add(): return (mine.astype(F32) + got.astype(F32)).astype(BF16)  17.6 us
  transfers between devices with their start and end apart: 33, of which 13 were waited for; matrix products, arithmetic and copies ran while one was open for 8% of the time, Pallas kernels for 35%

profile of v2, /device:TPU:0, one launch (start us, length us, event | category | flops | bytes accessed | tf_op | source)
XLA Modules:
  0.0 480.1 jit_solution(17056541775178143025)
XLA Ops:
  5.0 22.6 %all_to_all.60.refs_1_ = bf16[4,24,3200]{2,1,0:T(8,128)(2,1)S(1)} all-to-all(bf16[4,24,3200]{2,1,0:T(8,128)(2,1)S(1)} %broadcast_in_dim.19), channel_id=1, replica_groups=mesh['x'=2,'zh'=2,'zl'=2,'y'=2,'c'=2] {'zh','zl'}, dimensions={0} | all-to-all | bytes 1228800 | tf_op jit(solution)/shard_map/all_to_all | solution.py:619
  33.1 13.2 %all-to-all-done.2.refs_1_ = bf16[4,48,3072]{2,1,0:T(8,128)(2,1)S(1)} async-done(((bf16[4,48,3072]{2,1,0:T(8,128)(2,1)}), bf16[4,48,3072]{2,1,0:T(8,128)(2,1)S(1)}, u32[]{:S(2)}, u32[]{:S(2)}) %all-to-all-start.2) | async-done | bytes 1179680 | tf_op jit(solution)/shard_map/all_to_all | solution.py:619
  51.4 14.5 %collective-permute-done.1.refs_3_ = bf16[4,24,3200]{2,1,0:T(8,128)(2,1)} collective-permute-done((bf16[4,24,3200]{2,1,0:T(8,128)(2,1)S(1)}, bf16[4,24,3200]{2,1,0:T(8,128)(2,1)}, u32[]{:S(2)}, u32[]{:S(2)}) %collective-permute-start.1) | collective-permute-done | bytes 614432 | tf_op jit(solution)/shard_map/ppermute | solution.py:616
  69.0 11.1 %collective-permute-done.5.refs_7_ = bf16[4,24,3200]{2,1,0:T(8,128)(2,1)} collective-permute-done((bf16[4,24,3200]{2,1,0:T(8,128)(2,1)}, bf16[4,24,3200]{2,1,0:T(8,128)(2,1)}, u32[]{:S(2)}, u32[]{:S(2)}) %collective-permute-start.5) | collective-permute-done | bytes 614432 | tf_op jit(solution)/shard_map/ppermute | solution.py:616
  82.5 6.9 %place.3 = bf16[2,4,2,2,24,3200]{5,4,3,2,1,0:T(8,128)(2,1)} custom-call(s32[3]{0:T(128)} %pad_add_fusion.refs_0_, bf16[4,24,3200]{2,1,0:T(8,128)(2,1)} %copy-done.10, bf16[4,24,3200]{2,1,0:T(8,128)(2,1)} %collective-permute-done.refs_2_, bf16[4,24,3200]{2,1,0:T(8,128)(2,1)} %collective-permute-done.1.refs_3_, ...), custom_call_target="tpu_custom_call" | custom-call | flops 1 | bytes 1 | tf_op jit(solution)/shard_map/place/pallas_call | solution.py:589
  89.4 8.0 %project.1 = (bf16[576,2304]{1,0:T(8,128)(2,1)}, bf16[576,768]{1,0:T(8,128)(2,1)}, bf16[128,768]{1,0:T(8,128)(2,1)}) custom-call(bf16[576,768]{1,0:T(8,128)(2,1)} %tokens_ref.5, bf16[768,3200]{1,0:T(8,128)(2,1)} %bitcast.86, bf16[768,3200]{1,0:T(8,128)(2,1)} %bitcast.87), custom_call_target="tpu_custom_call" | custom-call | flops 1 | bytes 1 | tf_op jit(solution)/shard_map/project/pallas_call | solution.py:176
  97.4 10.4 %attention_forward.1 = (bf16[576,768]{1,0:T(8,128)(2,1)}, f32[1,6,2,576]{3,2,1,0:T(2,128)}) custom-call(bf16[576,2304]{1,0:T(8,128)(2,1)} %get-tuple-element.43.qkv_ref), custom_call_target="tpu_custom_call" | custom-call | flops 1 | bytes 1 | tf_op jit(solution)/shard_map/attention_forward/pallas_call | solution.py:135
  107.8 9.3 %middle.1 = (f32[576,768]{1,0:T(8,128)}, bf16[576,768]{1,0:T(8,128)(2,1)}, f32[576,128]{1,0:T(8,128)}, f32[8,576]{1,0:T(8,128)}, bf16[8,152,768]{2,1,0:T(8,128)(2,1)}) custom-call(s32[2,576]{1,0:T(2,128)} %bitcast.106, s32[2,576]{1,0:T(2,128)} %bitcast.108, bf16[576,768]{1,0:T(8,128)(2,1)} %tokens_ref.5, ...), custom_call_target="tpu_custom_call" | custom-call | flops 1 | bytes 1 | tf_op jit(solution)/shard_map/middle/pallas_call | solution.py:243
  119.6 27.1 %all_to_all.61 = bf16[8,152,768]{2,1,0:T(8,128)(2,1)} all-to-all(bf16[8,152,768]{2,1,0:T(8,128)(2,1)} %get-tuple-element.50), channel_id=1, replica_groups=mesh['x'=2,'zh'=2,'zl'=2,'y'=2,'c'=2] {'x','zl','y'}, dimensions={0} | all-to-all | bytes 3735552 | tf_op jit(solution)/shard_map/all_to_all | solution.py:619
  150.3 5.9 %slot_grads.1 = bf16[8,152,768]{2,1,0:T(8,128)(2,1)} custom-call(s32[2,576]{1,0:T(2,128)} %bitcast.107, s32[2,576]{1,0:T(2,128)} %bitcast.109, f32[8,576]{1,0:T(8,128)} %get-tuple-element.48.gates_ref, bf16[576,768]{1,0:T(8,128)(2,1)} %grad_ref.5), custom_call_target="tpu_custom_call" | custom-call | flops 1 | bytes 1 | tf_op jit(solution)/shard_map/slot_grads/pallas_call | solution.py:280
  156.2 6.9 %all-to-all-done.3.refs_3_ = bf16[4,48,3072]{2,1,0:T(8,128)(2,1)S(1)} async-done(((bf16[4,48,3072]{2,1,0:T(8,128)(2,1)}), bf16[4,48,3072]{2,1,0:T(8,128)(2,1)S(1)}, u32[]{:S(2)}, u32[]{:S(2)}) %all-to-all-start.3) | async-done | bytes 1179680 | tf_op jit(solution)/shard_map/all_to_all | solution.py:619
  178.4 16.3 %expert_up.1 = (bf16[1216,3072]{1,0:T(8,128)(2,1)}, bf16[1216,3072]{1,0:T(8,128)(2,1)}) custom-call(bf16[1216,768]{1,0:T(8,128)(2,1)} %bitcast.99, bf16[768,3072]{1,0:T(8,128)(2,1)} %bitcast.91), custom_call_target="tpu_custom_call" | custom-call | flops 1 | bytes 1 | tf_op jit(solution)/shard_map/expert_up/pallas_call | solution.py:304
  194.7 28.1 %collective-permute-done.10.refs_3_ = bf16[4,192,768]{2,1,0:T(8,128)(2,1)} collective-permute-done((bf16[4,192,768]{2,1,0:T(8,128)(2,1)S(1)}, bf16[4,192,768]{2,1,0:T(8,128)(2,1)}, u32[]{:S(2)}, u32[]{:S(2)}) %collective-permute-start.10) | collective-permute-done | bytes 1179680 | tf_op jit(solution)/shard_map/ppermute | solution.py:616
  231.8 10.3 %expert_down.1 = bf16[1216,768]{1,0:T(8,128)(2,1)} custom-call(bf16[1216,3072]{1,0:T(8,128)(2,1)} %get-tuple-element.54.hidden_ref, bf16[3072,768]{1,0:T(8,128)(2,1)} %bitcast.93), custom_call_target="tpu_custom_call" | custom-call | flops 1 | bytes 1 | tf_op jit(solution)/shard_map/expert_down/pallas_call | solution.py:320
  247.8 12.1 %out_grad.1 = (bf16[2,4,192,768]{3,2,1,0:T(8,128)(2,1)}, bf16[2,4,192,768]{3,2,1,0:T(8,128)(2,1)}) custom-call(s32[1]{0:T(128)} %bitcast.4.me_ref, bf16[1216,3072]{1,0:T(8,128)(2,1)} %get-tuple-element.54.hidden_ref, bf16[1216,768]{1,0:T(8,128)(2,1)} %bitcast.97), custom_call_target="tpu_custom_call" | custom-call | flops 1 | bytes 1 | tf_op jit(solution)/shard_map/out_grad/pallas_call | solution.py:363
  260.0 18.2 %expert_back.1 = (bf16[1216,3072]{1,0:T(8,128)(2,1)}, bf16[1216,768]{1,0:T(8,128)(2,1)}) custom-call(bf16[1216,768]{1,0:T(8,128)(2,1)} %bitcast.98, bf16[1216,3072]{1,0:T(8,128)(2,1)} %get-tuple-element.58.slope_ref, bf16[3072,768]{1,0:T(8,128)(2,1)} %bitcast.94, bf16[768,3072]{1,0:T(8,128)(2,1)} %bitcast.92), custom_call_target="tpu_custom_call" | custom-call | flops 1 | bytes 1 | tf_op jit(solution)/shard_map/expert_back/pallas_call | solution.py:341
  282.9 11.6 %in_grad.1 = (bf16[2,4,48,3072]{3,2,1,0:T(8,128)(2,1)}, bf16[2,4,48,3072]{3,2,1,0:T(8,128)(2,1)}) custom-call(s32[1]{0:T(128)} %bitcast.4.me_ref, bf16[1216,768]{1,0:T(8,128)(2,1)} %bitcast.100, bf16[1216,3072]{1,0:T(8,128)(2,1)} %get-tuple-element.72.grad_ref), custom_call_target="tpu_custom_call" | custom-call | flops 1 | bytes 1 | tf_op jit(solution)/shard_map/in_grad/pallas_call | solution.py:391
  307.1 7.1 %combine.1 = (bf16[576,768]{1,0:T(8,128)(2,1)}, bf16[576,128]{1,0:T(8,128)(2,1)}) custom-call(s32[576,2]{1,0:T(8,128)} %copy.115.routes_ref, s32[576,2]{1,0:T(8,128)} %add_select_fusion.targets_ref, f32[576,128]{1,0:T(8,128)} %get-tuple-element.46.columns_ref, f32[576,768]{1,0:T(8,128)} %get-tuple-element.47.mid_ref, bf16[576,768]{1,0:T(8,128)(2,1)} %grad_ref.5, ...), custom_call_target="tpu_custom_call" | custom-call | flops 1 | bytes 1 | tf_op jit(solution)/shard_map/combine/pallas_call | solution.py:432
  317.1 7.5 %middle_back.1 = (f32[576,768]{1,0:T(8,128)}, bf16[576,768]{1,0:T(8,128)(2,1)}, bf16[576,768]{1,0:T(8,128)(2,1)}, f32[8,768]{1,0:T(8,128)}) custom-call(s32[576,2]{1,0:T(8,128)} %add_select_fusion.targets_ref, bf16[576,128]{1,0:T(8,128)(2,1)} %get-tuple-element.64.logits_ref, f32[576,768]{1,0:T(8,128)} %get-tuple-element.47.mid_ref, ...), custom_call_target="tpu_custom_call" | custom-call | flops 1 | bytes 1 | tf_op jit(solution)/shard_map/middle_back/pallas_call | solution.py:474
  324.6 14.3 %attention_backward.1.grad_ref = bf16[576,2304]{1,0:T(8,128)(2,1)} custom-call(bf16[576,2304]{1,0:T(8,128)(2,1)} %get-tuple-element.43.qkv_ref, bf16[576,768]{1,0:T(8,128)(2,1)} %get-tuple-element.44.attended_ref.out_ref, f32[1,6,2,576]{3,2,1,0:T(2,128)} %get-tuple-element.63.log_ref, bf16[576,768]{1,0:T(8,128)(2,1)} %get-tuple-element.66.grad_ref), custom_call_target="tpu_custom_call" | custom-call | flops 1 | bytes 1 | tf_op jit(solution)/shard_map/attention_backward/pallas_call | solution.py:147
  338.9 7.9 %qkv_grads.1 = bf16[768,2304]{1,0:T(8,128)(2,1)} custom-call(bf16[576,768]{1,0:T(8,128)(2,1)} %get-tuple-element.68.act_ref, bf16[576,2304]{1,0:T(8,128)(2,1)} %attention_backward.1.grad_ref), custom_call_target="tpu_custom_call" | custom-call | flops 1 | bytes 1 | tf_op jit(solution)/shard_map/qkv_grads/pallas_call | solution.py:527
  374.0 38.3 %collective-permute-done.20 = bf16[4,48,3072]{2,1,0:T(8,128)(2,1)} collective-permute-done((bf16[4,48,3072]{2,1,0:T(8,128)(2,1)}, bf16[4,48,3072]{2,1,0:T(8,128)(2,1)}, u32[]{:S(2)}, u32[]{:S(2)}) %collective-permute-start.20) | collective-permute-done | bytes 1179680 | tf_op jit(solution)/shard_map/ppermute | solution.py:616
  423.5 24.8 %collective-permute-done.18 = bf16[4,24,896]{2,1,0:T(8,128)(2,1)S(1)} collective-permute-done((bf16[4,24,896]{2,1,0:T(8,128)(2,1)S(1)}, bf16[4,24,896]{2,1,0:T(8,128)(2,1)S(1)}, u32[]{:S(2)}, u32[]{:S(2)}) %collective-permute-start.18) | collective-permute-done | bytes 172064 | tf_op jit(solution)/shard_map/ppermute | solution.py:616
  468.2 8.1 %token_grads.1 = f32[576,768]{1,0:T(8,128)} custom-call(bf16[576,2304]{1,0:T(8,128)(2,1)} %attention_backward.1.grad_ref, bf16[768,3200]{1,0:T(8,128)(2,1)} %bitcast.90, bf16[576,768]{1,0:T(8,128)(2,1)} %tokens_ref.5, f32[576,768]{1,0:T(8,128)} %get-tuple-element.67.grad_mid_ref, bf16[128,768]{1,0:T(8,128)(2,1)} %get-tuple-element.45.table_ref), custom_call_target="tpu_custom_call" | custom-call | flops 1 | bytes 1 | tf_op jit(solution)/shard_map/token_grads/pallas_call | solution.py:547
  (144 shorter events, 138.5 us)
Async XLA Ops:
  27.6 18.7 %all-to-all-start.2 = ((bf16[4,48,3072]{2,1,0:T(8,128)(2,1)}), bf16[4,48,3072]{2,1,0:T(8,128)(2,1)S(1)}, u32[]{:S(2)}, u32[]{:S(2)}) async-start(bf16[4,48,3072]{2,1,0:T(8,128)(2,1)} %param.17), calls=%async_computation.2 | async-start | bytes 2359296 | tf_op jit(solution)/shard_map/all_to_all | solution.py:619
  31.1 34.8 %collective-permute-start.1 = (bf16[4,24,3200]{2,1,0:T(8,128)(2,1)S(1)}, bf16[4,24,3200]{2,1,0:T(8,128)(2,1)}, u32[]{:S(2)}, u32[]{:S(2)}) collective-permute-start(bf16[4,24,3200]{2,1,0:T(8,128)(2,1)S(1)} %all_to_all.60.refs_1_), channel_id=1, source_target_pairs={{0,2},{2,0},{1,3},{3,1},{4,6},{6,4},{5,7},{7,5},{8,10},{10,8},{9,1... | collective-permute-start | bytes 1843208 | tf_op jit(solution)/shard_map/ppermute | solution.py:616
  46.3 73.3 %all-to-all-start.4 = ((bf16[4,192,768]{2,1,0:T(8,128)(2,1)}), bf16[4,192,768]{2,1,0:T(8,128)(2,1)S(1)}, u32[]{:S(2)}, u32[]{:S(2)}) async-start(bf16[4,192,768]{2,1,0:T(8,128)(2,1)} %param.18), calls=%async_computation.4 | async-start | bytes 2359296 | tf_op jit(solution)/shard_map/all_to_all | solution.py:619
  49.9 19.1 %collective-permute-start.3 = (bf16[4,24,3200]{2,1,0:T(8,128)(2,1)S(1)}, bf16[4,24,3200]{2,1,0:T(8,128)(2,1)}, u32[]{:S(2)}, u32[]{:S(2)}) collective-permute-start(bf16[4,24,3200]{2,1,0:T(8,128)(2,1)S(1)} %all_to_all.60.refs_1_), channel_id=1, source_target_pairs={{0,16},{16,0},{1,17},{17,1},{2,18},{18,2},{3,19},{19,3},{4,20},{20... | collective-permute-start | bytes 1843208 | tf_op jit(solution)/shard_map/ppermute | solution.py:616
  65.9 14.2 %collective-permute-start.5 = (bf16[4,24,3200]{2,1,0:T(8,128)(2,1)}, bf16[4,24,3200]{2,1,0:T(8,128)(2,1)}, u32[]{:S(2)}, u32[]{:S(2)}) collective-permute-start(bf16[4,24,3200]{2,1,0:T(8,128)(2,1)} %collective-permute-done.1.refs_3_), channel_id=1, source_target_pairs={{0,16},{16,0},{1,17},{17,1},{2,18},{18,2},{3,19},{19,3},{4,20},{20... | collective-permute-start | bytes 1843208 | tf_op jit(solution)/shard_map/ppermute | solution.py:616
  67.4 52.2 %collective-permute-start.7 = (bf16[4,48,3072]{2,1,0:T(8,128)(2,1)}, bf16[4,48,3072]{2,1,0:T(8,128)(2,1)}, u32[]{:S(2)}, u32[]{:S(2)}) collective-permute-start(bf16[4,48,3072]{2,1,0:T(8,128)(2,1)} %param.17), channel_id=1, source_target_pairs={{0,8},{8,0},{1,9},{9,1},{2,10},{10,2},{3,11},{11,3},{4,12},{12,4},... | collective-permute-start | bytes 3538952 | tf_op jit(solution)/shard_map/ppermute | solution.py:616
  68.5 12.2 %collective-permute-start = (bf16[4,24,3200]{2,1,0:T(8,128)(2,1)S(1)}, bf16[4,24,3200]{2,1,0:T(8,128)(2,1)}, u32[]{:S(2)}, u32[]{:S(2)}) collective-permute-start(bf16[4,24,3200]{2,1,0:T(8,128)(2,1)S(1)} %all_to_all.60.refs_1_), channel_id=1, source_target_pairs={{0,1},{1,0},{2,3},{3,2},{4,5},{5,4},{6,7},{7,6},{8,9},{9,8},{10,11... | collective-permute-start | bytes 1843208 | tf_op jit(solution)/shard_map/ppermute | solution.py:616
  146.8 16.4 %all-to-all-start.3 = ((bf16[4,48,3072]{2,1,0:T(8,128)(2,1)}), bf16[4,48,3072]{2,1,0:T(8,128)(2,1)S(1)}, u32[]{:S(2)}, u32[]{:S(2)}) async-start(bf16[4,48,3072]{2,1,0:T(8,128)(2,1)} %collective-permute-done.7), calls=%async_computation.3 | async-start | bytes 2359296 | tf_op jit(solution)/shard_map/all_to_all | solution.py:619
  164.2 77.9 %all-to-all-start.5 = ((bf16[8,152,768]{2,1,0:T(8,128)(2,1)}), bf16[8,152,768]{2,1,0:T(8,128)(2,1)S(1)}, u32[]{:S(2)}, u32[]{:S(2)}) async-start(bf16[8,152,768]{2,1,0:T(8,128)(2,1)} %slot_grads.1), calls=%async_computation.5 | async-start | bytes 3735552 | tf_op jit(solution)/shard_map/all_to_all | solution.py:619
  168.4 54.4 %collective-permute-start.10 = (bf16[4,192,768]{2,1,0:T(8,128)(2,1)S(1)}, bf16[4,192,768]{2,1,0:T(8,128)(2,1)}, u32[]{:S(2)}, u32[]{:S(2)}) collective-permute-start(bf16[4,192,768]{2,1,0:T(8,128)(2,1)S(1)} %all-to-all-done.4.refs_1_), channel_id=1, source_target_pairs={{0,8},{8,0},{1,9},{9,1},{2,10},{10,2},{3,11},{11,3},{4,12},{12,4},... | collective-permute-start | bytes 3538952 | tf_op jit(solution)/shard_map/ppermute | solution.py:616
  171.8 51.0 %collective-permute-start.11 = (bf16[4,192,768]{2,1,0:T(8,128)(2,1)S(1)}, bf16[4,192,768]{2,1,0:T(8,128)(2,1)}, u32[]{:S(2)}, u32[]{:S(2)}) collective-permute-start(bf16[4,192,768]{2,1,0:T(8,128)(2,1)S(1)} %all-to-all-done.4.refs_1_), channel_id=1, source_target_pairs={{0,1},{1,0},{2,3},{3,2},{4,5},{5,4},{6,7},{7,6},{8,9},{9,8},{10,11... | collective-permute-start | bytes 3538952 | tf_op jit(solution)/shard_map/ppermute | solution.py:616
  243.3 34.9 %all-to-all-start.6 = ((bf16[8,152,768]{2,1,0:T(8,128)(2,1)}), bf16[8,152,768]{2,1,0:T(8,128)(2,1)}, u32[]{:S(2)}, u32[]{:S(2)}) async-start(bf16[8,152,768]{2,1,0:T(8,128)(2,1)} %bitcast.101), calls=%async_computation.6 | async-start | bytes 3735552 | tf_op jit(solution)/shard_map/all_to_all | solution.py:619
  259.9 37.0 %collective-permute-start.21 = (bf16[2,4,192,768]{3,2,1,0:T(8,128)(2,1)}, bf16[2,4,192,768]{3,2,1,0:T(8,128)(2,1)}, u32[]{:S(2)}, u32[]{:S(2)}) collective-permute-start(bf16[2,4,192,768]{3,2,1,0:T(8,128)(2,1)} %get-tuple-element.76), channel_id=1, source_target_pairs={{0,1},{1,0},{2,3},{3,2},{4,5},{5,4},{6,7},{7,6},{8,9},{9,8},{10,11... | collective-permute-start | bytes 7077896 | tf_op jit(solution)/shard_map/ppermute | solution.py:616
  278.2 38.9 %all-to-all-start.7 = ((bf16[8,152,768]{2,1,0:T(8,128)(2,1)}), bf16[8,152,768]{2,1,0:T(8,128)(2,1)}, u32[]{:S(2)}, u32[]{:S(2)}) async-start(bf16[8,152,768]{2,1,0:T(8,128)(2,1)} %bitcast.104), calls=%async_computation.7 | async-start | bytes 3735552 | tf_op jit(solution)/shard_map/all_to_all | solution.py:619
  301.0 58.3 %collective-permute-start.22 = (bf16[4,192,768]{2,1,0:T(8,128)(2,1)}, bf16[4,192,768]{2,1,0:T(8,128)(2,1)}, u32[]{:S(2)}, u32[]{:S(2)}) collective-permute-start(bf16[4,192,768]{2,1,0:T(8,128)(2,1)} %select_bitcast_fusion.1), channel_id=1, source_target_pairs={{0,8},{8,0},{1,9},{9,1},{2,10},{10,2},{3,11},{11,3},{4,12},{12,4},... | collective-permute-start | bytes 3538952 | tf_op jit(solution)/shard_map/ppermute | solution.py:616
  350.2 19.5 %collective-permute-start.13 = (bf16[2,4,2,24,2304]{4,3,2,1,0:T(8,128)(2,1)}, bf16[2,4,2,24,2304]{4,3,2,1,0:T(8,128)(2,1)}, u32[]{:S(2)}, u32[]{:S(2)}) collective-permute-start(bf16[2,4,2,24,2304]{4,3,2,1,0:T(8,128)(2,1)} %select_bitcast_fusion), channel_id=1, source_target_pairs={{0,1},{1,0},{2,3},{3,2},{4,5},{5,4},{6,7},{7,6},{8,9},{9,8},{10,11... | collective-permute-start | bytes 5308424 | tf_op jit(solution)/shard_map/ppermute | solution.py:616
  359.3 53.0 %collective-permute-start.20 = (bf16[4,48,3072]{2,1,0:T(8,128)(2,1)}, bf16[4,48,3072]{2,1,0:T(8,128)(2,1)}, u32[]{:S(2)}, u32[]{:S(2)}) collective-permute-start(bf16[4,48,3072]{2,1,0:T(8,128)(2,1)} %select_bitcast_fusion.2), channel_id=1, source_target_pairs={{0,8},{8,0},{1,9},{9,1},{2,10},{10,2},{3,11},{11,3},{4,12},{12,4},... | collective-permute-start | bytes 3538952 | tf_op jit(solution)/shard_map/ppermute | solution.py:616
  362.3 53.0 %all-to-all-start.11 = ((bf16[4,192,768]{2,1,0:T(8,128)(2,1)}), bf16[4,192,768]{2,1,0:T(8,128)(2,1)}, u32[]{:S(2)}, u32[]{:S(2)}) async-start(bf16[4,192,768]{2,1,0:T(8,128)(2,1)} %fusion.1), calls=%async_computation.11 | async-start | bytes 2359296 | tf_op jit(solution)/shard_map/all_to_all | solution.py:619
  368.6 46.6 %collective-permute-start.17 = (bf16[4,2,24,896]{3,2,0,1:T(8,128)(2,1)S(1)}, bf16[4,2,24,896]{3,2,0,1:T(8,128)(2,1)S(1)}, u32[]{:S(2)}, u32[]{:S(2)}) collective-permute-start(bf16[4,2,24,896]{3,2,0,1:T(8,128)(2,1)S(1)} %select_bitcast_fusion.6), channel_id=1, source_target_pairs={{0,16},{16,0},{1,17},{17,1},{2,18},{18,2},{3,19},{19,3},{4,20},{20... | collective-permute-start | bytes 1032200 | tf_op jit(solution)/shard_map/ppermute | solution.py:616
  373.0 46.7 %collective-permute-start.14 = (bf16[4,2,24,2304]{3,2,1,0:T(8,128)(2,1)}, bf16[4,2,24,2304]{3,2,1,0:T(8,128)(2,1)}, u32[]{:S(2)}, u32[]{:S(2)}) collective-permute-start(bf16[4,2,24,2304]{3,2,1,0:T(8,128)(2,1)} %select_bitcast_fusion.3), channel_id=1, source_target_pairs={{0,16},{16,0},{1,17},{17,1},{2,18},{18,2},{3,19},{19,3},{4,20},{20... | collective-permute-start | bytes 2654216 | tf_op jit(solution)/shard_map/ppermute | solution.py:616
  415.3 33.8 %all-to-all-start.10 = ((bf16[4,48,3072]{2,1,0:T(8,128)(2,1)}), bf16[4,48,3072]{2,1,0:T(8,128)(2,1)}, u32[]{:S(2)}, u32[]{:S(2)}) async-start(bf16[4,48,3072]{2,1,0:T(8,128)(2,1)} %fusion.2), calls=%async_computation.10 | async-start | bytes 2359296 | tf_op jit(solution)/shard_map/all_to_all | solution.py:619
  421.3 31.1 %collective-permute-start.15 = (bf16[4,24,2304]{2,1,0:T(8,128)(2,1)S(1)}, bf16[4,24,2304]{2,1,0:T(8,128)(2,1)S(1)}, u32[]{:S(2)}, u32[]{:S(2)}) collective-permute-start(bf16[4,24,2304]{2,1,0:T(8,128)(2,1)S(1)} %select_bitcast_fusion.5), channel_id=1, source_target_pairs={{0,2},{2,0},{1,3},{3,1},{4,6},{6,4},{5,7},{7,5},{8,10},{10,8},{9,1... | collective-permute-start | bytes 1327112 | tf_op jit(solution)/shard_map/ppermute | solution.py:616
  423.4 25.0 %collective-permute-start.18 = (bf16[4,24,896]{2,1,0:T(8,128)(2,1)S(1)}, bf16[4,24,896]{2,1,0:T(8,128)(2,1)S(1)}, u32[]{:S(2)}, u32[]{:S(2)}) collective-permute-start(bf16[4,24,896]{2,1,0:T(8,128)(2,1)S(1)} %select_bitcast_fusion.7), channel_id=1, source_target_pairs={{0,2},{2,0},{1,3},{3,1},{4,6},{6,4},{5,7},{7,5},{8,10},{10,8},{9,1... | collective-permute-start | bytes 516104 | tf_op jit(solution)/shard_map/ppermute | solution.py:616
  458.9 19.4 %all-to-all-start.8 = ((bf16[4,24,2304]{2,1,0:T(8,128)(2,1)}), bf16[4,24,2304]{2,1,0:T(8,128)(2,1)S(1)}, u32[]{:S(2)}, u32[]{:S(2)}) async-start(bf16[4,24,2304]{2,1,0:T(8,128)(2,1)} %fusion.6), calls=%async_computation.8 | async-start | bytes 884736 | tf_op jit(solution)/shard_map/all_to_all | solution.py:619
  (25 other events, 307.5 us)

commit v3 on v2

--- a/solution.py
+++ b/solution.py
@@ -494,45 +494,62 @@
     )(targets, logits, mid, cotangent, grad_rows, dense, table)
 
 
-def proj_grads_kernel(attended_ref, low_ref, act_ref, logits_ref, gain_ref, result_ref):
-    result_ref[:, :WIDTH] = dot_tn(attended_ref[...], low_ref[...]).astype(BF16)
+def write_halves(value, first, mine_ref, theirs_ref):
+    value = value.reshape(2, 4, 2, 2, value.shape[0] // 32, value.shape[1])
+    for x, y, z in ((x, y, z) for x in range(2) for y in range(2) for z in range(4)):
+        low, high = value[x, z, y, 0], value[x, z, y, 1]
+        mine_ref[x, y, z] = jnp.where(first, low, high).astype(BF16)
+        theirs_ref[x, y, z] = jnp.where(first, high, low).astype(BF16)
+
+
+def proj_grads_kernel(
+    me_ref, attended_ref, low_ref, act_ref, logits_ref, gain_ref, mine_ref, theirs_ref
+):
+    wide = dot_tn(attended_ref[...], low_ref[...])
     small = dot_tn(act_ref[...], logits_ref[...])
     lanes = lax.broadcasted_iota(jnp.int32, small.shape, 1)
     gain = gain_ref[...].T[:, 0:1]
-    result_ref[:, WIDTH:] = jnp.where(lanes == GAIN_TWO, gain, small).astype(BF16)
-
-
-def proj_grads(attended, low, act_two, logits, gain):
+    value = jnp.concatenate([wide, jnp.where(lanes == GAIN_TWO, gain, small)], axis=1)
+    write_halves(value, me_ref[0] == 0, mine_ref, theirs_ref)
+
+
+def proj_grads(me, attended, low, act_two, logits, gain):
     rows = low.shape[0]
+    half = (2, 2, 4, WIDTH // 32, WIDTH + LANES)
     return call(
         "proj_grads",
         proj_grads_kernel,
         (1,),
         [whole(rows, WIDTH)] * 3 + [whole(rows, LANES), whole(8, WIDTH)],
-        whole(WIDTH, WIDTH + LANES),
-        struct((WIDTH, WIDTH + LANES), BF16),
-    )(attended, low, act_two, logits, gain)
-
-
-def qkv_grads_kernel(act_ref, grad_ref, result_ref, turned_ref):
+        [whole(*half)] * 2,
+        [struct(half, BF16)] * 2,
+        scalars=1,
+    )(me, attended, low, act_two, logits, gain)
+
+
+def qkv_grads_kernel(me_ref, act_ref, grad_ref, mine_ref, theirs_ref, turned_ref):
     @pl.when(pl.program_id(0) == 0)
     def _():
         turned_ref[...] = act_ref[...].T
 
-    result_ref[...] = dot_nn(turned_ref[...], grad_ref[...]).astype(BF16)
-
-
-def qkv_grads(act_one, grad_qkv):
+    value = dot_nn(turned_ref[...], grad_ref[...])
+    write_halves(value, me_ref[0] == 0, mine_ref, theirs_ref)
+
+
+def qkv_grads(me, act_one, grad_qkv):
     rows = act_one.shape[0]
+    half = (2, 2, 4, WIDTH // 32)
+    spec = pl.BlockSpec(half + (3 * PAIR,), lambda pair, me: (0, 0, 0, 0, pair))
     return call(
         "qkv_grads",
         qkv_grads_kernel,
         (PAIRS,),
-        [whole(rows, WIDTH), pl.BlockSpec((rows, 3 * PAIR), lambda pair: (0, pair))],
-        pl.BlockSpec((WIDTH, 3 * PAIR), lambda pair: (0, pair)),
-        struct((WIDTH, 3 * WIDTH), BF16),
+        [whole(rows, WIDTH), pl.BlockSpec((rows, 3 * PAIR), lambda pair, me: (0, pair))],
+        [spec, spec],
+        [struct(half + (3 * WIDTH,), BF16)] * 2,
         scratch=[pltpu.VMEM((WIDTH, rows), BF16)],
-    )(act_one, grad_qkv)
+        scalars=1,
+    )(me, act_one, grad_qkv)
 
 
 def token_grads_kernel(grad_ref, weight_ref, tokens_ref, grad_mid_ref, table_ref, result_ref):
@@ -597,6 +614,200 @@
     )(me, *pieces)
 
 
+def join_kernel(bounds, me_ref, near_ref, near_core_ref, *refs):
+    zh, core = me_ref[0], me_ref[1]
+    result_ref = refs[-1]
+    result_ref[zh, 0, core] = near_ref[0]
+    result_ref[zh, 0, 1 - core] = near_core_ref[0]
+    for part, (begin, end) in enumerate(bounds):
+
+        @pl.when((pl.program_id(0) >= begin) & (pl.program_id(0) < end))
+        def _():
+            result_ref[1 - zh, 0, core] = refs[part][0]
+            result_ref[1 - zh, 0, 1 - core] = refs[len(bounds) + part][0]
+
+
+def join(me, near, near_core, far, far_core):
+    blocks, rest, columns = near.shape
+    bounds, end = [], 0
+    for part in far:
+        bounds.append((end, end + part.shape[0]))
+        end += part.shape[0]
+
+    def piece(begin, end):
+        return pl.BlockSpec(
+            (1, rest, columns), lambda b, me: (jnp.clip(b - begin, 0, end - begin - 1), 0, 0)
+        )
+
+    return call(
+        "join",
+        lambda *refs: join_kernel(bounds, *refs),
+        (blocks,),
+        [piece(0, blocks)] * 2 + [piece(*at) for at in bounds] * 2,
+        pl.BlockSpec((2, 1, 2, rest, columns), lambda b, me: (0, b, 0, 0, 0)),
+        struct((2, blocks, 2, rest, columns), near.dtype),
+        scalars=1,
+    )(me, near, near_core, *far, *far_core).reshape(-1, columns)
+
+
+def parts_of(columns):
+    return 3 if columns % (3 * LANES) == 0 else 1
+
+
+def columns_of(shape):
+    block = tuple(shape[:-1]) + (shape[-1] // parts_of(shape[-1]),)
+    return pl.BlockSpec(block, lambda i, me: (0,) * (len(shape) - 1) + (i,))
+
+
+def pick_kernel(count, me_ref, *refs):
+    parts, outs = refs[:-count], refs[-count:]
+    places = [(ref, at) for ref in parts for at in range(ref.shape[0])]
+    for place_at, (part, at) in enumerate(places):
+        for k, ref in enumerate(outs):
+
+            @pl.when((me_ref[0] ^ k) == place_at)
+            def _():
+                ref[...] = part[at]
+
+
+def pick(me, *parts):
+    count, shape = sum(part.shape[0] for part in parts), parts[0].shape[1:]
+    return call(
+        "pick",
+        lambda *refs: pick_kernel(count, *refs),
+        (parts_of(shape[-1]),),
+        [columns_of(part.shape) for part in parts],
+        [columns_of(shape)] * count,
+        [struct(shape, BF16)] * count,
+        scalars=1,
+    )(me, *parts)
+
+
+def pack_kernel(me_ref, *refs):
+    for k, ref in enumerate(refs[:-1]):
+        refs[-1][me_ref[0] ^ k] = ref[...].astype(refs[-1].dtype)
+
+
+def pack(me, pieces, dtype=BF16):
+    shape = (len(pieces),) + pieces[0].shape
+    return call(
+        "pack",
+        pack_kernel,
+        (parts_of(shape[-1]),),
+        [columns_of(shape[1:])] * len(pieces),
+        columns_of(shape),
+        struct(shape, dtype),
+        scalars=1,
+    )(me, *pieces)
+
+
+def add_halves_kernel(me_ref, mine_ref, got_ref, keep_ref, *send_refs):
+    def total(at):
+        return (mine_ref[at].astype(F32) + got_ref[at].astype(F32)).astype(BF16)
+
+    keep_ref[...] = total(me_ref[0])
+    send = total(1 - me_ref[0])
+    begin = 0
+    for ref in send_refs:
+        ref[...] = send[begin : begin + ref.shape[0]]
+        begin += ref.shape[0]
+
+
+def add_halves(me, mine, got, counts):
+    shapes = [(count,) + mine.shape[2:] for count in (mine.shape[1],) + counts]
+    return call(
+        "add_halves",
+        add_halves_kernel,
+        (parts_of(mine.shape[-1]),),
+        [columns_of(mine.shape)] * 2,
+        [columns_of(shape) for shape in shapes],
+        [struct(shape, BF16) for shape in shapes],
+        scalars=1,
+    )(me, mine, got)
+
+
+def add_pick_kernel(me_ref, mine_ref, *refs):
+    gots, outs = refs[: -mine_ref.shape[0]], refs[-mine_ref.shape[0] :]
+    got = jnp.concatenate([ref[...] for ref in gots], axis=0).astype(F32)
+    for at in range(mine_ref.shape[0]):
+        value = (mine_ref[at].astype(F32) + got[at]).astype(BF16)
+        for k, ref in enumerate(outs):
+
+            @pl.when((me_ref[0] ^ k) == at)
+            def _():
+                ref[...] = value
+
+
+def add_pick(me, mine, gots):
+    count, shape = mine.shape[0], mine.shape[1:]
+    return call(
+        "add_pick",
+        add_pick_kernel,
+        (parts_of(shape[-1]),),
+        [columns_of(mine.shape)] + [columns_of(got.shape) for got in gots],
+        [columns_of(shape)] * count,
+        [struct(shape, BF16)] * count,
+        scalars=1,
+    )(me, mine, *gots)
+
+
+def dense_pick_kernel(me_ref, *refs):
+    outs = refs[-4:]
+    begin = 0
+    for mine_ref, got_ref in zip(refs[:-4:2], refs[1:-4:2]):
+        end = begin + mine_ref.shape[-1]
+        for at in range(4):
+            value = (mine_ref[at].astype(F32) + got_ref[at].astype(F32)).astype(BF16)
+            for k, ref in enumerate(outs):
+
+                @pl.when((me_ref[0] ^ k) == at)
+                def _():
+                    ref[:, begin:end] = value
+
+        begin = end
+
+
+def dense_pick(me, pairs):
+    arrays = [array.reshape(4, -1, array.shape[-1]) for pair in pairs for array in pair]
+    shape = (arrays[0].shape[1], sum(array.shape[-1] for array in arrays[::2]))
+    half = shape[0] // 2
+    return call(
+        "dense_pick",
+        dense_pick_kernel,
+        (2,),
+        [pl.BlockSpec((4, half, array.shape[-1]), lambda i, me: (0, i, 0)) for array in arrays],
+        [pl.BlockSpec((half, shape[1]), lambda i, me: (i, 0))] * 4,
+        [struct(shape, BF16)] * 4,
+        scalars=1,
+    )(me, *arrays)
+
+
+def turn_kernel(me_ref, *refs):
+    outs = refs[-4:]
+    total = sum(ref[...].astype(F32) for ref in refs[:-4])
+    total = total.reshape(4, total.shape[0] // 4, total.shape[1])
+    for at in range(4):
+        value = total[at].astype(BF16)
+        for k, ref in enumerate(outs):
+
+            @pl.when((me_ref[0] ^ k) == at)
+            def _():
+                ref[...] = value
+
+
+def turn(me, pieces):
+    shape = (pieces[0].shape[0] // 4, pieces[0].shape[1])
+    return call(
+        "turn",
+        turn_kernel,
+        (1,),
+        [whole(*piece.shape) for piece in pieces],
+        [whole(*shape)] * 4,
+        [struct(shape, BF16)] * 4,
+        scalars=1,
+    )(me, *pieces)
+
+
 def together(*values):
     return lax.optimization_barrier(values)
 
@@ -621,46 +832,79 @@
     def place_of(self, *axes):
         return jnp.stack([lax.axis_index(axis) for axis in axes]).astype(jnp.int32)
 
-    def half(self, value, axis, at, other):
-        first = lax.axis_index(axis) == (1 if other else 0)
-        low = lax.index_in_dim(value, 0, at, keepdims=False)
-        high = lax.index_in_dim(value, 1, at, keepdims=False)
-        return jnp.where(first, low, high)
-
-    def add_halves(self, value, axis, at):
-        got = self.swap(self.half(value, axis, at, True), axis)
-        return add(self.half(value, axis, at, False), got)
-
-    def gather_all(self, dense, w_in, w_out):
-        rows, columns = dense.shape
-        in_raw = self.swap(w_in, "zh")
-        copies = jnp.broadcast_to(dense[None], (4, rows, columns))
-        own = self.trade(copies, ("zh", "zl"))
-        in_near = self.trade(w_in, ("zl", "y"))
-        over_y = self.swap(own, "y")
-        over_x = self.swap(own, "x")
+    def core(self):
+        return self.place_of("c")
+
+    def number(self, *axes):
+        index = 0
+        for axis in axes:
+            index = 2 * index + lax.axis_index(axis)
+        return index.astype(jnp.int32)[None]
+
+    def moved(self, pieces, *axes):
+        count = len(pieces)
+        routes = [[(i, i ^ k) for i in range(count)] for k in range(count)]
+        return [pieces[0]] + [lax.ppermute(pieces[k], axes, routes[k]) for k in range(1, count)]
+
+    def gather(self, dense, w_in, w_out):
+        near = self.number("zl", "y")
+        own = pack(self.number("zh", "zl"), self.moved([dense] * 4, "zh", "zl"))
+        in_parts, out_parts = pick(near, w_in), pick(near, w_out)
+        own, first, second, third, in_parts, out_parts = together(
+            own, w_in[:1], w_in[1:2], w_in[2:], in_parts, out_parts
+        )
+        over_y, over_x, first, second, third, in_parts = together(
+            self.swap(own, "y"), self.swap(own, "x"), self.swap(first, "zh"), second, third, in_parts
+        )
+        firsts = [own, over_y, over_x]
         over_xy = self.swap(over_y, "x")
-        pieces = [own, over_y, over_x, over_xy]
-        pieces = [piece for near in pieces for piece in (near, self.swap(near, "c"))]
-        full = place(self.place_of("x", "y", "c"), pieces, (0, 2, 3)).reshape(32 * rows, columns)
-
-        def finish(near, far):
-            pieces = [near, self.swap(near, "c"), far, self.swap(far, "c")]
-            joined = place(self.place_of("zh", "c"), pieces, (0, 2))
-            return joined.reshape(-1, near.shape[-1])
-
-        def finish_in(signal):
-            signal, raw = together(signal, in_raw)
-            return signal, finish(in_near, self.trade(raw, ("zl", "y")))
-
-        out_near = self.trade(w_out, ("zl", "y"))
-        out_far = self.swap(out_near, "zh")
-
-        def finish_out(signal):
-            signal, far = together(signal, out_far)
-            return signal, finish(out_near, far)
-
-        return full, finish_in, finish_out
+        second = self.swap(second, "zh")
+        theirs, in_parts = together([self.swap(value, "c") for value in firsts], in_parts)
+        in_near = self.moved(in_parts, "zl", "y")
+        over_xy, second, third = together(over_xy, second, third)
+        pieces = [value for pair in zip(firsts, theirs) for value in pair]
+        pieces += [over_xy, self.swap(over_xy, "c")]
+        third = self.swap(third, "zh")
+        full = place(self.place_of("x", "y", "c"), pieces, (0, 2, 3))
+        full = full.reshape(32 * dense.shape[0], dense.shape[1])
+        full, in_near, out_parts = together(full, in_near, out_parts)
+        out_near = self.moved(out_parts, "zl", "y")
+        return full, {"in_near": in_near, "in_far": [first, second, third], "out_near": out_near}
+
+    def after_project(self, kept, value):
+        near = self.number("zl", "y")
+        value, far, out_near = together(value, kept["in_far"], kept["out_near"])
+        value, far, out_near = together(value, pick(near, *far), pack(near, out_near))
+        kept["in_far"] = self.moved(far, "zl", "y")
+        kept["out_near"] = out_near
+        kept["out_far"] = [self.swap(out_near[:1], "zh")]
+        return value
+
+    def after_middle(self, kept, *values):
+        *values, kept["in_far"], near, first = together(
+            *values, kept["in_far"], kept["out_near"], kept["out_far"][0]
+        )
+        kept["out_near"] = near
+        kept["out_far"] = [first, self.swap(near[1:3], "zh")]
+        return values
+
+    def before_grads(self, kept, *values):
+        *values, near, second = together(*values, kept["out_near"], kept["out_far"][1])
+        kept["out_near"] = near
+        kept["out_far"] = [kept["out_far"][0], second, self.swap(near[3:], "zh")]
+        return values
+
+    def joined(self, near, far):
+        cores = [self.swap(part, "c") for part in far]
+        return join(self.place_of("zh", "c"), near, self.swap(near, "c"), far, cores)
+
+    def expert_in(self, kept):
+        near = self.number("zl", "y")
+        return self.joined(pack(near, kept["in_near"]), [pack(near, kept["in_far"])])
+
+    def expert_out(self, kept, *values):
+        *values, last = together(*values, kept["out_far"][2])
+        return *values, self.joined(kept["out_near"], kept["out_far"][:2] + [last])
 
     def send_slots(self, slots):
         return self.trade(slots, ("x", "zl", "y"))
@@ -668,26 +912,32 @@
     def return_slots(self, slots):
         return self.trade(slots, ("x", "zl", "y"))
 
-    def core(self):
-        return self.place_of("c")
-
-    def expert_cores(self, mine, theirs):
-        return add(mine, self.swap(theirs, "c"))
-
-    def expert_far(self, part):
-        got = self.swap(self.half(part, "zh", 0, True), "zh")
-        return self.half(part, "zh", 0, False), got
-
-    def expert_end(self, mine, got):
-        return self.trade(add(mine, got), ("zl", "y")).astype(F32)
-
-    def scatter_rows(self, value):
-        rows, columns = value.shape
-        part = value.reshape(2, 4, 2, 2, rows // 32, columns)
-        part = self.add_halves(part, "c", 3)
-        part = self.add_halves(part, "x", 0)
-        part = self.add_halves(part, "y", 1)
-        return jnp.sum(self.trade(part, ("zh", "zl")).astype(F32), axis=0)
+    def other_core(self, theirs):
+        return self.swap(theirs, "c")
+
+    def expert_parts(self, mine, got, counts):
+        return add_halves(self.place_of("zh"), mine, got, counts)
+
+    def expert_far(self, parts):
+        return parts[0], [self.swap(part, "zh") for part in parts[1:]]
+
+    def expert_pick(self, mine, got):
+        return add_pick(self.number("zl", "y"), mine, got)
+
+    def expert_end(self, pieces):
+        return pack(self.number("zl", "y"), self.moved(pieces, "zl", "y"), F32)
+
+    def rows_pick(self, *pairs):
+        return dense_pick(self.number("x", "y"), pairs)
+
+    def rows_send(self, pieces):
+        return self.moved(pieces, "x", "y")
+
+    def rows_turn(self, pieces):
+        return turn(self.number("zh", "zl"), pieces)
+
+    def rows_end(self, pieces):
+        return sum(piece.astype(F32) for piece in self.moved(pieces, "zh", "zl"))
 
 
 class AxisLinks:
@@ -697,14 +947,30 @@
         self.fsdp = "fsdp"
         self.dp = "dp"
 
-    def gather_all(self, dense, w_in, w_out):
-        def finish(shard):
-            return lambda signal: (
-                signal,
-                lax.all_gather(shard, "fsdp", axis=1, tiled=True).reshape(-1, shard.shape[-1]),
-            )
-
-        return lax.all_gather(dense, self.data, axis=0, tiled=True), finish(w_in), finish(w_out)
+    def core(self):
+        return jnp.zeros((1,), jnp.int32)
+
+    def gather(self, dense, w_in, w_out):
+        full = lax.all_gather(dense, self.data, axis=0, tiled=True)
+        return full, {"in": w_in, "out": w_out}
+
+    def after_project(self, kept, value):
+        return value
+
+    def after_middle(self, kept, *values):
+        return values
+
+    def before_grads(self, kept, *values):
+        return values
+
+    def full_rows(self, shard):
+        return lax.all_gather(shard, "fsdp", axis=1, tiled=True).reshape(-1, shard.shape[-1])
+
+    def expert_in(self, kept):
+        return self.full_rows(kept["in"])
+
+    def expert_out(self, kept, *values):
+        return *values, self.full_rows(kept["out"])
 
     def send_slots(self, slots):
         return lax.all_to_all(slots, "dp", 0, 0, tiled=True)
@@ -712,30 +978,44 @@
     def return_slots(self, slots):
         return lax.all_to_all(slots, "dp", 0, 0, tiled=True)
 
-    def core(self):
-        return jnp.zeros((1,), jnp.int32)
-
-    def expert_cores(self, mine, theirs):
-        return jnp.stack([mine, theirs], axis=2)
-
-    def expert_far(self, part):
-        return part, None
-
-    def expert_end(self, part, got):
-        grad = part.reshape(1, -1, part.shape[-1])
-        return lax.psum_scatter(grad, "fsdp", scatter_dimension=1, tiled=True).astype(F32)
-
-    def scatter_rows(self, value):
-        return lax.psum_scatter(value.astype(F32), self.data, scatter_dimension=0, tiled=True)
+    def other_core(self, theirs):
+        return theirs
+
+    def expert_parts(self, mine, got, counts):
+        return [jnp.stack([mine, got], axis=2).reshape(1, -1, mine.shape[-1])]
+
+    def expert_far(self, parts):
+        return parts[0], []
+
+    def expert_pick(self, mine, got):
+        return [mine]
+
+    def expert_end(self, pieces):
+        return lax.psum_scatter(pieces[0], "fsdp", scatter_dimension=1, tiled=True).astype(F32)
+
+    def rows_pick(self, *pairs):
+        value = jnp.concatenate([jnp.stack(pair, axis=3) for pair in pairs], axis=-1)
+        value = value.transpose(0, 2, 1, 3, 4, 5)
+        return [value.reshape(-1, value.shape[-1]).astype(F32)]
+
+    def rows_send(self, pieces):
+        return [lax.psum_scatter(pieces[0], self.data, scatter_dimension=0, tiled=True)]
+
+    def rows_turn(self, pieces):
+        return pieces
+
+    def rows_end(self, pieces):
+        return pieces[0]
 
 
 def per_device(
     links, tokens, gain_attn, w_qkv, w_proj, gain_moe, w_router, w_in, w_out, routes, slot_ids, cotangent
 ):
+    core = links.core()
     small = jnp.concatenate([w_router, gain_attn[:, None], gain_moe[:, None]], axis=1)
     small = jnp.pad(small, ((0, 0), (0, LANES - small.shape[1])))
     own_qkv = by_pair(w_qkv)
-    dense, finish_in, finish_out = links.gather_all(
+    dense, kept = links.gather(
         jnp.concatenate([own_qkv, w_proj, small], axis=1), w_in, w_out
     )
     routes_t = routes.T
@@ -743,43 +1023,72 @@
     targets = jnp.where(slot_ids < CAP, routes * CAP + slot_ids, -1)
 
     qkv, act_one, table = project(tokens, dense)
+    qkv = links.after_project(kept, qkv)
     attended, logs = attention_forward(qkv)
     mid, act_two, columns, gates, rows_sent = middle(
         routes_t, slots_t, tokens, attended, dense, table
     )
-    rows_sent, expert_in = finish_in(rows_sent)
+    rows_sent, gates = links.after_middle(kept, rows_sent, gates)
     slot_rows = links.send_slots(rows_sent)
-    grads_sent, slot_rows = together(slot_grads(routes_t, slots_t, gates, cotangent), slot_rows)
+    grads_sent = slot_grads(routes_t, slots_t, gates, cotangent)
+    expert_in = links.expert_in(kept)
+    grads_sent, slot_rows, expert_in = links.before_grads(kept, grads_sent, slot_rows, expert_in)
     grad_slots = links.send_slots(grads_sent)
     held = slot_rows.shape
     expert_rows = slot_rows.reshape(-1, WIDTH)
     hidden, slope = expert_up(expert_rows, expert_in)
-    hidden, expert_out = finish_out(hidden)
-    result, grad_slots = together(expert_down(hidden, expert_out), grad_slots)
+    hidden, expert_out = links.expert_out(kept, hidden)
+    result, grad_slots, slope = together(expert_down(hidden, expert_out), grad_slots, slope)
     flat_result = links.return_slots(result.reshape(held)).reshape(SLOTS, WIDTH)
     grad_result = grad_slots.reshape(-1, WIDTH)
 
-    core = links.core()
-    out_part = links.expert_cores(*out_grad(core, hidden, grad_result))
+    out_mine, out_theirs = out_grad(core, hidden, grad_result)
+    out_theirs, slope = together(out_theirs, slope)
+    out_got = links.other_core(out_theirs)
     grad_pre, grad_rows = expert_back(grad_result, slope, expert_out, expert_in)
-    grad_rows, flat_result = together(grad_rows, flat_result)
+    grad_rows, out_got = together(grad_rows, out_got)
     rows_back = links.return_slots(grad_rows.reshape(held)).reshape(SLOTS, WIDTH)
-    out_mine, out_got = links.expert_far(out_part)
-    in_part = links.expert_cores(*in_grad(core, expert_rows, grad_pre))
-    in_mine, in_got = links.expert_far(in_part)
-
+    grad_pre, *out_parts = together(grad_pre, *links.expert_parts(out_mine, out_got, (4,)))
+    out_keep, out_far = links.expert_far(out_parts)
+    in_mine, in_theirs = in_grad(core, expert_rows, grad_pre)
+    in_theirs, flat_result = together(in_theirs, flat_result)
+    in_got = links.other_core(in_theirs)
     output, grad_logits = combine_results(routes, targets, columns, mid, cotangent, flat_result)
+    grad_logits, rows_back = together(grad_logits, rows_back)
     grad_mid, low, grad_attended, d_gain = middle_back(
         targets, grad_logits, mid, cotangent, rows_back, dense, table
     )
+    rest_mine, rest_theirs = proj_grads(core, attended, low, act_two, grad_logits, d_gain)
+    rest_theirs, grad_attended = together(rest_theirs, grad_attended)
     grad_qkv = attention_backward(qkv, attended, logs, grad_attended)
-    d_qkv = qkv_grads(act_one, grad_qkv)
-    d_rest = proj_grads(attended, low, act_two, grad_logits, d_gain)
+    grad_qkv, rest_theirs, out_far, in_got = together(grad_qkv, rest_theirs, out_far, in_got)
+    rest_got = links.other_core(rest_theirs)
+    in_parts, grad_qkv = together(links.expert_parts(in_mine, in_got, (1, 2, 1)), grad_qkv)
+    in_keep, in_first = links.expert_far(in_parts[:2])
+    qkv_mine, qkv_theirs = qkv_grads(core, act_one, grad_qkv)
+    qkv_theirs, rest_got, in_first, in_later = together(
+        qkv_theirs, rest_got, in_first, in_parts[2:]
+    )
+    qkv_got = links.other_core(qkv_theirs)
+    qkv_parts, grad_qkv, out_keep, in_later = together(
+        links.rows_pick((qkv_mine, qkv_got), (rest_mine, rest_got)), grad_qkv, out_keep, in_later
+    )
+    qkv_sent = links.rows_send(qkv_parts)
+    _, in_second = links.expert_far([in_keep] + list(in_later[:1]))
     grad_tokens = token_grads(grad_qkv, dense, tokens, grad_mid, table)
-    d_out = links.expert_end(out_mine, out_got)
-    d_in = links.expert_end(in_mine, in_got)
-    d_rest = links.scatter_rows(d_rest)
-    d_qkv = links.scatter_rows(d_qkv)
+    out_pieces = links.expert_pick(out_keep, out_far)
+    qkv_sent, grad_tokens, out_pieces, in_second, in_later = together(
+        qkv_sent, grad_tokens, out_pieces, in_second, in_later
+    )
+    turned, out_pieces, in_keep, in_last = together(
+        links.rows_turn(qkv_sent), out_pieces, in_keep, in_later[1:]
+    )
+    _, in_third = links.expert_far([in_keep] + list(in_last))
+    d_dense = links.rows_end(turned)
+    d_out = links.expert_end(out_pieces)
+    d_in = links.expert_end(links.expert_pick(in_keep, in_first + in_second + in_third))
+    d_qkv = d_dense[:, : 3 * WIDTH]
+    d_rest = d_dense[:, 3 * WIDTH :]
     d_gain_attn = jnp.sum(d_qkv * own_qkv.astype(F32), axis=1) / gain_attn.astype(F32)
     return (
         output,

time: 482 us -> 474 us (0.983)
  Pallas kernels: 170 us -> 223 us
  blocking collectives: 49.7 us -> 0 us
  other arithmetic: 35.1 us -> 5.52 us
  local copies, waits for them, and re-layouts: 13.2 us -> 28.6 us
  starting transfers between devices: 57.6 us -> 67.3 us
  waiting for transfers between devices: 154 us -> 146 us
    pallas_call x0 -> x17, Pallas kernels: none -> 65.2 us  [the longest x6 19 us: pack(): call('pack', pack_kernel, (parts_of(shape[-1]),), [columns_of(shape[1:])]...]
    all_to_all x2 -> x0, blocking collectives: 49.7 us -> none  [trade(): return lax.all_to_all(value, axes, 0, 0, tiled=True)]
    ppermute x0 -> x24, waiting for transfers between devices: none -> 38.7 us  [moved(): lax.ppermute(pieces[k], axes, routes[k])]
    ppermute x0 -> x24, starting transfers between devices: none -> 30.7 us  [moved(): lax.ppermute(pieces[k], axes, routes[k])]
    ppermute x23 -> x27, waiting for transfers between devices: 125 us -> 96.6 us  [swap(): return lax.ppermute(value, axis, [(0, 1), (1, 0)])]
    convert_element_type x12 -> x0, other arithmetic: 23.4 us -> none  [the longest x10 17.6 us: add(): return (mine.astype(F32) + got.astype(F32)).astype(BF16)]
    all_to_all x10 -> x4, waiting for transfers between devices: 28.5 us -> 10.4 us  [trade(): return lax.all_to_all(value, axes, 0, 0, tiled=True)]
    all_to_all x10 -> x4, starting transfers between devices: 39.1 us -> 22.7 us  [trade(): return lax.all_to_all(value, axes, 0, 0, tiled=True)]
  transfers between devices with their start and end apart: 33 -> 55, of which waited for: 13 -> 20; matrix products, arithmetic and copies ran while one was open for 8% -> 3% of each run, Pallas kernels for 35% -> 43%
where the time goes in v3:
time: 474 us; the launch traced here: 471 us
  Pallas kernels  223 us (47%)
  waiting for transfers between devices  146 us (31%)
  starting transfers between devices  67.3 us (14%)
  local copies, waits for them, and re-layouts  28.6 us (6%)
  other arithmetic  5.52 us (1%)
    ppermute x27, waiting for transfers between devices, swap(): return lax.ppermute(value, axis, [(0, 1), (1, 0)])  96.6 us
    ppermute x24, waiting for transfers between devices, moved(): lax.ppermute(pieces[k], axes, routes[k])  38.7 us
    ppermute x24, starting transfers between devices, moved(): lax.ppermute(pieces[k], axes, routes[k])  30.7 us
    all_to_all x4, starting transfers between devices, trade(): return lax.all_to_all(value, axes, 0, 0, tiled=True)  22.7 us
    pallas_call x6, Pallas kernels, pack(): call('pack', pack_kernel, (parts_of(shape[-1]),), [columns_of(shape[1:])]...  19 us
    pallas_call x1, Pallas kernels, expert_back(): call('expert_back', expert_back_kernel, (count // ROW_BLOCK,), [narrow, w...  18.2 us
    unnamed x100, local copies, waits for them, and re-layouts  17.4 us
    pallas_call x1, Pallas kernels, expert_up(): call('expert_up', expert_up_kernel, (depth // F_BLOCK,), [whole(count, WI...  16.3 us
  transfers between devices with their start and end apart: 55, of which 20 were waited for; matrix products, arithmetic and copies ran while one was open for 3% of the time, Pallas kernels for 43%

profile of v3, /device:TPU:0, one launch (start us, length us, event | category | flops | bytes accessed | tf_op | source)
XLA Modules:
  0.0 471.4 jit_solution(14275387462601472128)
XLA Ops:
  31.7 11.9 %collective-permute-done.6.refs_1_ = bf16[1,48,3072]{2,1,0:T(8,128)(2,1)S(1)} collective-permute-done((bf16[1,48,3072]{2,1,0:T(8,128)(2,1)S(1)}, bf16[1,48,3072]{2,1,0:T(8,128)(2,1)S(1)}, u32[]{:S(2)}, u32[]{:S(2)}) %collective-permute-start.6) | collective-permute-done | bytes 294944 | tf_op jit(solution)/shard_map/ppermute | solution.py:827
  46.9 14.6 %collective-permute-done.10.refs_2_ = bf16[1,48,3072]{2,1,0:T(8,128)(2,1)S(1)} collective-permute-done((bf16[1,48,3072]{2,1,0:T(8,128)(2,1)}, bf16[1,48,3072]{2,1,0:T(8,128)(2,1)S(1)}, u32[]{:S(2)}, u32[]{:S(2)}) %collective-permute-start.10) | collective-permute-done | bytes 294944 | tf_op jit(solution)/shard_map/ppermute | solution.py:827
  73.7 8.7 %collective-permute-done.13.refs_2_ = bf16[48,3072]{1,0:T(8,128)(2,1)} collective-permute-done((bf16[48,3072]{1,0:T(8,128)(2,1)}, bf16[48,3072]{1,0:T(8,128)(2,1)}, u32[]{:S(2)}, u32[]{:S(2)}) %collective-permute-start.13) | collective-permute-done | bytes 294944 | tf_op jit(solution)/shard_map/ppermute | solution.py:847
  82.3 7.4 %collective-permute-done.14.refs_3_ = bf16[48,3072]{1,0:T(8,128)(2,1)} collective-permute-done((bf16[48,3072]{1,0:T(8,128)(2,1)}, bf16[48,3072]{1,0:T(8,128)(2,1)}, u32[]{:S(2)}, u32[]{:S(2)}) %collective-permute-start.14) | collective-permute-done | bytes 294944 | tf_op jit(solution)/shard_map/ppermute | solution.py:847
  93.2 7.9 %project.1 = (bf16[576,2304]{1,0:T(8,128)(2,1)}, bf16[576,768]{1,0:T(8,128)(2,1)}, bf16[128,768]{1,0:T(8,128)(2,1)}) custom-call(bf16[576,768]{1,0:T(8,128)(2,1)} %tokens_ref.5, bf16[768,3200]{1,0:T(8,128)(2,1)} %bitcast.26, bf16[768,3200]{1,0:T(8,128)(2,1)} %bitcast.27), custom_call_target="tpu_custom_call" | custom-call | flops 1 | bytes 1 | tf_op jit(solution)/shard_map/project/pallas_call | solution.py:176
  118.6 10.4 %attention_forward.1 = (bf16[576,768]{1,0:T(8,128)(2,1)}, f32[1,6,2,576]{3,2,1,0:T(2,128)}) custom-call(bf16[576,2304]{1,0:T(8,128)(2,1)} %get-tuple-element.256.qkv_ref), custom_call_target="tpu_custom_call" | custom-call | flops 1 | bytes 1 | tf_op jit(solution)/shard_map/attention_forward/pallas_call | solution.py:135
  129.0 9.3 %middle.1 = (f32[576,768]{1,0:T(8,128)}, bf16[576,768]{1,0:T(8,128)(2,1)}, f32[576,128]{1,0:T(8,128)}, f32[8,576]{1,0:T(8,128)}, bf16[8,152,768]{2,1,0:T(8,128)(2,1)}) custom-call(s32[2,576]{1,0:T(2,128)} %bitcast.48, s32[2,576]{1,0:T(2,128)} %bitcast.50, bf16[576,768]{1,0:T(8,128)(2,1)} %tokens_ref.5, ...), custom_call_target="tpu_custom_call" | custom-call | flops 1 | bytes 1 | tf_op jit(solution)/shard_map/middle/pallas_call | solution.py:243
  166.0 11.3 %collective-permute-done.25.refs_4_ = bf16[2,192,768]{2,1,0:T(8,128)(2,1)} collective-permute-done((bf16[2,192,768]{2,1,0:T(8,128)(2,1)}, bf16[2,192,768]{2,1,0:T(8,128)(2,1)}, u32[]{:S(2)}, u32[]{:S(2)}) %collective-permute-start.25) | collective-permute-done | bytes 589856 | tf_op jit(solution)/shard_map/ppermute | solution.py:827
  190.5 16.3 %expert_up.1 = (bf16[1216,3072]{1,0:T(8,128)(2,1)}, bf16[1216,3072]{1,0:T(8,128)(2,1)}) custom-call(bf16[1216,768]{1,0:T(8,128)(2,1)} %bitcast.37, bf16[768,3072]{1,0:T(8,128)(2,1)} %bitcast.31), custom_call_target="tpu_custom_call" | custom-call | flops 1 | bytes 1 | tf_op jit(solution)/shard_map/expert_up/pallas_call | solution.py:304
  206.8 7.0 %collective-permute-done.26.refs_5_ = bf16[1,192,768]{2,1,0:T(8,128)(2,1)} collective-permute-done((bf16[1,192,768]{2,1,0:T(8,128)(2,1)}, bf16[1,192,768]{2,1,0:T(8,128)(2,1)}, u32[]{:S(2)}, u32[]{:S(2)}) %collective-permute-start.26) | collective-permute-done | bytes 294944 | tf_op jit(solution)/shard_map/ppermute | solution.py:827
  221.7 10.3 %expert_down.1 = bf16[1216,768]{1,0:T(8,128)(2,1)} custom-call(bf16[1216,3072]{1,0:T(8,128)(2,1)} %get-tuple-element.283.hidden_ref, bf16[3072,768]{1,0:T(8,128)(2,1)} %bitcast.33), custom_call_target="tpu_custom_call" | custom-call | flops 1 | bytes 1 | tf_op jit(solution)/shard_map/expert_down/pallas_call | solution.py:320
  233.2 8.8 %all-to-all-start.2 = ((bf16[8,152,768]{2,1,0:T(8,128)(2,1)}), bf16[8,152,768]{2,1,0:T(8,128)(2,1)}, u32[]{:S(2)}, u32[]{:S(2)}) async-start(bf16[8,152,768]{2,1,0:T(8,128)(2,1)} %bitcast.40), calls=%async_computation.2 | async-start | bytes 3735552 | tf_op jit(solution)/shard_map/all_to_all | solution.py:830
  242.0 12.0 %out_grad.1 = (bf16[2,4,192,768]{3,2,1,0:T(8,128)(2,1)}, bf16[2,4,192,768]{3,2,1,0:T(8,128)(2,1)}) custom-call(s32[1]{0:T(128)} %bitcast.4.me_ref, bf16[1216,3072]{1,0:T(8,128)(2,1)} %get-tuple-element.283.hidden_ref, bf16[1216,768]{1,0:T(8,128)(2,1)} %bitcast.35), custom_call_target="tpu_custom_call" | custom-call | flops 1 | bytes 1 | tf_op jit(solution)/shard_map/out_grad/pallas_call | solution.py:363
  254.1 18.2 %expert_back.1 = (bf16[1216,3072]{1,0:T(8,128)(2,1)}, bf16[1216,768]{1,0:T(8,128)(2,1)}) custom-call(bf16[1216,768]{1,0:T(8,128)(2,1)} %bitcast.36, bf16[1216,3072]{1,0:T(8,128)(2,1)} %get-tuple-element.292.slope_ref, bf16[3072,768]{1,0:T(8,128)(2,1)} %bitcast.34, bf16[768,3072]{1,0:T(8,128)(2,1)} %bitcast.32), custom_call_target="tpu_custom_call" | custom-call | flops 1 | bytes 1 | tf_op jit(solution)/shard_map/expert_back/pallas_call | solution.py:341
  283.4 11.5 %in_grad.1 = (bf16[2,4,48,3072]{3,2,1,0:T(8,128)(2,1)}, bf16[2,4,48,3072]{3,2,1,0:T(8,128)(2,1)}) custom-call(s32[1]{0:T(128)} %bitcast.4.me_ref, bf16[1216,768]{1,0:T(8,128)(2,1)} %bitcast.38, bf16[1216,3072]{1,0:T(8,128)(2,1)} %get-tuple-element.300.grad_ref), custom_call_target="tpu_custom_call" | custom-call | flops 1 | bytes 1 | tf_op jit(solution)/shard_map/in_grad/pallas_call | solution.py:391
  298.9 7.1 %combine.1 = (bf16[576,768]{1,0:T(8,128)(2,1)}, bf16[576,128]{1,0:T(8,128)(2,1)}) custom-call(s32[576,2]{1,0:T(8,128)} %copy.51.routes_ref, s32[576,2]{1,0:T(8,128)} %add_select_fusion.targets_ref, f32[576,128]{1,0:T(8,128)} %get-tuple-element.259.columns_ref, f32[576,768]{1,0:T(8,128)} %get-tuple-element.260.mid_ref, bf16[576,768]{1,0:T(8,128)(2,1)} %grad_ref.5, ...), custom_call_target="tpu_custom_call" | custom-call | flops 1 | bytes 1 | tf_op jit(solution)/shard_map/combine/pallas_call | solution.py:432
  312.8 7.5 %middle_back.1 = (f32[576,768]{1,0:T(8,128)}, bf16[576,768]{1,0:T(8,128)(2,1)}, bf16[576,768]{1,0:T(8,128)(2,1)}, f32[8,768]{1,0:T(8,128)}) custom-call(s32[576,2]{1,0:T(8,128)} %add_select_fusion.targets_ref, bf16[576,128]{1,0:T(8,128)(2,1)} %get-tuple-element.310.logits_ref, f32[576,768]{1,0:T(8,128)} %get-tuple-element.260.mid_ref, ...), custom_call_target="tpu_custom_call" | custom-call | flops 1 | bytes 1 | tf_op jit(solution)/shard_map/middle_back/pallas_call | solution.py:474
  324.6 14.3 %attention_backward.1.grad_ref = bf16[576,2304]{1,0:T(8,128)(2,1)} custom-call(bf16[576,2304]{1,0:T(8,128)(2,1)} %get-tuple-element.256.qkv_ref, bf16[576,768]{1,0:T(8,128)(2,1)} %get-tuple-element.257.attended_ref.out_ref, f32[1,6,2,576]{3,2,1,0:T(2,128)} %get-tuple-element.307.log_ref, bf16[576,768]{1,0:T(8,128)(2,1)} %get-tuple-element.317.grad_ref), custom_call_target="tpu_custom_call" | custom-call | flops 1 | bytes 1 | tf_op jit(solution)/shard_map/attention_backward/pallas_call | solution.py:147
  338.9 10.7 %collective-permute-done.32.refs_0_ = bf16[4,192,768]{2,1,0:T(8,128)(2,1)S(1)} collective-permute-done((bf16[4,192,768]{2,1,0:T(8,128)(2,1)}, bf16[4,192,768]{2,1,0:T(8,128)(2,1)S(1)}, u32[]{:S(2)}, u32[]{:S(2)}) %collective-permute-start.32) | collective-permute-done | bytes 1179680 | tf_op jit(solution)/shard_map/ppermute | solution.py:827
  354.7 7.9 %qkv_grads.1 = (bf16[2,2,4,24,2304]{4,3,2,1,0:T(8,128)(2,1)}, bf16[2,2,4,24,2304]{4,3,2,1,0:T(8,128)(2,1)}) custom-call(s32[1]{0:T(128)} %bitcast.4.me_ref, bf16[576,768]{1,0:T(8,128)(2,1)} %get-tuple-element.305.act_ref, bf16[576,2304]{1,0:T(8,128)(2,1)} %attention_backward.1.grad_ref), custom_call_target="tpu_custom_call" | custom-call | flops 1 | bytes 1 | tf_op jit(solution)/shard_map/qkv_grads/pallas_call | solution.py:543
  362.5 7.7 %collective-permute-done.35.refs_0_ = bf16[1,48,3072]{2,1,0:T(8,128)(2,1)S(1)} collective-permute-done((bf16[1,48,3072]{2,1,0:T(8,128)(2,1)}, bf16[1,48,3072]{2,1,0:T(8,128)(2,1)S(1)}, u32[]{:S(2)}, u32[]{:S(2)}) %collective-permute-start.35) | collective-permute-done | bytes 294944 | tf_op jit(solution)/shard_map/ppermute | solution.py:827
  387.8 8.1 %token_grads.1 = f32[576,768]{1,0:T(8,128)} custom-call(bf16[576,2304]{1,0:T(8,128)(2,1)} %attention_backward.1.grad_ref, bf16[768,3200]{1,0:T(8,128)(2,1)} %bitcast.30, bf16[576,768]{1,0:T(8,128)(2,1)} %tokens_ref.5, f32[576,768]{1,0:T(8,128)} %get-tuple-element.349.grad_mid_ref, bf16[128,768]{1,0:T(8,128)(2,1)} %get-tuple-element.258.table_ref), custom_call_target="tpu_custom_call" | custom-call | flops 1 | bytes 1 | tf_op jit(solution)/shard_map/token_grads/pallas_call | solution.py:564
  395.9 15.8 %collective-permute-done.40.refs_1_ = bf16[2,48,3072]{2,1,0:T(8,128)(2,1)S(1)} collective-permute-done((bf16[2,48,3072]{2,1,0:T(8,128)(2,1)S(1)}, bf16[2,48,3072]{2,1,0:T(8,128)(2,1)S(1)}, u32[]{:S(2)}, u32[]{:S(2)}) %collective-permute-start.40) | collective-permute-done | bytes 589856 | tf_op jit(solution)/shard_map/ppermute | solution.py:827
  434.2 11.7 %collective-permute-done.44.refs_2_ = bf16[1,48,3072]{2,1,0:T(8,128)(2,1)S(1)} collective-permute-done((bf16[1,48,3072]{2,1,0:T(8,128)(2,1)}, bf16[1,48,3072]{2,1,0:T(8,128)(2,1)S(1)}, u32[]{:S(2)}, u32[]{:S(2)}) %collective-permute-start.44) | collective-permute-done | bytes 294944 | tf_op jit(solution)/shard_map/ppermute | solution.py:827
  (247 shorter events, 213.8 us)
Async XLA Ops:
  63.1 26.7 %collective-permute-start.14 = (bf16[48,3072]{1,0:T(8,128)(2,1)}, bf16[48,3072]{1,0:T(8,128)(2,1)}, u32[]{:S(2)}, u32[]{:S(2)}) collective-permute-start(bf16[48,3072]{1,0:T(8,128)(2,1)} %get-tuple-element.230), channel_id=1, source_target_pairs={{0,6},{2,4},{4,2},{6,0},{1,7},{3,5},{5,3},{7,1},{8,14},{10,12},{12... | collective-permute-start | bytes 884744 | tf_op jit(solution)/shard_map/ppermute | solution.py:847
  66.0 35.1 %collective-permute-start.15 = (bf16[2,48,3072]{2,1,0:T(8,128)(2,1)}, bf16[2,48,3072]{2,1,0:T(8,128)(2,1)}, u32[]{:S(2)}, u32[]{:S(2)}) collective-permute-start(bf16[2,48,3072]{2,1,0:T(8,128)(2,1)} %slice.36), channel_id=1, source_target_pairs={{0,8},{8,0},{1,9},{9,1},{2,10},{10,2},{3,11},{11,3},{4,12},{12,4},... | collective-permute-start | bytes 1769480 | tf_op jit(solution)/shard_map/ppermute | solution.py:827
  114.9 23.4 %collective-permute-start.22 = (bf16[1,192,768]{2,1,0:T(8,128)(2,1)S(1)}, bf16[1,192,768]{2,1,0:T(8,128)(2,1)S(1)}, u32[]{:S(2)}, u32[]{:S(2)}) collective-permute-start(bf16[1,192,768]{2,1,0:T(8,128)(2,1)S(1)} %slice.37), channel_id=1, source_target_pairs={{0,8},{8,0},{1,9},{9,1},{2,10},{10,2},{3,11},{11,3},{4,12},{12,4},... | collective-permute-start | bytes 884744 | tf_op jit(solution)/shard_map/ppermute | solution.py:827
  115.0 23.3 %collective-permute-start.19 = (bf16[48,3072]{1,0:T(8,128)(2,1)S(1)}, bf16[48,3072]{1,0:T(8,128)(2,1)S(1)}, u32[]{:S(2)}, u32[]{:S(2)}) collective-permute-start(bf16[48,3072]{1,0:T(8,128)(2,1)S(1)} %copy-done.47), channel_id=1, source_target_pairs={{0,2},{2,0},{4,6},{6,4},{1,3},{3,1},{5,7},{7,5},{8,10},{10,8},{12,... | collective-permute-start | bytes 884744 | tf_op jit(solution)/shard_map/ppermute | solution.py:847
  116.6 21.8 %collective-permute-start.20 = (bf16[48,3072]{1,0:T(8,128)(2,1)S(1)}, bf16[48,3072]{1,0:T(8,128)(2,1)S(1)}, u32[]{:S(2)}, u32[]{:S(2)}) collective-permute-start(bf16[48,3072]{1,0:T(8,128)(2,1)S(1)} %copy-done.46), channel_id=1, source_target_pairs={{0,4},{2,6},{4,0},{6,2},{1,5},{3,7},{5,1},{7,3},{8,12},{10,14},{12... | collective-permute-start | bytes 884744 | tf_op jit(solution)/shard_map/ppermute | solution.py:847
  139.4 42.9 %all-to-all-start = ((bf16[8,152,768]{2,1,0:T(8,128)(2,1)}), bf16[8,152,768]{2,1,0:T(8,128)(2,1)S(1)}, u32[]{:S(2)}, u32[]{:S(2)}) async-start(bf16[8,152,768]{2,1,0:T(8,128)(2,1)} %get-tuple-element.269), calls=%async_computation | async-start | bytes 3735552 | tf_op jit(solution)/shard_map/all_to_all | solution.py:830
  152.4 24.9 %collective-permute-start.25 = (bf16[2,192,768]{2,1,0:T(8,128)(2,1)}, bf16[2,192,768]{2,1,0:T(8,128)(2,1)}, u32[]{:S(2)}, u32[]{:S(2)}) collective-permute-start(bf16[2,192,768]{2,1,0:T(8,128)(2,1)} %slice.38), channel_id=1, source_target_pairs={{0,8},{8,0},{1,9},{9,1},{2,10},{10,2},{3,11},{11,3},{4,12},{12,4},... | collective-permute-start | bytes 1769480 | tf_op jit(solution)/shard_map/ppermute | solution.py:827
  183.5 48.5 %all-to-all-start.1 = ((bf16[8,152,768]{2,1,0:T(8,128)(2,1)}), bf16[8,152,768]{2,1,0:T(8,128)(2,1)S(1)}, u32[]{:S(2)}, u32[]{:S(2)}) async-start(bf16[8,152,768]{2,1,0:T(8,128)(2,1)} %slot_grads.1), calls=%async_computation.1 | async-start | bytes 3735552 | tf_op jit(solution)/shard_map/all_to_all | solution.py:830
  187.3 28.5 %collective-permute-start.27 = (bf16[4,192,768]{2,1,0:T(8,128)(2,1)S(1)}, bf16[4,192,768]{2,1,0:T(8,128)(2,1)}, u32[]{:S(2)}, u32[]{:S(2)}) collective-permute-start(bf16[4,192,768]{2,1,0:T(8,128)(2,1)S(1)} %copy-done.2), channel_id=1, source_target_pairs={{0,1},{1,0},{2,3},{3,2},{4,5},{5,4},{6,7},{7,6},{8,9},{9,8},{10,11... | collective-permute-start | bytes 3538952 | tf_op jit(solution)/shard_map/ppermute | solution.py:827
  188.1 25.7 %collective-permute-start.26 = (bf16[1,192,768]{2,1,0:T(8,128)(2,1)}, bf16[1,192,768]{2,1,0:T(8,128)(2,1)}, u32[]{:S(2)}, u32[]{:S(2)}) collective-permute-start(bf16[1,192,768]{2,1,0:T(8,128)(2,1)} %slice.39), channel_id=1, source_target_pairs={{0,8},{8,0},{1,9},{9,1},{2,10},{10,2},{3,11},{11,3},{4,12},{12,4},... | collective-permute-start | bytes 884744 | tf_op jit(solution)/shard_map/ppermute | solution.py:827
  190.0 25.8 %collective-permute-start.29 = (bf16[2,192,768]{2,1,0:T(8,128)(2,1)}, bf16[2,192,768]{2,1,0:T(8,128)(2,1)}, u32[]{:S(2)}, u32[]{:S(2)}) collective-permute-start(bf16[2,192,768]{2,1,0:T(8,128)(2,1)} %collective-permute-done.25.refs_4_), channel_id=1, source_target_pairs={{0,1},{1,0},{2,3},{3,2},{4,5},{5,4},{6,7},{7,6},{8,9},{9,8},{10,11... | collective-permute-start | bytes 1769480 | tf_op jit(solution)/shard_map/ppermute | solution.py:827
  190.2 23.6 %collective-permute-start.28 = (bf16[1,192,768]{2,1,0:T(8,128)(2,1)S(1)}, bf16[1,192,768]{2,1,0:T(8,128)(2,1)}, u32[]{:S(2)}, u32[]{:S(2)}) collective-permute-start(bf16[1,192,768]{2,1,0:T(8,128)(2,1)S(1)} %collective-permute-done.22.refs_3_), channel_id=1, source_target_pairs={{0,1},{1,0},{2,3},{3,2},{4,5},{5,4},{6,7},{7,6},{8,9},{9,8},{10,11... | collective-permute-start | bytes 884744 | tf_op jit(solution)/shard_map/ppermute | solution.py:827
  233.2 39.0 %all-to-all-start.2 = ((bf16[8,152,768]{2,1,0:T(8,128)(2,1)}), bf16[8,152,768]{2,1,0:T(8,128)(2,1)}, u32[]{:S(2)}, u32[]{:S(2)}) async-start(bf16[8,152,768]{2,1,0:T(8,128)(2,1)} %bitcast.40), calls=%async_computation.2 | async-start | bytes 3735552 | tf_op jit(solution)/shard_map/all_to_all | solution.py:830
  273.7 37.8 %all-to-all-start.3 = ((bf16[8,152,768]{2,1,0:T(8,128)(2,1)}), bf16[8,152,768]{2,1,0:T(8,128)(2,1)S(1)}, u32[]{:S(2)}, u32[]{:S(2)}) async-start(bf16[8,152,768]{2,1,0:T(8,128)(2,1)} %bitcast.41), calls=%async_computation.3 | async-start | bytes 3735552 | tf_op jit(solution)/shard_map/all_to_all | solution.py:830
  294.8 54.8 %collective-permute-start.33 = (bf16[2,4,48,3072]{3,2,1,0:T(8,128)(2,1)}, bf16[2,4,48,3072]{3,2,1,0:T(8,128)(2,1)}, u32[]{:S(2)}, u32[]{:S(2)}) collective-permute-start(bf16[2,4,48,3072]{3,2,1,0:T(8,128)(2,1)} %get-tuple-element.320), channel_id=1, source_target_pairs={{0,1},{1,0},{2,3},{3,2},{4,5},{5,4},{6,7},{7,6},{8,9},{9,8},{10,11... | collective-permute-start | bytes 7077896 | tf_op jit(solution)/shard_map/ppermute | solution.py:827
  295.1 54.6 %collective-permute-start.32 = (bf16[4,192,768]{2,1,0:T(8,128)(2,1)}, bf16[4,192,768]{2,1,0:T(8,128)(2,1)S(1)}, u32[]{:S(2)}, u32[]{:S(2)}) collective-permute-start(bf16[4,192,768]{2,1,0:T(8,128)(2,1)} %get-tuple-element.319), channel_id=1, source_target_pairs={{0,8},{8,0},{1,9},{9,1},{2,10},{10,2},{3,11},{11,3},{4,12},{12,4},... | collective-permute-start | bytes 3538952 | tf_op jit(solution)/shard_map/ppermute | solution.py:827
  349.7 20.6 %collective-permute-start.34 = (bf16[2,2,4,24,896]{4,3,2,1,0:T(8,128)(2,1)S(1)}, bf16[2,2,4,24,896]{4,3,2,1,0:T(8,128)(2,1)S(1)}, u32[]{:S(2)}, u32[]{:S(2)}) collective-permute-start(bf16[2,2,4,24,896]{4,3,2,1,0:T(8,128)(2,1)S(1)} %copy-done.43), channel_id=1, source_target_pairs={{0,1},{1,0},{2,3},{3,2},{4,5},{5,4},{6,7},{7,6},{8,9},{9,8},{10,11... | collective-permute-start | bytes 2064392 | tf_op jit(solution)/shard_map/ppermute | solution.py:827
  380.5 31.3 %collective-permute-start.37 = (bf16[96,3200]{1,0:T(8,128)(2,1)}, bf16[96,3200]{1,0:T(8,128)(2,1)S(1)}, u32[]{:S(2)}, u32[]{:S(2)}) collective-permute-start(bf16[96,3200]{1,0:T(8,128)(2,1)} %get-tuple-element.345), channel_id=1, source_target_pairs={{0,2},{2,0},{16,18},{18,16},{1,3},{3,1},{17,19},{19,17},{4,6},{6,4... | collective-permute-start | bytes 1843208 | tf_op jit(solution)/shard_map/ppermute | solution.py:847
  381.9 29.8 %collective-permute-start.38 = (bf16[96,3200]{1,0:T(8,128)(2,1)}, bf16[96,3200]{1,0:T(8,128)(2,1)S(1)}, u32[]{:S(2)}, u32[]{:S(2)}) collective-permute-start(bf16[96,3200]{1,0:T(8,128)(2,1)} %get-tuple-element.346), channel_id=1, source_target_pairs={{0,16},{2,18},{16,0},{18,2},{1,17},{3,19},{17,1},{19,3},{4,20},{6,... | collective-permute-start | bytes 1843208 | tf_op jit(solution)/shard_map/ppermute | solution.py:847
  383.4 28.4 %collective-permute-start.39 = (bf16[96,3200]{1,0:T(8,128)(2,1)}, bf16[96,3200]{1,0:T(8,128)(2,1)S(1)}, u32[]{:S(2)}, u32[]{:S(2)}) collective-permute-start(bf16[96,3200]{1,0:T(8,128)(2,1)} %get-tuple-element.347), channel_id=1, source_target_pairs={{0,18},{2,16},{16,2},{18,0},{1,19},{3,17},{17,3},{19,1},{4,22},{6,... | collective-permute-start | bytes 1843208 | tf_op jit(solution)/shard_map/ppermute | solution.py:847
  383.9 27.8 %collective-permute-start.40 = (bf16[2,48,3072]{2,1,0:T(8,128)(2,1)S(1)}, bf16[2,48,3072]{2,1,0:T(8,128)(2,1)S(1)}, u32[]{:S(2)}, u32[]{:S(2)}) collective-permute-start(bf16[2,48,3072]{2,1,0:T(8,128)(2,1)S(1)} %copy-done.44), channel_id=1, source_target_pairs={{0,8},{8,0},{1,9},{9,1},{2,10},{10,2},{3,11},{11,3},{4,12},{12,4},... | collective-permute-start | bytes 1769480 | tf_op jit(solution)/shard_map/ppermute | solution.py:827
  420.6 33.7 %collective-permute-start.48 = (bf16[192,768]{1,0:T(8,128)(2,1)}, bf16[192,768]{1,0:T(8,128)(2,1)S(1)}, u32[]{:S(2)}, u32[]{:S(2)}) collective-permute-start(bf16[192,768]{1,0:T(8,128)(2,1)} %get-tuple-element.386), channel_id=1, source_target_pairs={{0,2},{2,0},{4,6},{6,4},{1,3},{3,1},{5,7},{7,5},{8,10},{10,8},{12,... | collective-permute-start | bytes 884744 | tf_op jit(solution)/shard_map/ppermute | solution.py:847
  422.2 33.3 %collective-permute-start.49 = (bf16[192,768]{1,0:T(8,128)(2,1)}, bf16[192,768]{1,0:T(8,128)(2,1)S(1)}, u32[]{:S(2)}, u32[]{:S(2)}) collective-permute-start(bf16[192,768]{1,0:T(8,128)(2,1)} %get-tuple-element.387), channel_id=1, source_target_pairs={{0,4},{2,6},{4,0},{6,2},{1,5},{3,7},{5,1},{7,3},{8,12},{10,14},{12... | collective-permute-start | bytes 884744 | tf_op jit(solution)/shard_map/ppermute | solution.py:847
  425.1 30.4 %collective-permute-start.50 = (bf16[192,768]{1,0:T(8,128)(2,1)}, bf16[192,768]{1,0:T(8,128)(2,1)S(1)}, u32[]{:S(2)}, u32[]{:S(2)}) collective-permute-start(bf16[192,768]{1,0:T(8,128)(2,1)} %get-tuple-element.388), channel_id=1, source_target_pairs={{0,6},{2,4},{4,2},{6,0},{1,7},{3,5},{5,3},{7,1},{8,14},{10,12},{12... | collective-permute-start | bytes 884744 | tf_op jit(solution)/shard_map/ppermute | solution.py:847
  (79 other events, 783.6 us)

commit v4 on v3

--- a/solution.py
+++ b/solution.py
@@ -861,14 +861,15 @@
         second = self.swap(second, "zh")
         theirs, in_parts = together([self.swap(value, "c") for value in firsts], in_parts)
         in_near = self.moved(in_parts, "zl", "y")
-        over_xy, second, third = together(over_xy, second, third)
+        over_xy, second, third, in_near, out_parts = together(
+            over_xy, second, third, in_near, out_parts
+        )
         pieces = [value for pair in zip(firsts, theirs) for value in pair]
         pieces += [over_xy, self.swap(over_xy, "c")]
         third = self.swap(third, "zh")
+        out_near = self.moved(out_parts, "zl", "y")
         full = place(self.place_of("x", "y", "c"), pieces, (0, 2, 3))
         full = full.reshape(32 * dense.shape[0], dense.shape[1])
-        full, in_near, out_parts = together(full, in_near, out_parts)
-        out_near = self.moved(out_parts, "zl", "y")
         return full, {"in_near": in_near, "in_far": [first, second, third], "out_near": out_near}
 
     def after_project(self, kept, value):
@@ -877,7 +878,7 @@
         value, far, out_near = together(value, pick(near, *far), pack(near, out_near))
         kept["in_far"] = self.moved(far, "zl", "y")
         kept["out_near"] = out_near
-        kept["out_far"] = [self.swap(out_near[:1], "zh")]
+        kept["out_far"] = [self.swap(out_near[:2], "zh")]
         return value
 
     def after_middle(self, kept, *values):
@@ -885,7 +886,7 @@
             *values, kept["in_far"], kept["out_near"], kept["out_far"][0]
         )
         kept["out_near"] = near
-        kept["out_far"] = [first, self.swap(near[1:3], "zh")]
+        kept["out_far"] = [first, self.swap(near[2:3], "zh")]
         return values
 
     def before_grads(self, kept, *values):
@@ -1042,17 +1043,17 @@
     flat_result = links.return_slots(result.reshape(held)).reshape(SLOTS, WIDTH)
     grad_result = grad_slots.reshape(-1, WIDTH)
 
+    grad_pre, grad_rows = expert_back(grad_result, slope, expert_out, expert_in)
+    grad_rows, grad_pre, hidden = together(grad_rows, grad_pre, hidden)
+    rows_back = links.return_slots(grad_rows.reshape(held)).reshape(SLOTS, WIDTH)
     out_mine, out_theirs = out_grad(core, hidden, grad_result)
-    out_theirs, slope = together(out_theirs, slope)
+    out_theirs, grad_pre = together(out_theirs, grad_pre)
     out_got = links.other_core(out_theirs)
-    grad_pre, grad_rows = expert_back(grad_result, slope, expert_out, expert_in)
-    grad_rows, out_got = together(grad_rows, out_got)
-    rows_back = links.return_slots(grad_rows.reshape(held)).reshape(SLOTS, WIDTH)
-    grad_pre, *out_parts = together(grad_pre, *links.expert_parts(out_mine, out_got, (4,)))
+    in_mine, in_theirs = in_grad(core, expert_rows, grad_pre)
+    in_theirs, out_got = together(in_theirs, out_got)
+    in_got = links.other_core(in_theirs)
+    flat_result, out_parts = together(flat_result, links.expert_parts(out_mine, out_got, (4,)))
     out_keep, out_far = links.expert_far(out_parts)
-    in_mine, in_theirs = in_grad(core, expert_rows, grad_pre)
-    in_theirs, flat_result = together(in_theirs, flat_result)
-    in_got = links.other_core(in_theirs)
     output, grad_logits = combine_results(routes, targets, columns, mid, cotangent, flat_result)
     grad_logits, rows_back = together(grad_logits, rows_back)
     grad_mid, low, grad_attended, d_gain = middle_back(
@@ -1061,32 +1062,27 @@
     rest_mine, rest_theirs = proj_grads(core, attended, low, act_two, grad_logits, d_gain)
     rest_theirs, grad_attended = together(rest_theirs, grad_attended)
     grad_qkv = attention_backward(qkv, attended, logs, grad_attended)
-    grad_qkv, rest_theirs, out_far, in_got = together(grad_qkv, rest_theirs, out_far, in_got)
+    qkv_mine, qkv_theirs = qkv_grads(core, act_one, grad_qkv)
+    qkv_theirs, rest_theirs, grad_qkv, out_far, in_got = together(
+        qkv_theirs, rest_theirs, grad_qkv, out_far, in_got
+    )
     rest_got = links.other_core(rest_theirs)
-    in_parts, grad_qkv = together(links.expert_parts(in_mine, in_got, (1, 2, 1)), grad_qkv)
-    in_keep, in_first = links.expert_far(in_parts[:2])
-    qkv_mine, qkv_theirs = qkv_grads(core, act_one, grad_qkv)
-    qkv_theirs, rest_got, in_first, in_later = together(
-        qkv_theirs, rest_got, in_first, in_parts[2:]
-    )
     qkv_got = links.other_core(qkv_theirs)
-    qkv_parts, grad_qkv, out_keep, in_later = together(
-        links.rows_pick((qkv_mine, qkv_got), (rest_mine, rest_got)), grad_qkv, out_keep, in_later
+    qkv_got, in_parts = together(qkv_got, links.expert_parts(in_mine, in_got, (4,)))
+    qkv_parts, grad_qkv, out_keep, in_parts = together(
+        links.rows_pick((qkv_mine, qkv_got), (rest_mine, rest_got)), grad_qkv, out_keep, in_parts
     )
     qkv_sent = links.rows_send(qkv_parts)
-    _, in_second = links.expert_far([in_keep] + list(in_later[:1]))
+    in_keep, in_far = links.expert_far(in_parts)
     grad_tokens = token_grads(grad_qkv, dense, tokens, grad_mid, table)
     out_pieces = links.expert_pick(out_keep, out_far)
-    qkv_sent, grad_tokens, out_pieces, in_second, in_later = together(
-        qkv_sent, grad_tokens, out_pieces, in_second, in_later
+    qkv_sent, grad_tokens, out_pieces, in_far = together(
+        qkv_sent, grad_tokens, out_pieces, in_far
     )
-    turned, out_pieces, in_keep, in_last = together(
-        links.rows_turn(qkv_sent), out_pieces, in_keep, in_later[1:]
-    )
-    _, in_third = links.expert_far([in_keep] + list(in_last))
+    turned, out_pieces, in_keep = together(links.rows_turn(qkv_sent), out_pieces, in_keep)
     d_dense = links.rows_end(turned)
     d_out = links.expert_end(out_pieces)
-    d_in = links.expert_end(links.expert_pick(in_keep, in_first + in_second + in_third))
+    d_in = links.expert_end(links.expert_pick(in_keep, in_far))
     d_qkv = d_dense[:, : 3 * WIDTH]
     d_rest = d_dense[:, 3 * WIDTH :]
     d_gain_attn = jnp.sum(d_qkv * own_qkv.astype(F32), axis=1) / gain_attn.astype(F32)

time: 474 us -> 448 us (0.945)
  waiting for transfers between devices: 146 us -> 130 us
  local copies, waits for them, and re-layouts: 28.6 us -> 23.3 us
    ppermute x27 -> x25, waiting for transfers between devices: 96.6 us -> 63.1 us  [swap(): return lax.ppermute(value, axis, [(0, 1), (1, 0)])]
    ppermute x24, waiting for transfers between devices: 38.7 us -> 57.2 us  [moved(): lax.ppermute(pieces[k], axes, routes[k])]
    all_to_all x4, starting transfers between devices: 22.7 us -> 16.7 us  [trade(): return lax.all_to_all(value, axes, 0, 0, tiled=True)]
    unnamed x100 -> x86, local copies, waits for them, and re-layouts: 17.4 us -> 12.1 us
    ppermute x27 -> x25, starting transfers between devices: 13.9 us -> 15.2 us  [swap(): return lax.ppermute(value, axis, [(0, 1), (1, 0)])]
  transfers between devices with their start and end apart: 55 -> 53, of which waited for: 20 -> 23; matrix products, arithmetic and copies ran while one was open for 3% -> 3% of each run, Pallas kernels for 43% -> 46%
where the time goes in v4:
time: 448 us; the launch traced here: 445 us
  Pallas kernels  223 us (50%)
  waiting for transfers between devices  130 us (29%)
  starting transfers between devices  63.4 us (14%)
  local copies, waits for them, and re-layouts  23.3 us (5%)
  other arithmetic  4.66 us (1%)
    ppermute x25, waiting for transfers between devices, swap(): return lax.ppermute(value, axis, [(0, 1), (1, 0)])  63.1 us
    ppermute x24, waiting for transfers between devices, moved(): lax.ppermute(pieces[k], axes, routes[k])  57.2 us
    ppermute x24, starting transfers between devices, moved(): lax.ppermute(pieces[k], axes, routes[k])  31.5 us
    pallas_call x6, Pallas kernels, pack(): call('pack', pack_kernel, (parts_of(shape[-1]),), [columns_of(shape[1:])]...  19 us
    pallas_call x1, Pallas kernels, expert_back(): call('expert_back', expert_back_kernel, (count // ROW_BLOCK,), [narrow, w...  18.2 us
    all_to_all x4, starting transfers between devices, trade(): return lax.all_to_all(value, axes, 0, 0, tiled=True)  16.7 us
    pallas_call x1, Pallas kernels, expert_up(): call('expert_up', expert_up_kernel, (depth // F_BLOCK,), [whole(count, WI...  16.3 us
    ppermute x25, starting transfers between devices, swap(): return lax.ppermute(value, axis, [(0, 1), (1, 0)])  15.2 us
  transfers between devices with their start and end apart: 53, of which 23 were waited for; matrix products, arithmetic and copies ran while one was open for 3% of the time, Pallas kernels for 46%

profile of v4, /device:TPU:0, one launch (start us, length us, event | category | flops | bytes accessed | tf_op | source)
XLA Modules:
  0.0 445.3 jit_solution(7673152294882236903)
XLA Ops:
  31.7 11.9 %collective-permute-done.6.refs_1_ = bf16[1,48,3072]{2,1,0:T(8,128)(2,1)S(1)} collective-permute-done((bf16[1,48,3072]{2,1,0:T(8,128)(2,1)S(1)}, bf16[1,48,3072]{2,1,0:T(8,128)(2,1)S(1)}, u32[]{:S(2)}, u32[]{:S(2)}) %collective-permute-start.6) | collective-permute-done | bytes 294944 | tf_op jit(solution)/shard_map/ppermute | solution.py:827
  50.7 10.5 %collective-permute-done.10.refs_2_ = bf16[1,48,3072]{2,1,0:T(8,128)(2,1)S(1)} collective-permute-done((bf16[1,48,3072]{2,1,0:T(8,128)(2,1)}, bf16[1,48,3072]{2,1,0:T(8,128)(2,1)S(1)}, u32[]{:S(2)}, u32[]{:S(2)}) %collective-permute-start.10) | collective-permute-done | bytes 294944 | tf_op jit(solution)/shard_map/ppermute | solution.py:827
  64.2 6.2 %collective-permute-done.13.refs_3_ = bf16[48,3072]{1,0:T(8,128)(2,1)} collective-permute-done((bf16[48,3072]{1,0:T(8,128)(2,1)}, bf16[48,3072]{1,0:T(8,128)(2,1)}, u32[]{:S(2)}, u32[]{:S(2)}) %collective-permute-start.13) | collective-permute-done | bytes 294944 | tf_op jit(solution)/shard_map/ppermute | solution.py:847
  74.4 6.9 %place.1 = bf16[2,4,2,2,24,3200]{5,4,3,2,1,0:T(8,128)(2,1)} custom-call(s32[3]{0:T(128)} %pad_add_fusion.refs_0_, bf16[4,24,3200]{2,1,0:T(8,128)(2,1)} %pack.6.refs_1_, bf16[4,24,3200]{2,1,0:T(8,128)(2,1)} %copy-done.10, bf16[4,24,3200]{2,1,0:T(8,128)(2,1)} %copy-done.8, bf16[4,24,3200]{2,1,0:T(8,128)(2,1)} %copy-done.11, bf16[4,24,3200]{2,1,0:T(8,128)(2,1)} %copy-done.9, ...), custom_call_target="tpu_custom_call" | custom-call | flops 1 | bytes 1 | tf_op jit(solution)/shard_map/place/pallas_call | solution.py:606
  81.4 7.9 %project.1 = (bf16[576,2304]{1,0:T(8,128)(2,1)}, bf16[576,768]{1,0:T(8,128)(2,1)}, bf16[128,768]{1,0:T(8,128)(2,1)}) custom-call(bf16[576,768]{1,0:T(8,128)(2,1)} %tokens_ref.5, bf16[768,3200]{1,0:T(8,128)(2,1)} %bitcast.26, bf16[768,3200]{1,0:T(8,128)(2,1)} %bitcast.27), custom_call_target="tpu_custom_call" | custom-call | flops 1 | bytes 1 | tf_op jit(solution)/shard_map/project/pallas_call | solution.py:176
  90.7 9.4 %collective-permute-done.18.refs_3_ = bf16[192,768]{1,0:T(8,128)(2,1)} collective-permute-done((bf16[192,768]{1,0:T(8,128)(2,1)}, bf16[192,768]{1,0:T(8,128)(2,1)}, u32[]{:S(2)}, u32[]{:S(2)}) %collective-permute-start.18) | collective-permute-done | bytes 294944 | tf_op jit(solution)/shard_map/ppermute | solution.py:847
  111.6 10.4 %attention_forward.1 = (bf16[576,768]{1,0:T(8,128)(2,1)}, f32[1,6,2,576]{3,2,1,0:T(2,128)}) custom-call(bf16[576,2304]{1,0:T(8,128)(2,1)} %get-tuple-element.245.qkv_ref), custom_call_target="tpu_custom_call" | custom-call | flops 1 | bytes 1 | tf_op jit(solution)/shard_map/attention_forward/pallas_call | solution.py:135
  122.1 9.3 %middle.1 = (f32[576,768]{1,0:T(8,128)}, bf16[576,768]{1,0:T(8,128)(2,1)}, f32[576,128]{1,0:T(8,128)}, f32[8,576]{1,0:T(8,128)}, bf16[8,152,768]{2,1,0:T(8,128)(2,1)}) custom-call(s32[2,576]{1,0:T(2,128)} %bitcast.47, s32[2,576]{1,0:T(2,128)} %bitcast.49, bf16[576,768]{1,0:T(8,128)(2,1)} %tokens_ref.5, ...), custom_call_target="tpu_custom_call" | custom-call | flops 1 | bytes 1 | tf_op jit(solution)/shard_map/middle/pallas_call | solution.py:243
  150.4 5.9 %slot_grads.1 = bf16[8,152,768]{2,1,0:T(8,128)(2,1)} custom-call(s32[2,576]{1,0:T(2,128)} %bitcast.48, s32[2,576]{1,0:T(2,128)} %bitcast.50, f32[8,576]{1,0:T(8,128)} %get-tuple-element.257.gates_ref, bf16[576,768]{1,0:T(8,128)(2,1)} %grad_ref.5), custom_call_target="tpu_custom_call" | custom-call | flops 1 | bytes 1 | tf_op jit(solution)/shard_map/slot_grads/pallas_call | solution.py:280
  161.9 6.0 %collective-permute-done.25.refs_4_ = bf16[1,192,768]{2,1,0:T(8,128)(2,1)S(1)} collective-permute-done((bf16[1,192,768]{2,1,0:T(8,128)(2,1)}, bf16[1,192,768]{2,1,0:T(8,128)(2,1)S(1)}, u32[]{:S(2)}, u32[]{:S(2)}) %collective-permute-start.25) | collective-permute-done | bytes 294944 | tf_op jit(solution)/shard_map/ppermute | solution.py:827
  178.9 16.3 %expert_up.1 = (bf16[1216,3072]{1,0:T(8,128)(2,1)}, bf16[1216,3072]{1,0:T(8,128)(2,1)}) custom-call(bf16[1216,768]{1,0:T(8,128)(2,1)} %bitcast.37, bf16[768,3072]{1,0:T(8,128)(2,1)} %bitcast.31), custom_call_target="tpu_custom_call" | custom-call | flops 1 | bytes 1 | tf_op jit(solution)/shard_map/expert_up/pallas_call | solution.py:304
  195.2 8.7 %collective-permute-done.26.refs_5_ = bf16[1,192,768]{2,1,0:T(8,128)(2,1)} collective-permute-done((bf16[1,192,768]{2,1,0:T(8,128)(2,1)}, bf16[1,192,768]{2,1,0:T(8,128)(2,1)}, u32[]{:S(2)}, u32[]{:S(2)}) %collective-permute-start.26) | collective-permute-done | bytes 294944 | tf_op jit(solution)/shard_map/ppermute | solution.py:827
  211.4 10.3 %expert_down.1 = bf16[1216,768]{1,0:T(8,128)(2,1)} custom-call(bf16[1216,3072]{1,0:T(8,128)(2,1)} %get-tuple-element.283.hidden_ref, bf16[3072,768]{1,0:T(8,128)(2,1)} %bitcast.33), custom_call_target="tpu_custom_call" | custom-call | flops 1 | bytes 1 | tf_op jit(solution)/shard_map/expert_down/pallas_call | solution.py:320
  227.3 18.2 %expert_back.1 = (bf16[1216,3072]{1,0:T(8,128)(2,1)}, bf16[1216,768]{1,0:T(8,128)(2,1)}) custom-call(bf16[1216,768]{1,0:T(8,128)(2,1)} %bitcast.35, bf16[1216,3072]{1,0:T(8,128)(2,1)} %get-tuple-element.280.slope_ref, bf16[3072,768]{1,0:T(8,128)(2,1)} %bitcast.34, bf16[768,3072]{1,0:T(8,128)(2,1)} %bitcast.32), custom_call_target="tpu_custom_call" | custom-call | flops 1 | bytes 1 | tf_op jit(solution)/shard_map/expert_back/pallas_call | solution.py:341
  245.5 12.1 %out_grad.1 = (bf16[2,4,192,768]{3,2,1,0:T(8,128)(2,1)}, bf16[2,4,192,768]{3,2,1,0:T(8,128)(2,1)}) custom-call(s32[1]{0:T(128)} %bitcast.4.me_ref, bf16[1216,3072]{1,0:T(8,128)(2,1)} %get-tuple-element.283.hidden_ref, bf16[1216,768]{1,0:T(8,128)(2,1)} %bitcast.36), custom_call_target="tpu_custom_call" | custom-call | flops 1 | bytes 1 | tf_op jit(solution)/shard_map/out_grad/pallas_call | solution.py:363
  262.6 11.5 %in_grad.1 = (bf16[2,4,48,3072]{3,2,1,0:T(8,128)(2,1)}, bf16[2,4,48,3072]{3,2,1,0:T(8,128)(2,1)}) custom-call(s32[1]{0:T(128)} %bitcast.4.me_ref, bf16[1216,768]{1,0:T(8,128)(2,1)} %bitcast.38, bf16[1216,3072]{1,0:T(8,128)(2,1)} %get-tuple-element.287.grad_ref), custom_call_target="tpu_custom_call" | custom-call | flops 1 | bytes 1 | tf_op jit(solution)/shard_map/in_grad/pallas_call | solution.py:391
  286.1 7.1 %combine.1 = (bf16[576,768]{1,0:T(8,128)(2,1)}, bf16[576,128]{1,0:T(8,128)(2,1)}) custom-call(s32[576,2]{1,0:T(8,128)} %copy.51.routes_ref, s32[576,2]{1,0:T(8,128)} %add_select_fusion.targets_ref, f32[576,128]{1,0:T(8,128)} %get-tuple-element.248.columns_ref, f32[576,768]{1,0:T(8,128)} %get-tuple-element.249.mid_ref, bf16[576,768]{1,0:T(8,128)(2,1)} %grad_ref.5, ...), custom_call_target="tpu_custom_call" | custom-call | flops 1 | bytes 1 | tf_op jit(solution)/shard_map/combine/pallas_call | solution.py:432
  299.9 7.6 %middle_back.1 = (f32[576,768]{1,0:T(8,128)}, bf16[576,768]{1,0:T(8,128)(2,1)}, bf16[576,768]{1,0:T(8,128)(2,1)}, f32[8,768]{1,0:T(8,128)}) custom-call(s32[576,2]{1,0:T(8,128)} %add_select_fusion.targets_ref, bf16[576,128]{1,0:T(8,128)(2,1)} %get-tuple-element.299.logits_ref, f32[576,768]{1,0:T(8,128)} %get-tuple-element.249.mid_ref, ...), custom_call_target="tpu_custom_call" | custom-call | flops 1 | bytes 1 | tf_op jit(solution)/shard_map/middle_back/pallas_call | solution.py:474
  311.7 14.4 %attention_backward.1.grad_ref = bf16[576,2304]{1,0:T(8,128)(2,1)} custom-call(bf16[576,2304]{1,0:T(8,128)(2,1)} %get-tuple-element.245.qkv_ref, bf16[576,768]{1,0:T(8,128)(2,1)} %get-tuple-element.246.attended_ref.out_ref, f32[1,6,2,576]{3,2,1,0:T(2,128)} %get-tuple-element.296.log_ref, bf16[576,768]{1,0:T(8,128)(2,1)} %get-tuple-element.306.grad_ref), custom_call_target="tpu_custom_call" | custom-call | flops 1 | bytes 1 | tf_op jit(solution)/shard_map/attention_backward/pallas_call | solution.py:147
  326.1 7.9 %qkv_grads.1 = (bf16[2,2,4,24,2304]{4,3,2,1,0:T(8,128)(2,1)}, bf16[2,2,4,24,2304]{4,3,2,1,0:T(8,128)(2,1)}) custom-call(s32[1]{0:T(128)} %bitcast.4.me_ref, bf16[576,768]{1,0:T(8,128)(2,1)} %get-tuple-element.295.act_ref, bf16[576,2304]{1,0:T(8,128)(2,1)} %attention_backward.1.grad_ref), custom_call_target="tpu_custom_call" | custom-call | flops 1 | bytes 1 | tf_op jit(solution)/shard_map/qkv_grads/pallas_call | solution.py:543
  351.9 8.1 %token_grads.1 = f32[576,768]{1,0:T(8,128)} custom-call(bf16[576,2304]{1,0:T(8,128)(2,1)} %attention_backward.1.grad_ref, bf16[768,3200]{1,0:T(8,128)(2,1)} %bitcast.30, bf16[576,768]{1,0:T(8,128)(2,1)} %tokens_ref.5, f32[576,768]{1,0:T(8,128)} %get-tuple-element.333.grad_mid_ref, bf16[128,768]{1,0:T(8,128)(2,1)} %get-tuple-element.247.table_ref), custom_call_target="tpu_custom_call" | custom-call | flops 1 | bytes 1 | tf_op jit(solution)/shard_map/token_grads/pallas_call | solution.py:564
  363.5 11.8 %collective-permute-done.38.refs_3_ = bf16[96,3200]{1,0:T(8,128)(2,1)S(1)} collective-permute-done((bf16[96,3200]{1,0:T(8,128)(2,1)}, bf16[96,3200]{1,0:T(8,128)(2,1)S(1)}, u32[]{:S(2)}, u32[]{:S(2)}) %collective-permute-start.38) | collective-permute-done | bytes 614432 | tf_op jit(solution)/shard_map/ppermute | solution.py:847
  375.3 23.5 %collective-permute-done.39.refs_0_ = bf16[4,48,3072]{2,1,0:T(8,128)(2,1)S(1)} collective-permute-done((bf16[4,48,3072]{2,1,0:T(8,128)(2,1)}, bf16[4,48,3072]{2,1,0:T(8,128)(2,1)S(1)}, u32[]{:S(2)}, u32[]{:S(2)}) %collective-permute-start.39) | collective-permute-done | bytes 1179680 | tf_op jit(solution)/shard_map/ppermute | solution.py:827
  435.0 6.1 %collective-permute-done.45.refs_3_ = bf16[48,3072]{1,0:T(8,128)(2,1)S(1)} collective-permute-done((bf16[48,3072]{1,0:T(8,128)(2,1)S(1)}, bf16[48,3072]{1,0:T(8,128)(2,1)S(1)}, u32[]{:S(2)}, u32[]{:S(2)}) %collective-permute-start.45) | collective-permute-done | bytes 294944 | tf_op jit(solution)/shard_map/ppermute | solution.py:847
  (229 shorter events, 196.4 us)
Async XLA Ops:
  25.3 18.3 %collective-permute-start.4 = (bf16[4,24,3200]{2,1,0:T(8,128)(2,1)}, bf16[4,24,3200]{2,1,0:T(8,128)(2,1)S(1)}, u32[]{:S(2)}, u32[]{:S(2)}) collective-permute-start(bf16[4,24,3200]{2,1,0:T(8,128)(2,1)} %pack.6.refs_1_), channel_id=1, source_target_pairs={{0,2},{2,0},{1,3},{3,1},{4,6},{6,4},{5,7},{7,5},{8,10},{10,8},{9,1... | collective-permute-start | bytes 1843208 | tf_op jit(solution)/shard_map/ppermute | solution.py:827
  47.7 22.6 %collective-permute-start.13 = (bf16[48,3072]{1,0:T(8,128)(2,1)}, bf16[48,3072]{1,0:T(8,128)(2,1)}, u32[]{:S(2)}, u32[]{:S(2)}) collective-permute-start(bf16[48,3072]{1,0:T(8,128)(2,1)} %get-tuple-element.219), channel_id=1, source_target_pairs={{0,6},{2,4},{4,2},{6,0},{1,7},{3,5},{5,3},{7,1},{8,14},{10,12},{12... | collective-permute-start | bytes 884744 | tf_op jit(solution)/shard_map/ppermute | solution.py:847
  70.3 29.9 %collective-permute-start.15 = (bf16[2,48,3072]{2,1,0:T(8,128)(2,1)}, bf16[2,48,3072]{2,1,0:T(8,128)(2,1)}, u32[]{:S(2)}, u32[]{:S(2)}) collective-permute-start(bf16[2,48,3072]{2,1,0:T(8,128)(2,1)} %slice.36), channel_id=1, source_target_pairs={{0,8},{8,0},{1,9},{9,1},{2,10},{10,2},{3,11},{11,3},{4,12},{12,4},... | collective-permute-start | bytes 1769480 | tf_op jit(solution)/shard_map/ppermute | solution.py:827
  70.3 19.0 %collective-permute-start.16 = (bf16[192,768]{1,0:T(8,128)(2,1)}, bf16[192,768]{1,0:T(8,128)(2,1)}, u32[]{:S(2)}, u32[]{:S(2)}) collective-permute-start(bf16[192,768]{1,0:T(8,128)(2,1)} %get-tuple-element.230), channel_id=1, source_target_pairs={{0,2},{2,0},{4,6},{6,4},{1,3},{3,1},{5,7},{7,5},{8,10},{10,8},{12,... | collective-permute-start | bytes 884744 | tf_op jit(solution)/shard_map/ppermute | solution.py:847
  70.8 19.9 %collective-permute-start.17 = (bf16[192,768]{1,0:T(8,128)(2,1)}, bf16[192,768]{1,0:T(8,128)(2,1)}, u32[]{:S(2)}, u32[]{:S(2)}) collective-permute-start(bf16[192,768]{1,0:T(8,128)(2,1)} %get-tuple-element.231), channel_id=1, source_target_pairs={{0,4},{2,6},{4,0},{6,2},{1,5},{3,7},{5,1},{7,3},{8,12},{10,14},{12... | collective-permute-start | bytes 884744 | tf_op jit(solution)/shard_map/ppermute | solution.py:847
  71.4 28.8 %collective-permute-start.18 = (bf16[192,768]{1,0:T(8,128)(2,1)}, bf16[192,768]{1,0:T(8,128)(2,1)}, u32[]{:S(2)}, u32[]{:S(2)}) collective-permute-start(bf16[192,768]{1,0:T(8,128)(2,1)} %get-tuple-element.232), channel_id=1, source_target_pairs={{0,6},{2,4},{4,2},{6,0},{1,7},{3,5},{5,3},{7,1},{8,14},{10,12},{12... | collective-permute-start | bytes 884744 | tf_op jit(solution)/shard_map/ppermute | solution.py:847
  108.0 28.5 %collective-permute-start.22 = (bf16[2,192,768]{2,1,0:T(8,128)(2,1)S(1)}, bf16[2,192,768]{2,1,0:T(8,128)(2,1)S(1)}, u32[]{:S(2)}, u32[]{:S(2)}) collective-permute-start(bf16[2,192,768]{2,1,0:T(8,128)(2,1)S(1)} %slice.37), channel_id=1, source_target_pairs={{0,8},{8,0},{1,9},{9,1},{2,10},{10,2},{3,11},{11,3},{4,12},{12,4},... | collective-permute-start | bytes 1769480 | tf_op jit(solution)/shard_map/ppermute | solution.py:827
  108.1 23.3 %collective-permute-start.19 = (bf16[48,3072]{1,0:T(8,128)(2,1)S(1)}, bf16[48,3072]{1,0:T(8,128)(2,1)S(1)}, u32[]{:S(2)}, u32[]{:S(2)}) collective-permute-start(bf16[48,3072]{1,0:T(8,128)(2,1)S(1)} %copy-done.40), channel_id=1, source_target_pairs={{0,2},{2,0},{4,6},{6,4},{1,3},{3,1},{5,7},{7,5},{8,10},{10,8},{12,... | collective-permute-start | bytes 884744 | tf_op jit(solution)/shard_map/ppermute | solution.py:847
  108.7 22.7 %collective-permute-start.20 = (bf16[48,3072]{1,0:T(8,128)(2,1)S(1)}, bf16[48,3072]{1,0:T(8,128)(2,1)S(1)}, u32[]{:S(2)}, u32[]{:S(2)}) collective-permute-start(bf16[48,3072]{1,0:T(8,128)(2,1)S(1)} %copy-done.39), channel_id=1, source_target_pairs={{0,4},{2,6},{4,0},{6,2},{1,5},{3,7},{5,1},{7,3},{8,12},{10,14},{12... | collective-permute-start | bytes 884744 | tf_op jit(solution)/shard_map/ppermute | solution.py:847
  110.2 26.3 %collective-permute-start.21 = (bf16[48,3072]{1,0:T(8,128)(2,1)S(1)}, bf16[48,3072]{1,0:T(8,128)(2,1)S(1)}, u32[]{:S(2)}, u32[]{:S(2)}) collective-permute-start(bf16[48,3072]{1,0:T(8,128)(2,1)S(1)} %copy-done.38), channel_id=1, source_target_pairs={{0,6},{2,4},{4,2},{6,0},{1,7},{3,5},{5,3},{7,1},{8,14},{10,12},{12... | collective-permute-start | bytes 884744 | tf_op jit(solution)/shard_map/ppermute | solution.py:847
  137.4 35.1 %all-to-all-start = ((bf16[8,152,768]{2,1,0:T(8,128)(2,1)}), bf16[8,152,768]{2,1,0:T(8,128)(2,1)S(1)}, u32[]{:S(2)}, u32[]{:S(2)}) async-start(bf16[8,152,768]{2,1,0:T(8,128)(2,1)} %get-tuple-element.258), calls=%async_computation | async-start | bytes 3735552 | tf_op jit(solution)/shard_map/all_to_all | solution.py:830
  148.8 19.1 %collective-permute-start.25 = (bf16[1,192,768]{2,1,0:T(8,128)(2,1)}, bf16[1,192,768]{2,1,0:T(8,128)(2,1)S(1)}, u32[]{:S(2)}, u32[]{:S(2)}) collective-permute-start(bf16[1,192,768]{2,1,0:T(8,128)(2,1)} %slice.38), channel_id=1, source_target_pairs={{0,8},{8,0},{1,9},{9,1},{2,10},{10,2},{3,11},{11,3},{4,12},{12,4},... | collective-permute-start | bytes 884744 | tf_op jit(solution)/shard_map/ppermute | solution.py:827
  173.8 47.9 %all-to-all-start.1 = ((bf16[8,152,768]{2,1,0:T(8,128)(2,1)}), bf16[8,152,768]{2,1,0:T(8,128)(2,1)S(1)}, u32[]{:S(2)}, u32[]{:S(2)}) async-start(bf16[8,152,768]{2,1,0:T(8,128)(2,1)} %slot_grads.1), calls=%async_computation.1 | async-start | bytes 3735552 | tf_op jit(solution)/shard_map/all_to_all | solution.py:830
  177.5 28.3 %collective-permute-start.27 = (bf16[4,192,768]{2,1,0:T(8,128)(2,1)S(1)}, bf16[4,192,768]{2,1,0:T(8,128)(2,1)}, u32[]{:S(2)}, u32[]{:S(2)}) collective-permute-start(bf16[4,192,768]{2,1,0:T(8,128)(2,1)S(1)} %copy-done.2), channel_id=1, source_target_pairs={{0,1},{1,0},{2,3},{3,2},{4,5},{5,4},{6,7},{7,6},{8,9},{9,8},{10,11... | collective-permute-start | bytes 3538952 | tf_op jit(solution)/shard_map/ppermute | solution.py:827
  178.4 25.5 %collective-permute-start.26 = (bf16[1,192,768]{2,1,0:T(8,128)(2,1)}, bf16[1,192,768]{2,1,0:T(8,128)(2,1)}, u32[]{:S(2)}, u32[]{:S(2)}) collective-permute-start(bf16[1,192,768]{2,1,0:T(8,128)(2,1)} %slice.39), channel_id=1, source_target_pairs={{0,8},{8,0},{1,9},{9,1},{2,10},{10,2},{3,11},{11,3},{4,12},{12,4},... | collective-permute-start | bytes 884744 | tf_op jit(solution)/shard_map/ppermute | solution.py:827
  178.4 25.5 %collective-permute-start.28 = (bf16[2,192,768]{2,1,0:T(8,128)(2,1)}, bf16[2,192,768]{2,1,0:T(8,128)(2,1)}, u32[]{:S(2)}, u32[]{:S(2)}) collective-permute-start(bf16[2,192,768]{2,1,0:T(8,128)(2,1)} %copy-done.17), channel_id=1, source_target_pairs={{0,1},{1,0},{2,3},{3,2},{4,5},{5,4},{6,7},{7,6},{8,9},{9,8},{10,11... | collective-permute-start | bytes 1769480 | tf_op jit(solution)/shard_map/ppermute | solution.py:827
  178.9 25.0 %collective-permute-start.29 = (bf16[1,192,768]{2,1,0:T(8,128)(2,1)S(1)}, bf16[1,192,768]{2,1,0:T(8,128)(2,1)}, u32[]{:S(2)}, u32[]{:S(2)}) collective-permute-start(bf16[1,192,768]{2,1,0:T(8,128)(2,1)S(1)} %collective-permute-done.25.refs_4_), channel_id=1, source_target_pairs={{0,1},{1,0},{2,3},{3,2},{4,5},{5,4},{6,7},{7,6},{8,9},{9,8},{10,11... | collective-permute-start | bytes 884744 | tf_op jit(solution)/shard_map/ppermute | solution.py:827
  222.9 34.7 %all-to-all-start.2 = ((bf16[8,152,768]{2,1,0:T(8,128)(2,1)}), bf16[8,152,768]{2,1,0:T(8,128)(2,1)}, u32[]{:S(2)}, u32[]{:S(2)}) async-start(bf16[8,152,768]{2,1,0:T(8,128)(2,1)} %bitcast.40), calls=%async_computation.2 | async-start | bytes 3735552 | tf_op jit(solution)/shard_map/all_to_all | solution.py:830
  257.7 40.9 %all-to-all-start.3 = ((bf16[8,152,768]{2,1,0:T(8,128)(2,1)}), bf16[8,152,768]{2,1,0:T(8,128)(2,1)S(1)}, u32[]{:S(2)}, u32[]{:S(2)}) async-start(bf16[8,152,768]{2,1,0:T(8,128)(2,1)} %bitcast.41), calls=%async_computation.3 | async-start | bytes 3735552 | tf_op jit(solution)/shard_map/all_to_all | solution.py:830
  274.1 60.1 %collective-permute-start.33 = (bf16[2,4,48,3072]{3,2,1,0:T(8,128)(2,1)}, bf16[2,4,48,3072]{3,2,1,0:T(8,128)(2,1)}, u32[]{:S(2)}, u32[]{:S(2)}) collective-permute-start(bf16[2,4,48,3072]{3,2,1,0:T(8,128)(2,1)} %get-tuple-element.311), channel_id=1, source_target_pairs={{0,1},{1,0},{2,3},{3,2},{4,5},{5,4},{6,7},{7,6},{8,9},{9,8},{10,11... | collective-permute-start | bytes 7077896 | tf_op jit(solution)/shard_map/ppermute | solution.py:827
  278.9 55.3 %collective-permute-start.32 = (bf16[4,192,768]{2,1,0:T(8,128)(2,1)}, bf16[4,192,768]{2,1,0:T(8,128)(2,1)S(1)}, u32[]{:S(2)}, u32[]{:S(2)}) collective-permute-start(bf16[4,192,768]{2,1,0:T(8,128)(2,1)} %get-tuple-element.310), channel_id=1, source_target_pairs={{0,8},{8,0},{1,9},{9,1},{2,10},{10,2},{3,11},{11,3},{4,12},{12,4},... | collective-permute-start | bytes 3538952 | tf_op jit(solution)/shard_map/ppermute | solution.py:827
  344.5 54.3 %collective-permute-start.39 = (bf16[4,48,3072]{2,1,0:T(8,128)(2,1)}, bf16[4,48,3072]{2,1,0:T(8,128)(2,1)S(1)}, u32[]{:S(2)}, u32[]{:S(2)}) collective-permute-start(bf16[4,48,3072]{2,1,0:T(8,128)(2,1)} %get-tuple-element.340), channel_id=1, source_target_pairs={{0,8},{8,0},{1,9},{9,1},{2,10},{10,2},{3,11},{11,3},{4,12},{12,4},... | collective-permute-start | bytes 3538952 | tf_op jit(solution)/shard_map/ppermute | solution.py:827
  348.0 27.3 %collective-permute-start.38 = (bf16[96,3200]{1,0:T(8,128)(2,1)}, bf16[96,3200]{1,0:T(8,128)(2,1)S(1)}, u32[]{:S(2)}, u32[]{:S(2)}) collective-permute-start(bf16[96,3200]{1,0:T(8,128)(2,1)} %get-tuple-element.331), channel_id=1, source_target_pairs={{0,18},{2,16},{16,2},{18,0},{1,19},{3,17},{17,3},{19,1},{4,22},{6,... | collective-permute-start | bytes 1843208 | tf_op jit(solution)/shard_map/ppermute | solution.py:847
  421.7 19.4 %collective-permute-start.45 = (bf16[48,3072]{1,0:T(8,128)(2,1)S(1)}, bf16[48,3072]{1,0:T(8,128)(2,1)S(1)}, u32[]{:S(2)}, u32[]{:S(2)}) collective-permute-start(bf16[48,3072]{1,0:T(8,128)(2,1)S(1)} %copy-done.37), channel_id=1, source_target_pairs={{0,6},{2,4},{4,2},{6,0},{1,7},{3,5},{5,3},{7,1},{8,14},{10,12},{12... | collective-permute-start | bytes 884744 | tf_op jit(solution)/shard_map/ppermute | solution.py:847
  (70 other events, 807.3 us)

commit v5 on v4

--- a/solution.py
+++ b/solution.py
@@ -847,36 +847,31 @@
         return [pieces[0]] + [lax.ppermute(pieces[k], axes, routes[k]) for k in range(1, count)]
 
     def gather(self, dense, w_in, w_out):
-        near = self.number("zl", "y")
+        near = ("zl", "y")
         own = pack(self.number("zh", "zl"), self.moved([dense] * 4, "zh", "zl"))
-        in_parts, out_parts = pick(near, w_in), pick(near, w_out)
-        own, first, second, third, in_parts, out_parts = together(
-            own, w_in[:1], w_in[1:2], w_in[2:], in_parts, out_parts
+        own, first, second, third, w_in, w_out = together(
+            own, w_in[:1], w_in[1:3], w_in[3:], w_in, w_out
         )
-        over_y, over_x, first, second, third, in_parts = together(
-            self.swap(own, "y"), self.swap(own, "x"), self.swap(first, "zh"), second, third, in_parts
+        over_y, over_x, first, second, third, w_in = together(
+            self.swap(own, "y"), self.swap(own, "x"), self.swap(first, "zh"), second, third, w_in
         )
         firsts = [own, over_y, over_x]
         over_xy = self.swap(over_y, "x")
         second = self.swap(second, "zh")
-        theirs, in_parts = together([self.swap(value, "c") for value in firsts], in_parts)
-        in_near = self.moved(in_parts, "zl", "y")
-        over_xy, second, third, in_near, out_parts = together(
-            over_xy, second, third, in_near, out_parts
-        )
+        in_near = self.trade(w_in, near)
+        theirs = [self.swap(value, "c") for value in firsts]
+        over_xy, second, third, in_near, w_out = together(over_xy, second, third, in_near, w_out)
         pieces = [value for pair in zip(firsts, theirs) for value in pair]
         pieces += [over_xy, self.swap(over_xy, "c")]
         third = self.swap(third, "zh")
-        out_near = self.moved(out_parts, "zl", "y")
+        out_near = self.trade(w_out, near)
         full = place(self.place_of("x", "y", "c"), pieces, (0, 2, 3))
         full = full.reshape(32 * dense.shape[0], dense.shape[1])
         return full, {"in_near": in_near, "in_far": [first, second, third], "out_near": out_near}
 
     def after_project(self, kept, value):
-        near = self.number("zl", "y")
         value, far, out_near = together(value, kept["in_far"], kept["out_near"])
-        value, far, out_near = together(value, pick(near, *far), pack(near, out_near))
-        kept["in_far"] = self.moved(far, "zl", "y")
+        kept["in_far"] = self.trade(jnp.concatenate(far, axis=0), ("zl", "y"))
         kept["out_near"] = out_near
         kept["out_far"] = [self.swap(out_near[:2], "zh")]
         return value
@@ -900,8 +895,7 @@
         return join(self.place_of("zh", "c"), near, self.swap(near, "c"), far, cores)
 
     def expert_in(self, kept):
-        near = self.number("zl", "y")
-        return self.joined(pack(near, kept["in_near"]), [pack(near, kept["in_far"])])
+        return self.joined(kept["in_near"], [kept["in_far"]])
 
     def expert_out(self, kept, *values):
         *values, last = together(*values, kept["out_far"][2])
@@ -1060,29 +1054,33 @@
         targets, grad_logits, mid, cotangent, rows_back, dense, table
     )
     rest_mine, rest_theirs = proj_grads(core, attended, low, act_two, grad_logits, d_gain)
-    rest_theirs, grad_attended = together(rest_theirs, grad_attended)
+    rest_theirs, grad_attended, in_got = together(rest_theirs, grad_attended, in_got)
+    in_parts, grad_attended = together(
+        links.expert_parts(in_mine, in_got, (1, 3)), grad_attended
+    )
     grad_qkv = attention_backward(qkv, attended, logs, grad_attended)
     qkv_mine, qkv_theirs = qkv_grads(core, act_one, grad_qkv)
-    qkv_theirs, rest_theirs, grad_qkv, out_far, in_got = together(
-        qkv_theirs, rest_theirs, grad_qkv, out_far, in_got
+    qkv_theirs, rest_theirs, grad_qkv, out_far, in_parts = together(
+        qkv_theirs, rest_theirs, grad_qkv, out_far, in_parts
     )
+    in_keep, in_first = links.expert_far(in_parts[:2])
     rest_got = links.other_core(rest_theirs)
     qkv_got = links.other_core(qkv_theirs)
-    qkv_got, in_parts = together(qkv_got, links.expert_parts(in_mine, in_got, (4,)))
-    qkv_parts, grad_qkv, out_keep, in_parts = together(
-        links.rows_pick((qkv_mine, qkv_got), (rest_mine, rest_got)), grad_qkv, out_keep, in_parts
+    qkv_got, rest_got, in_first, in_later = together(qkv_got, rest_got, in_first, in_parts[2:])
+    qkv_parts, grad_qkv, out_keep, in_later = together(
+        links.rows_pick((qkv_mine, qkv_got), (rest_mine, rest_got)), grad_qkv, out_keep, in_later
     )
     qkv_sent = links.rows_send(qkv_parts)
-    in_keep, in_far = links.expert_far(in_parts)
+    _, in_second = links.expert_far([in_keep] + list(in_later))
     grad_tokens = token_grads(grad_qkv, dense, tokens, grad_mid, table)
     out_pieces = links.expert_pick(out_keep, out_far)
-    qkv_sent, grad_tokens, out_pieces, in_far = together(
-        qkv_sent, grad_tokens, out_pieces, in_far
+    qkv_sent, grad_tokens, out_pieces = together(qkv_sent, grad_tokens, out_pieces)
+    turned, out_pieces, in_keep, in_second = together(
+        links.rows_turn(qkv_sent), out_pieces, in_keep, in_second
     )
-    turned, out_pieces, in_keep = together(links.rows_turn(qkv_sent), out_pieces, in_keep)
     d_dense = links.rows_end(turned)
     d_out = links.expert_end(out_pieces)
-    d_in = links.expert_end(links.expert_pick(in_keep, in_far))
+    d_in = links.expert_end(links.expert_pick(in_keep, in_first + in_second))
     d_qkv = d_dense[:, : 3 * WIDTH]
     d_rest = d_dense[:, 3 * WIDTH :]
     d_gain_attn = jnp.sum(d_qkv * own_qkv.astype(F32), axis=1) / gain_attn.astype(F32)

time: 448 us -> 442 us (0.987)
  Pallas kernels: 223 us -> 202 us
  waiting for transfers between devices: 130 us -> 139 us
    ppermute x25 -> x26, waiting for transfers between devices: 63.1 us -> 89.2 us  [swap(): return lax.ppermute(value, axis, [(0, 1), (1, 0)])]
    ppermute x24 -> x15, waiting for transfers between devices: 57.2 us -> 39.3 us  [moved(): lax.ppermute(pieces[k], axes, routes[k])]
    ppermute x24 -> x15, starting transfers between devices: 31.5 us -> 18.6 us  [moved(): lax.ppermute(pieces[k], axes, routes[k])]
    all_to_all x4 -> x7, starting transfers between devices: 16.7 us -> 28.9 us  [trade(): return lax.all_to_all(value, axes, 0, 0, tiled=True)]
    pallas_call x6 -> x3, Pallas kernels: 19 us -> 9.08 us  [pack(): call('pack', pack_kernel, (parts_of(shape[-1]),), [columns_of(shape[1:])]...]
    pallas_call x3 -> x0, Pallas kernels: 9.87 us -> none  [pick(): call('pick', lambda *refs: pick_kernel(count, *refs), (parts_of(shape[-1]...]
    ppermute x25 -> x26, starting transfers between devices: 15.2 us -> 18.7 us  [swap(): return lax.ppermute(value, axis, [(0, 1), (1, 0)])]
    unnamed x86 -> x72, local copies, waits for them, and re-layouts: 12.1 us -> 12.8 us
  transfers between devices with their start and end apart: 53 -> 48, of which waited for: 23 -> 22; matrix products, arithmetic and copies ran while one was open for 3% -> 3% of each run, Pallas kernels for 46% -> 44%
where the time goes in v5:
time: 442 us; the launch traced here: 440 us
  Pallas kernels  202 us (46%)
  waiting for transfers between devices  139 us (31%)
  starting transfers between devices  66.2 us (15%)
  local copies, waits for them, and re-layouts  24.8 us (6%)
  other arithmetic  6.9 us (2%)
    ppermute x26, waiting for transfers between devices, swap(): return lax.ppermute(value, axis, [(0, 1), (1, 0)])  89.2 us
    ppermute x15, waiting for transfers between devices, moved(): lax.ppermute(pieces[k], axes, routes[k])  39.3 us
    all_to_all x7, starting transfers between devices, trade(): return lax.all_to_all(value, axes, 0, 0, tiled=True)  28.9 us
    ppermute x26, starting transfers between devices, swap(): return lax.ppermute(value, axis, [(0, 1), (1, 0)])  18.7 us
    ppermute x15, starting transfers between devices, moved(): lax.ppermute(pieces[k], axes, routes[k])  18.6 us
    pallas_call x1, Pallas kernels, expert_back(): call('expert_back', expert_back_kernel, (count // ROW_BLOCK,), [narrow, w...  18.2 us
    pallas_call x1, Pallas kernels, expert_up(): call('expert_up', expert_up_kernel, (depth // F_BLOCK,), [whole(count, WI...  16.3 us
    pallas_call x1, Pallas kernels, attention_backward(): call('attention_backward', attention_back_kernel, (qkv.shape[0] // SEQ, P...  14.3 us
  transfers between devices with their start and end apart: 48, of which 22 were waited for; matrix products, arithmetic and copies ran while one was open for 3% of the time, Pallas kernels for 44%

profile of v5, /device:TPU:0, one launch (start us, length us, event | category | flops | bytes accessed | tf_op | source)
XLA Modules:
  0.0 439.6 jit_solution(17628809985604975421)
XLA Ops:
  14.4 8.0 %collective-permute-done.1.refs_2_ = bf16[24,3200]{1,0:T(8,128)(2,1)S(1)} collective-permute-done((bf16[24,3200]{1,0:T(8,128)(2,1)S(1)}, bf16[24,3200]{1,0:T(8,128)(2,1)S(1)}, u32[]{:S(2)}, u32[]{:S(2)}) %collective-permute-start.1) | collective-permute-done | bytes 153632 | tf_op jit(solution)/shard_map/ppermute | solution.py:847
  31.6 11.9 %collective-permute-done.6 = bf16[1,48,3072]{2,1,0:T(8,128)(2,1)S(1)} collective-permute-done((bf16[1,48,3072]{2,1,0:T(8,128)(2,1)S(1)}, bf16[1,48,3072]{2,1,0:T(8,128)(2,1)S(1)}, u32[]{:S(2)}, u32[]{:S(2)}) %collective-permute-start.6) | collective-permute-done | bytes 294944 | tf_op jit(solution)/shard_map/ppermute | solution.py:827
  49.9 25.7 %collective-permute-done.10 = bf16[2,48,3072]{2,1,0:T(8,128)(2,1)S(1)} collective-permute-done((bf16[2,48,3072]{2,1,0:T(8,128)(2,1)}, bf16[2,48,3072]{2,1,0:T(8,128)(2,1)S(1)}, u32[]{:S(2)}, u32[]{:S(2)}) %collective-permute-start.10) | collective-permute-done | bytes 589856 | tf_op jit(solution)/shard_map/ppermute | solution.py:827
  85.9 7.0 %place.1 = bf16[2,4,2,2,24,3200]{5,4,3,2,1,0:T(8,128)(2,1)} custom-call(s32[3]{0:T(128)} %pad_add_fusion.refs_0_, bf16[4,24,3200]{2,1,0:T(8,128)(2,1)} %pack.3.refs_1_, bf16[4,24,3200]{2,1,0:T(8,128)(2,1)} %collective-permute-done.3.refs_2_, bf16[4,24,3200]{2,1,0:T(8,128)(2,1)} %copy-done.10, bf16[4,24,3200]{2,1,0:T(8,128)(2,1)} %collective-permute-done.7.refs_4_, ...), custom_call_target="tpu_custom_call" | custom-call | flops 1 | bytes 1 | tf_op jit(solution)/shard_map/place/pallas_call | solution.py:606
  92.9 8.0 %project.1 = (bf16[576,2304]{1,0:T(8,128)(2,1)}, bf16[576,768]{1,0:T(8,128)(2,1)}, bf16[128,768]{1,0:T(8,128)(2,1)}) custom-call(bf16[576,768]{1,0:T(8,128)(2,1)} %tokens_ref.5, bf16[768,3200]{1,0:T(8,128)(2,1)} %bitcast.26, bf16[768,3200]{1,0:T(8,128)(2,1)} %bitcast.27), custom_call_target="tpu_custom_call" | custom-call | flops 1 | bytes 1 | tf_op jit(solution)/shard_map/project/pallas_call | solution.py:176
  109.3 10.4 %attention_forward.1 = (bf16[576,768]{1,0:T(8,128)(2,1)}, f32[1,6,2,576]{3,2,1,0:T(2,128)}) custom-call(bf16[576,2304]{1,0:T(8,128)(2,1)} %get-tuple-element.168.qkv_ref), custom_call_target="tpu_custom_call" | custom-call | flops 1 | bytes 1 | tf_op jit(solution)/shard_map/attention_forward/pallas_call | solution.py:135
  119.8 9.3 %middle.1 = (f32[576,768]{1,0:T(8,128)}, bf16[576,768]{1,0:T(8,128)(2,1)}, f32[576,128]{1,0:T(8,128)}, f32[8,576]{1,0:T(8,128)}, bf16[8,152,768]{2,1,0:T(8,128)(2,1)}) custom-call(s32[2,576]{1,0:T(2,128)} %bitcast.47, s32[2,576]{1,0:T(2,128)} %bitcast.49, bf16[576,768]{1,0:T(8,128)(2,1)} %tokens_ref.5, ...), custom_call_target="tpu_custom_call" | custom-call | flops 1 | bytes 1 | tf_op jit(solution)/shard_map/middle/pallas_call | solution.py:243
  129.1 8.0 %collective-permute-done.13.refs_3_ = bf16[2,192,768]{2,1,0:T(8,128)(2,1)S(1)} collective-permute-done((bf16[2,192,768]{2,1,0:T(8,128)(2,1)}, bf16[2,192,768]{2,1,0:T(8,128)(2,1)S(1)}, u32[]{:S(2)}, u32[]{:S(2)}) %collective-permute-start.13) | collective-permute-done | bytes 589856 | tf_op jit(solution)/shard_map/ppermute | solution.py:827
  145.6 5.9 %slot_grads.1 = bf16[8,152,768]{2,1,0:T(8,128)(2,1)} custom-call(s32[2,576]{1,0:T(2,128)} %bitcast.48, s32[2,576]{1,0:T(2,128)} %bitcast.50, f32[8,576]{1,0:T(8,128)} %get-tuple-element.179.gates_ref, bf16[576,768]{1,0:T(8,128)(2,1)} %grad_ref.5), custom_call_target="tpu_custom_call" | custom-call | flops 1 | bytes 1 | tf_op jit(solution)/shard_map/slot_grads/pallas_call | solution.py:280
  157.1 11.3 %collective-permute-done.16.refs_4_ = bf16[1,192,768]{2,1,0:T(8,128)(2,1)S(1)} collective-permute-done((bf16[1,192,768]{2,1,0:T(8,128)(2,1)}, bf16[1,192,768]{2,1,0:T(8,128)(2,1)S(1)}, u32[]{:S(2)}, u32[]{:S(2)}) %collective-permute-start.16) | collective-permute-done | bytes 294944 | tf_op jit(solution)/shard_map/ppermute | solution.py:827
  178.6 16.3 %expert_up.1 = (bf16[1216,3072]{1,0:T(8,128)(2,1)}, bf16[1216,3072]{1,0:T(8,128)(2,1)}) custom-call(bf16[1216,768]{1,0:T(8,128)(2,1)} %bitcast.37, bf16[768,3072]{1,0:T(8,128)(2,1)} %bitcast.31), custom_call_target="tpu_custom_call" | custom-call | flops 1 | bytes 1 | tf_op jit(solution)/shard_map/expert_up/pallas_call | solution.py:304
  194.9 8.3 %collective-permute-done.17.refs_5_ = bf16[1,192,768]{2,1,0:T(8,128)(2,1)} collective-permute-done((bf16[1,192,768]{2,1,0:T(8,128)(2,1)}, bf16[1,192,768]{2,1,0:T(8,128)(2,1)}, u32[]{:S(2)}, u32[]{:S(2)}) %collective-permute-start.17) | collective-permute-done | bytes 294944 | tf_op jit(solution)/shard_map/ppermute | solution.py:827
  210.7 10.3 %expert_down.1 = bf16[1216,768]{1,0:T(8,128)(2,1)} custom-call(bf16[1216,3072]{1,0:T(8,128)(2,1)} %get-tuple-element.199.hidden_ref, bf16[3072,768]{1,0:T(8,128)(2,1)} %bitcast.33), custom_call_target="tpu_custom_call" | custom-call | flops 1 | bytes 1 | tf_op jit(solution)/shard_map/expert_down/pallas_call | solution.py:320
  227.3 18.2 %expert_back.1 = (bf16[1216,3072]{1,0:T(8,128)(2,1)}, bf16[1216,768]{1,0:T(8,128)(2,1)}) custom-call(bf16[1216,768]{1,0:T(8,128)(2,1)} %bitcast.35, bf16[1216,3072]{1,0:T(8,128)(2,1)} %get-tuple-element.196.slope_ref, bf16[3072,768]{1,0:T(8,128)(2,1)} %bitcast.34, bf16[768,3072]{1,0:T(8,128)(2,1)} %bitcast.32), custom_call_target="tpu_custom_call" | custom-call | flops 1 | bytes 1 | tf_op jit(solution)/shard_map/expert_back/pallas_call | solution.py:341
  245.5 12.1 %out_grad.1 = (bf16[2,4,192,768]{3,2,1,0:T(8,128)(2,1)}, bf16[2,4,192,768]{3,2,1,0:T(8,128)(2,1)}) custom-call(s32[1]{0:T(128)} %bitcast.4.me_ref, bf16[1216,3072]{1,0:T(8,128)(2,1)} %get-tuple-element.199.hidden_ref, bf16[1216,768]{1,0:T(8,128)(2,1)} %bitcast.36), custom_call_target="tpu_custom_call" | custom-call | flops 1 | bytes 1 | tf_op jit(solution)/shard_map/out_grad/pallas_call | solution.py:363
  262.6 11.4 %in_grad.1 = (bf16[2,4,48,3072]{3,2,1,0:T(8,128)(2,1)}, bf16[2,4,48,3072]{3,2,1,0:T(8,128)(2,1)}) custom-call(s32[1]{0:T(128)} %bitcast.4.me_ref, bf16[1216,768]{1,0:T(8,128)(2,1)} %bitcast.38, bf16[1216,3072]{1,0:T(8,128)(2,1)} %get-tuple-element.203.grad_ref), custom_call_target="tpu_custom_call" | custom-call | flops 1 | bytes 1 | tf_op jit(solution)/shard_map/in_grad/pallas_call | solution.py:391
  285.5 7.1 %combine.1 = (bf16[576,768]{1,0:T(8,128)(2,1)}, bf16[576,128]{1,0:T(8,128)(2,1)}) custom-call(s32[576,2]{1,0:T(8,128)} %copy.51.routes_ref, s32[576,2]{1,0:T(8,128)} %add_select_fusion.targets_ref, f32[576,128]{1,0:T(8,128)} %get-tuple-element.171.columns_ref, f32[576,768]{1,0:T(8,128)} %get-tuple-element.172.mid_ref, bf16[576,768]{1,0:T(8,128)(2,1)} %grad_ref.5, ...), custom_call_target="tpu_custom_call" | custom-call | flops 1 | bytes 1 | tf_op jit(solution)/shard_map/combine/pallas_call | solution.py:432
  292.6 6.0 %all-to-all-done.6 = bf16[8,152,768]{2,1,0:T(8,128)(2,1)S(1)} async-done(((bf16[8,152,768]{2,1,0:T(8,128)(2,1)}), bf16[8,152,768]{2,1,0:T(8,128)(2,1)S(1)}, u32[]{:S(2)}, u32[]{:S(2)}) %all-to-all-start.6) | async-done | bytes 1867808 | tf_op jit(solution)/shard_map/all_to_all | solution.py:830
  299.9 7.6 %middle_back.1 = (f32[576,768]{1,0:T(8,128)}, bf16[576,768]{1,0:T(8,128)(2,1)}, bf16[576,768]{1,0:T(8,128)(2,1)}, f32[8,768]{1,0:T(8,128)}) custom-call(s32[576,2]{1,0:T(8,128)} %add_select_fusion.targets_ref, bf16[576,128]{1,0:T(8,128)(2,1)} %get-tuple-element.216.logits_ref, f32[576,768]{1,0:T(8,128)} %get-tuple-element.172.mid_ref, ...), custom_call_target="tpu_custom_call" | custom-call | flops 1 | bytes 1 | tf_op jit(solution)/shard_map/middle_back/pallas_call | solution.py:474
  316.2 14.3 %attention_backward.1.grad_ref = bf16[576,2304]{1,0:T(8,128)(2,1)} custom-call(bf16[576,2304]{1,0:T(8,128)(2,1)} %get-tuple-element.168.qkv_ref, bf16[576,768]{1,0:T(8,128)(2,1)} %get-tuple-element.169.attended_ref.out_ref, f32[1,6,2,576]{3,2,1,0:T(2,128)} %get-tuple-element.212.log_ref, bf16[576,768]{1,0:T(8,128)(2,1)} %get-tuple-element.229.grad_ref), custom_call_target="tpu_custom_call" | custom-call | flops 1 | bytes 1 | tf_op jit(solution)/shard_map/attention_backward/pallas_call | solution.py:147
  330.4 7.9 %qkv_grads.1 = (bf16[2,2,4,24,2304]{4,3,2,1,0:T(8,128)(2,1)}, bf16[2,2,4,24,2304]{4,3,2,1,0:T(8,128)(2,1)}) custom-call(s32[1]{0:T(128)} %bitcast.4.me_ref, bf16[576,768]{1,0:T(8,128)(2,1)} %get-tuple-element.211.act_ref, bf16[576,2304]{1,0:T(8,128)(2,1)} %attention_backward.1.grad_ref), custom_call_target="tpu_custom_call" | custom-call | flops 1 | bytes 1 | tf_op jit(solution)/shard_map/qkv_grads/pallas_call | solution.py:543
  338.9 15.1 %collective-permute-done.27.refs_0_ = bf16[1,48,3072]{2,1,0:T(8,128)(2,1)S(1)} collective-permute-done((bf16[1,48,3072]{2,1,0:T(8,128)(2,1)}, bf16[1,48,3072]{2,1,0:T(8,128)(2,1)S(1)}, u32[]{:S(2)}, u32[]{:S(2)}) %collective-permute-start.27) | collective-permute-done | bytes 294944 | tf_op jit(solution)/shard_map/ppermute | solution.py:827
  362.9 8.1 %token_grads.1 = f32[576,768]{1,0:T(8,128)} custom-call(bf16[576,2304]{1,0:T(8,128)(2,1)} %attention_backward.1.grad_ref, bf16[768,3200]{1,0:T(8,128)(2,1)} %bitcast.30, bf16[576,768]{1,0:T(8,128)(2,1)} %tokens_ref.5, f32[576,768]{1,0:T(8,128)} %get-tuple-element.256.grad_mid_ref, bf16[128,768]{1,0:T(8,128)(2,1)} %get-tuple-element.170.table_ref), custom_call_target="tpu_custom_call" | custom-call | flops 1 | bytes 1 | tf_op jit(solution)/shard_map/token_grads/pallas_call | solution.py:564
  376.5 13.3 %collective-permute-done.30.refs_3_ = bf16[96,3200]{1,0:T(8,128)(2,1)} collective-permute-done((bf16[96,3200]{1,0:T(8,128)(2,1)}, bf16[96,3200]{1,0:T(8,128)(2,1)}, u32[]{:S(2)}, u32[]{:S(2)}) %collective-permute-start.30) | collective-permute-done | bytes 614432 | tf_op jit(solution)/shard_map/ppermute | solution.py:847
  (200 shorter events, 177.4 us)
Async XLA Ops:
  25.2 18.3 %collective-permute-start.4 = (bf16[4,24,3200]{2,1,0:T(8,128)(2,1)}, bf16[4,24,3200]{2,1,0:T(8,128)(2,1)S(1)}, u32[]{:S(2)}, u32[]{:S(2)}) collective-permute-start(bf16[4,24,3200]{2,1,0:T(8,128)(2,1)} %pack.3.refs_1_), channel_id=1, source_target_pairs={{0,2},{2,0},{1,3},{3,1},{4,6},{6,4},{5,7},{7,5},{8,10},{10,8},{9,1... | collective-permute-start | bytes 1843208 | tf_op jit(solution)/shard_map/ppermute | solution.py:827
  43.5 32.9 %all-to-all-start = ((bf16[4,48,3072]{2,1,0:T(8,128)(2,1)}), bf16[4,48,3072]{2,1,0:T(8,128)(2,1)S(1)}, u32[]{:S(2)}, u32[]{:S(2)}) async-start(bf16[4,48,3072]{2,1,0:T(8,128)(2,1)} %param.17), calls=%async_computation | async-start | bytes 2359296 | tf_op jit(solution)/shard_map/all_to_all | solution.py:830
  47.1 29.3 %collective-permute-start.9 = (bf16[4,24,3200]{2,1,0:T(8,128)(2,1)S(1)}, bf16[4,24,3200]{2,1,0:T(8,128)(2,1)}, u32[]{:S(2)}, u32[]{:S(2)}) collective-permute-start(bf16[4,24,3200]{2,1,0:T(8,128)(2,1)S(1)} %collective-permute-done.4.refs_3_), channel_id=1, source_target_pairs={{0,16},{16,0},{1,17},{17,1},{2,18},{18,2},{3,19},{19,3},{4,20},{20... | collective-permute-start | bytes 1843208 | tf_op jit(solution)/shard_map/ppermute | solution.py:827
  47.7 27.9 %collective-permute-start.10 = (bf16[2,48,3072]{2,1,0:T(8,128)(2,1)}, bf16[2,48,3072]{2,1,0:T(8,128)(2,1)S(1)}, u32[]{:S(2)}, u32[]{:S(2)}) collective-permute-start(bf16[2,48,3072]{2,1,0:T(8,128)(2,1)} %slice.35), channel_id=1, source_target_pairs={{0,8},{8,0},{1,9},{9,1},{2,10},{10,2},{3,11},{11,3},{4,12},{12,4},... | collective-permute-start | bytes 1769480 | tf_op jit(solution)/shard_map/ppermute | solution.py:827
  77.4 23.4 %all-to-all-start.1 = ((bf16[4,192,768]{2,1,0:T(8,128)(2,1)}), bf16[4,192,768]{2,1,0:T(8,128)(2,1)S(1)}, u32[]{:S(2)}, u32[]{:S(2)}) async-start(bf16[4,192,768]{2,1,0:T(8,128)(2,1)} %param.18), calls=%async_computation.1 | async-start | bytes 2359296 | tf_op jit(solution)/shard_map/all_to_all | solution.py:830
  82.1 18.8 %collective-permute-start.12 = (bf16[1,48,3072]{2,1,0:T(8,128)(2,1)}, bf16[1,48,3072]{2,1,0:T(8,128)(2,1)}, u32[]{:S(2)}, u32[]{:S(2)}) collective-permute-start(bf16[1,48,3072]{2,1,0:T(8,128)(2,1)} %get-tuple-element.166), channel_id=1, source_target_pairs={{0,8},{8,0},{1,9},{9,1},{2,10},{10,2},{3,11},{11,3},{4,12},{12,4},... | collective-permute-start | bytes 884744 | tf_op jit(solution)/shard_map/ppermute | solution.py:827
  103.2 33.8 %all-to-all-start.2 = ((bf16[4,48,3072]{2,1,0:T(8,128)(2,1)}), bf16[4,48,3072]{2,1,0:T(8,128)(2,1)S(1)}, u32[]{:S(2)}, u32[]{:S(2)}) async-start(bf16[4,48,3072]{2,1,0:T(8,128)(2,1)} %pad_maximum_fusion), calls=%async_computation.2 | async-start | bytes 2359296 | tf_op jit(solution)/shard_map/all_to_all | solution.py:830
  108.2 28.9 %collective-permute-start.13 = (bf16[2,192,768]{2,1,0:T(8,128)(2,1)}, bf16[2,192,768]{2,1,0:T(8,128)(2,1)S(1)}, u32[]{:S(2)}, u32[]{:S(2)}) collective-permute-start(bf16[2,192,768]{2,1,0:T(8,128)(2,1)} %slice.37), channel_id=1, source_target_pairs={{0,8},{8,0},{1,9},{9,1},{2,10},{10,2},{3,11},{11,3},{4,12},{12,4},... | collective-permute-start | bytes 1769480 | tf_op jit(solution)/shard_map/ppermute | solution.py:827
  138.3 34.1 %all-to-all-start.3 = ((bf16[8,152,768]{2,1,0:T(8,128)(2,1)}), bf16[8,152,768]{2,1,0:T(8,128)(2,1)S(1)}, u32[]{:S(2)}, u32[]{:S(2)}) async-start(bf16[8,152,768]{2,1,0:T(8,128)(2,1)} %get-tuple-element.180), calls=%async_computation.3 | async-start | bytes 3735552 | tf_op jit(solution)/shard_map/all_to_all | solution.py:830
  143.4 25.0 %collective-permute-start.16 = (bf16[1,192,768]{2,1,0:T(8,128)(2,1)}, bf16[1,192,768]{2,1,0:T(8,128)(2,1)S(1)}, u32[]{:S(2)}, u32[]{:S(2)}) collective-permute-start(bf16[1,192,768]{2,1,0:T(8,128)(2,1)} %slice.38), channel_id=1, source_target_pairs={{0,8},{8,0},{1,9},{9,1},{2,10},{10,2},{3,11},{11,3},{4,12},{12,4},... | collective-permute-start | bytes 884744 | tf_op jit(solution)/shard_map/ppermute | solution.py:827
  173.7 47.3 %all-to-all-start.4 = ((bf16[8,152,768]{2,1,0:T(8,128)(2,1)}), bf16[8,152,768]{2,1,0:T(8,128)(2,1)S(1)}, u32[]{:S(2)}, u32[]{:S(2)}) async-start(bf16[8,152,768]{2,1,0:T(8,128)(2,1)} %slot_grads.1), calls=%async_computation.4 | async-start | bytes 3735552 | tf_op jit(solution)/shard_map/all_to_all | solution.py:830
  177.3 27.8 %collective-permute-start.18 = (bf16[4,192,768]{2,1,0:T(8,128)(2,1)S(1)}, bf16[4,192,768]{2,1,0:T(8,128)(2,1)}, u32[]{:S(2)}, u32[]{:S(2)}) collective-permute-start(bf16[4,192,768]{2,1,0:T(8,128)(2,1)S(1)} %all-to-all-done.1.refs_1_), channel_id=1, source_target_pairs={{0,1},{1,0},{2,3},{3,2},{4,5},{5,4},{6,7},{7,6},{8,9},{9,8},{10,11... | collective-permute-start | bytes 3538952 | tf_op jit(solution)/shard_map/ppermute | solution.py:827
  178.1 25.1 %collective-permute-start.17 = (bf16[1,192,768]{2,1,0:T(8,128)(2,1)}, bf16[1,192,768]{2,1,0:T(8,128)(2,1)}, u32[]{:S(2)}, u32[]{:S(2)}) collective-permute-start(bf16[1,192,768]{2,1,0:T(8,128)(2,1)} %slice.39), channel_id=1, source_target_pairs={{0,8},{8,0},{1,9},{9,1},{2,10},{10,2},{3,11},{11,3},{4,12},{12,4},... | collective-permute-start | bytes 884744 | tf_op jit(solution)/shard_map/ppermute | solution.py:827
  178.1 25.1 %collective-permute-start.19 = (bf16[2,192,768]{2,1,0:T(8,128)(2,1)}, bf16[2,192,768]{2,1,0:T(8,128)(2,1)}, u32[]{:S(2)}, u32[]{:S(2)}) collective-permute-start(bf16[2,192,768]{2,1,0:T(8,128)(2,1)} %copy-done.14), channel_id=1, source_target_pairs={{0,1},{1,0},{2,3},{3,2},{4,5},{5,4},{6,7},{7,6},{8,9},{9,8},{10,11... | collective-permute-start | bytes 1769480 | tf_op jit(solution)/shard_map/ppermute | solution.py:827
  178.6 24.6 %collective-permute-start.20 = (bf16[1,192,768]{2,1,0:T(8,128)(2,1)S(1)}, bf16[1,192,768]{2,1,0:T(8,128)(2,1)}, u32[]{:S(2)}, u32[]{:S(2)}) collective-permute-start(bf16[1,192,768]{2,1,0:T(8,128)(2,1)S(1)} %collective-permute-done.16.refs_4_), channel_id=1, source_target_pairs={{0,1},{1,0},{2,3},{3,2},{4,5},{5,4},{6,7},{7,6},{8,9},{9,8},{10,11... | collective-permute-start | bytes 884744 | tf_op jit(solution)/shard_map/ppermute | solution.py:827
  222.2 35.3 %all-to-all-start.5 = ((bf16[8,152,768]{2,1,0:T(8,128)(2,1)}), bf16[8,152,768]{2,1,0:T(8,128)(2,1)}, u32[]{:S(2)}, u32[]{:S(2)}) async-start(bf16[8,152,768]{2,1,0:T(8,128)(2,1)} %bitcast.40), calls=%async_computation.5 | async-start | bytes 3735552 | tf_op jit(solution)/shard_map/all_to_all | solution.py:830
  257.5 41.1 %all-to-all-start.6 = ((bf16[8,152,768]{2,1,0:T(8,128)(2,1)}), bf16[8,152,768]{2,1,0:T(8,128)(2,1)S(1)}, u32[]{:S(2)}, u32[]{:S(2)}) async-start(bf16[8,152,768]{2,1,0:T(8,128)(2,1)} %bitcast.41), calls=%async_computation.6 | async-start | bytes 3735552 | tf_op jit(solution)/shard_map/all_to_all | solution.py:830
  274.1 37.6 %collective-permute-start.23 = (bf16[2,4,48,3072]{3,2,1,0:T(8,128)(2,1)}, bf16[2,4,48,3072]{3,2,1,0:T(8,128)(2,1)}, u32[]{:S(2)}, u32[]{:S(2)}) collective-permute-start(bf16[2,4,48,3072]{3,2,1,0:T(8,128)(2,1)} %get-tuple-element.223), channel_id=1, source_target_pairs={{0,1},{1,0},{2,3},{3,2},{4,5},{5,4},{6,7},{7,6},{8,9},{9,8},{10,11... | collective-permute-start | bytes 7077896 | tf_op jit(solution)/shard_map/ppermute | solution.py:827
  278.9 59.4 %collective-permute-start.24 = (bf16[4,192,768]{2,1,0:T(8,128)(2,1)}, bf16[4,192,768]{2,1,0:T(8,128)(2,1)S(1)}, u32[]{:S(2)}, u32[]{:S(2)}) collective-permute-start(bf16[4,192,768]{2,1,0:T(8,128)(2,1)} %get-tuple-element.233), channel_id=1, source_target_pairs={{0,8},{8,0},{1,9},{9,1},{2,10},{10,2},{3,11},{11,3},{4,12},{12,4},... | collective-permute-start | bytes 3538952 | tf_op jit(solution)/shard_map/ppermute | solution.py:827
  359.3 38.7 %collective-permute-start.31 = (bf16[3,48,3072]{2,1,0:T(8,128)(2,1)}, bf16[3,48,3072]{2,1,0:T(8,128)(2,1)S(1)}, u32[]{:S(2)}, u32[]{:S(2)}) collective-permute-start(bf16[3,48,3072]{2,1,0:T(8,128)(2,1)} %get-tuple-element.277), channel_id=1, source_target_pairs={{0,8},{8,0},{1,9},{9,1},{2,10},{10,2},{3,11},{11,3},{4,12},{12,4},... | collective-permute-start | bytes 2654216 | tf_op jit(solution)/shard_map/ppermute | solution.py:827
  360.4 29.4 %collective-permute-start.30 = (bf16[96,3200]{1,0:T(8,128)(2,1)}, bf16[96,3200]{1,0:T(8,128)(2,1)}, u32[]{:S(2)}, u32[]{:S(2)}) collective-permute-start(bf16[96,3200]{1,0:T(8,128)(2,1)} %get-tuple-element.254), channel_id=1, source_target_pairs={{0,18},{2,16},{16,2},{18,0},{1,19},{3,17},{17,3},{19,1},{4,22},{6,... | collective-permute-start | bytes 1843208 | tf_op jit(solution)/shard_map/ppermute | solution.py:847
  402.3 17.7 %collective-permute-start.39 = (bf16[192,768]{1,0:T(8,128)(2,1)}, bf16[192,768]{1,0:T(8,128)(2,1)S(1)}, u32[]{:S(2)}, u32[]{:S(2)}) collective-permute-start(bf16[192,768]{1,0:T(8,128)(2,1)} %get-tuple-element.291), channel_id=1, source_target_pairs={{0,4},{2,6},{4,0},{6,2},{1,5},{3,7},{5,1},{7,3},{8,12},{10,14},{12... | collective-permute-start | bytes 884744 | tf_op jit(solution)/shard_map/ppermute | solution.py:847
  412.8 17.8 %collective-permute-start.36 = (bf16[48,3072]{1,0:T(8,128)(2,1)}, bf16[48,3072]{1,0:T(8,128)(2,1)S(1)}, u32[]{:S(2)}, u32[]{:S(2)}) collective-permute-start(bf16[48,3072]{1,0:T(8,128)(2,1)} %get-tuple-element.287), channel_id=1, source_target_pairs={{0,4},{2,6},{4,0},{6,2},{1,5},{3,7},{5,1},{7,3},{8,12},{10,14},{12... | collective-permute-start | bytes 884744 | tf_op jit(solution)/shard_map/ppermute | solution.py:847
  417.9 17.4 %collective-permute-start.37 = (bf16[48,3072]{1,0:T(8,128)(2,1)S(1)}, bf16[48,3072]{1,0:T(8,128)(2,1)S(1)}, u32[]{:S(2)}, u32[]{:S(2)}) collective-permute-start(bf16[48,3072]{1,0:T(8,128)(2,1)S(1)} %copy-done.33), channel_id=1, source_target_pairs={{0,6},{2,4},{4,2},{6,0},{1,7},{3,5},{5,3},{7,1},{8,14},{10,12},{12... | collective-permute-start | bytes 884744 | tf_op jit(solution)/shard_map/ppermute | solution.py:847
  (58 other events, 719.0 us)

commit v6 on v5

--- a/solution.py
+++ b/solution.py
@@ -931,8 +931,11 @@
     def rows_turn(self, pieces):
         return turn(self.number("zh", "zl"), pieces)
 
+    def rows_last(self, pieces):
+        return self.moved(pieces, "zh", "zl")
+
     def rows_end(self, pieces):
-        return sum(piece.astype(F32) for piece in self.moved(pieces, "zh", "zl"))
+        return sum(piece.astype(F32) for piece in pieces)
 
 
 class AxisLinks:
@@ -997,6 +1000,9 @@
         return [lax.psum_scatter(pieces[0], self.data, scatter_dimension=0, tiled=True)]
 
     def rows_turn(self, pieces):
+        return pieces
+
+    def rows_last(self, pieces):
         return pieces
 
     def rows_end(self, pieces):
@@ -1078,7 +1084,8 @@
     turned, out_pieces, in_keep, in_second = together(
         links.rows_turn(qkv_sent), out_pieces, in_keep, in_second
     )
-    d_dense = links.rows_end(turned)
+    dense_pieces, out_pieces = together(links.rows_last(turned), out_pieces)
+    d_dense = links.rows_end(dense_pieces)
     d_out = links.expert_end(out_pieces)
     d_in = links.expert_end(links.expert_pick(in_keep, in_first + in_second))
     d_qkv = d_dense[:, : 3 * WIDTH]

time: 442 us -> 443 us (level)
    unnamed x72 -> x74, local copies, waits for them, and re-layouts: 12.8 us -> 12.7 us
where the time goes in v6:
time: 443 us; the launch traced here: 441 us
  Pallas kernels  202 us (46%)
  waiting for transfers between devices  137 us (31%)
  starting transfers between devices  68.8 us (16%)
  local copies, waits for them, and re-layouts  24.8 us (6%)
  other arithmetic  6.78 us (2%)
    ppermute x26, waiting for transfers between devices, swap(): return lax.ppermute(value, axis, [(0, 1), (1, 0)])  89.2 us
    ppermute x15, waiting for transfers between devices, moved(): lax.ppermute(pieces[k], axes, routes[k])  37.7 us
    all_to_all x7, starting transfers between devices, trade(): return lax.all_to_all(value, axes, 0, 0, tiled=True)  28.9 us
    ppermute x15, starting transfers between devices, moved(): lax.ppermute(pieces[k], axes, routes[k])  21.3 us
    ppermute x26, starting transfers between devices, swap(): return lax.ppermute(value, axis, [(0, 1), (1, 0)])  18.6 us
    pallas_call x1, Pallas kernels, expert_back(): call('expert_back', expert_back_kernel, (count // ROW_BLOCK,), [narrow, w...  18.2 us
    pallas_call x1, Pallas kernels, expert_up(): call('expert_up', expert_up_kernel, (depth // F_BLOCK,), [whole(count, WI...  16.4 us
    pallas_call x1, Pallas kernels, attention_backward(): call('attention_backward', attention_back_kernel, (qkv.shape[0] // SEQ, P...  14.3 us
  transfers between devices with their start and end apart: 48, of which 22 were waited for; matrix products, arithmetic and copies ran while one was open for 3% of the time, Pallas kernels for 44%

profile of v6, /device:TPU:0, one launch (start us, length us, event | category | flops | bytes accessed | tf_op | source)
XLA Modules:
  0.0 440.6 jit_solution(16664641677292242092)
XLA Ops:
  14.4 8.0 %collective-permute-done.1.refs_2_ = bf16[24,3200]{1,0:T(8,128)(2,1)S(1)} collective-permute-done((bf16[24,3200]{1,0:T(8,128)(2,1)S(1)}, bf16[24,3200]{1,0:T(8,128)(2,1)S(1)}, u32[]{:S(2)}, u32[]{:S(2)}) %collective-permute-start.1) | collective-permute-done | bytes 153632 | tf_op jit(solution)/shard_map/ppermute | solution.py:847
  31.6 11.9 %collective-permute-done.6 = bf16[1,48,3072]{2,1,0:T(8,128)(2,1)S(1)} collective-permute-done((bf16[1,48,3072]{2,1,0:T(8,128)(2,1)S(1)}, bf16[1,48,3072]{2,1,0:T(8,128)(2,1)S(1)}, u32[]{:S(2)}, u32[]{:S(2)}) %collective-permute-start.6) | collective-permute-done | bytes 294944 | tf_op jit(solution)/shard_map/ppermute | solution.py:827
  49.9 25.7 %collective-permute-done.10 = bf16[2,48,3072]{2,1,0:T(8,128)(2,1)S(1)} collective-permute-done((bf16[2,48,3072]{2,1,0:T(8,128)(2,1)}, bf16[2,48,3072]{2,1,0:T(8,128)(2,1)S(1)}, u32[]{:S(2)}, u32[]{:S(2)}) %collective-permute-start.10) | collective-permute-done | bytes 589856 | tf_op jit(solution)/shard_map/ppermute | solution.py:827
  85.8 7.0 %place.1 = bf16[2,4,2,2,24,3200]{5,4,3,2,1,0:T(8,128)(2,1)} custom-call(s32[3]{0:T(128)} %pad_add_fusion.refs_0_, bf16[4,24,3200]{2,1,0:T(8,128)(2,1)} %pack.3.refs_1_, bf16[4,24,3200]{2,1,0:T(8,128)(2,1)} %collective-permute-done.3.refs_2_, bf16[4,24,3200]{2,1,0:T(8,128)(2,1)} %copy-done.10, bf16[4,24,3200]{2,1,0:T(8,128)(2,1)} %collective-permute-done.7.refs_4_, ...), custom_call_target="tpu_custom_call" | custom-call | flops 1 | bytes 1 | tf_op jit(solution)/shard_map/place/pallas_call | solution.py:606
  92.8 8.0 %project.1 = (bf16[576,2304]{1,0:T(8,128)(2,1)}, bf16[576,768]{1,0:T(8,128)(2,1)}, bf16[128,768]{1,0:T(8,128)(2,1)}) custom-call(bf16[576,768]{1,0:T(8,128)(2,1)} %tokens_ref.5, bf16[768,3200]{1,0:T(8,128)(2,1)} %bitcast.26, bf16[768,3200]{1,0:T(8,128)(2,1)} %bitcast.27), custom_call_target="tpu_custom_call" | custom-call | flops 1 | bytes 1 | tf_op jit(solution)/shard_map/project/pallas_call | solution.py:176
  109.3 10.4 %attention_forward.1 = (bf16[576,768]{1,0:T(8,128)(2,1)}, f32[1,6,2,576]{3,2,1,0:T(2,128)}) custom-call(bf16[576,2304]{1,0:T(8,128)(2,1)} %get-tuple-element.176.qkv_ref), custom_call_target="tpu_custom_call" | custom-call | flops 1 | bytes 1 | tf_op jit(solution)/shard_map/attention_forward/pallas_call | solution.py:135
  119.7 9.3 %middle.1 = (f32[576,768]{1,0:T(8,128)}, bf16[576,768]{1,0:T(8,128)(2,1)}, f32[576,128]{1,0:T(8,128)}, f32[8,576]{1,0:T(8,128)}, bf16[8,152,768]{2,1,0:T(8,128)(2,1)}) custom-call(s32[2,576]{1,0:T(2,128)} %bitcast.47, s32[2,576]{1,0:T(2,128)} %bitcast.49, bf16[576,768]{1,0:T(8,128)(2,1)} %tokens_ref.5, ...), custom_call_target="tpu_custom_call" | custom-call | flops 1 | bytes 1 | tf_op jit(solution)/shard_map/middle/pallas_call | solution.py:243
  129.1 7.9 %collective-permute-done.13.refs_3_ = bf16[2,192,768]{2,1,0:T(8,128)(2,1)S(1)} collective-permute-done((bf16[2,192,768]{2,1,0:T(8,128)(2,1)}, bf16[2,192,768]{2,1,0:T(8,128)(2,1)S(1)}, u32[]{:S(2)}, u32[]{:S(2)}) %collective-permute-start.13) | collective-permute-done | bytes 589856 | tf_op jit(solution)/shard_map/ppermute | solution.py:827
  145.4 5.9 %slot_grads.1 = bf16[8,152,768]{2,1,0:T(8,128)(2,1)} custom-call(s32[2,576]{1,0:T(2,128)} %bitcast.48, s32[2,576]{1,0:T(2,128)} %bitcast.50, f32[8,576]{1,0:T(8,128)} %get-tuple-element.187.gates_ref, bf16[576,768]{1,0:T(8,128)(2,1)} %grad_ref.5), custom_call_target="tpu_custom_call" | custom-call | flops 1 | bytes 1 | tf_op jit(solution)/shard_map/slot_grads/pallas_call | solution.py:280
  157.0 11.3 %collective-permute-done.16.refs_4_ = bf16[1,192,768]{2,1,0:T(8,128)(2,1)S(1)} collective-permute-done((bf16[1,192,768]{2,1,0:T(8,128)(2,1)}, bf16[1,192,768]{2,1,0:T(8,128)(2,1)S(1)}, u32[]{:S(2)}, u32[]{:S(2)}) %collective-permute-start.16) | collective-permute-done | bytes 294944 | tf_op jit(solution)/shard_map/ppermute | solution.py:827
  178.5 16.4 %expert_up.1 = (bf16[1216,3072]{1,0:T(8,128)(2,1)}, bf16[1216,3072]{1,0:T(8,128)(2,1)}) custom-call(bf16[1216,768]{1,0:T(8,128)(2,1)} %bitcast.37, bf16[768,3072]{1,0:T(8,128)(2,1)} %bitcast.31), custom_call_target="tpu_custom_call" | custom-call | flops 1 | bytes 1 | tf_op jit(solution)/shard_map/expert_up/pallas_call | solution.py:304
  194.9 8.2 %collective-permute-done.17.refs_5_ = bf16[1,192,768]{2,1,0:T(8,128)(2,1)} collective-permute-done((bf16[1,192,768]{2,1,0:T(8,128)(2,1)}, bf16[1,192,768]{2,1,0:T(8,128)(2,1)}, u32[]{:S(2)}, u32[]{:S(2)}) %collective-permute-start.17) | collective-permute-done | bytes 294944 | tf_op jit(solution)/shard_map/ppermute | solution.py:827
  210.6 10.3 %expert_down.1 = bf16[1216,768]{1,0:T(8,128)(2,1)} custom-call(bf16[1216,3072]{1,0:T(8,128)(2,1)} %get-tuple-element.207.hidden_ref, bf16[3072,768]{1,0:T(8,128)(2,1)} %bitcast.33), custom_call_target="tpu_custom_call" | custom-call | flops 1 | bytes 1 | tf_op jit(solution)/shard_map/expert_down/pallas_call | solution.py:320
  227.2 18.2 %expert_back.1 = (bf16[1216,3072]{1,0:T(8,128)(2,1)}, bf16[1216,768]{1,0:T(8,128)(2,1)}) custom-call(bf16[1216,768]{1,0:T(8,128)(2,1)} %bitcast.35, bf16[1216,3072]{1,0:T(8,128)(2,1)} %get-tuple-element.204.slope_ref, bf16[3072,768]{1,0:T(8,128)(2,1)} %bitcast.34, bf16[768,3072]{1,0:T(8,128)(2,1)} %bitcast.32), custom_call_target="tpu_custom_call" | custom-call | flops 1 | bytes 1 | tf_op jit(solution)/shard_map/expert_back/pallas_call | solution.py:341
  245.4 12.1 %out_grad.1 = (bf16[2,4,192,768]{3,2,1,0:T(8,128)(2,1)}, bf16[2,4,192,768]{3,2,1,0:T(8,128)(2,1)}) custom-call(s32[1]{0:T(128)} %bitcast.4.me_ref, bf16[1216,3072]{1,0:T(8,128)(2,1)} %get-tuple-element.207.hidden_ref, bf16[1216,768]{1,0:T(8,128)(2,1)} %bitcast.36), custom_call_target="tpu_custom_call" | custom-call | flops 1 | bytes 1 | tf_op jit(solution)/shard_map/out_grad/pallas_call | solution.py:363
  262.6 11.5 %in_grad.1 = (bf16[2,4,48,3072]{3,2,1,0:T(8,128)(2,1)}, bf16[2,4,48,3072]{3,2,1,0:T(8,128)(2,1)}) custom-call(s32[1]{0:T(128)} %bitcast.4.me_ref, bf16[1216,768]{1,0:T(8,128)(2,1)} %bitcast.38, bf16[1216,3072]{1,0:T(8,128)(2,1)} %get-tuple-element.211.grad_ref), custom_call_target="tpu_custom_call" | custom-call | flops 1 | bytes 1 | tf_op jit(solution)/shard_map/in_grad/pallas_call | solution.py:391
  285.5 7.1 %combine.1 = (bf16[576,768]{1,0:T(8,128)(2,1)}, bf16[576,128]{1,0:T(8,128)(2,1)}) custom-call(s32[576,2]{1,0:T(8,128)} %copy.51.routes_ref, s32[576,2]{1,0:T(8,128)} %add_select_fusion.targets_ref, f32[576,128]{1,0:T(8,128)} %get-tuple-element.179.columns_ref, f32[576,768]{1,0:T(8,128)} %get-tuple-element.180.mid_ref, bf16[576,768]{1,0:T(8,128)(2,1)} %grad_ref.5, ...), custom_call_target="tpu_custom_call" | custom-call | flops 1 | bytes 1 | tf_op jit(solution)/shard_map/combine/pallas_call | solution.py:432
  292.5 6.0 %all-to-all-done.6 = bf16[8,152,768]{2,1,0:T(8,128)(2,1)S(1)} async-done(((bf16[8,152,768]{2,1,0:T(8,128)(2,1)}), bf16[8,152,768]{2,1,0:T(8,128)(2,1)S(1)}, u32[]{:S(2)}, u32[]{:S(2)}) %all-to-all-start.6) | async-done | bytes 1867808 | tf_op jit(solution)/shard_map/all_to_all | solution.py:830
  299.7 7.5 %middle_back.1 = (f32[576,768]{1,0:T(8,128)}, bf16[576,768]{1,0:T(8,128)(2,1)}, bf16[576,768]{1,0:T(8,128)(2,1)}, f32[8,768]{1,0:T(8,128)}) custom-call(s32[576,2]{1,0:T(8,128)} %add_select_fusion.targets_ref, bf16[576,128]{1,0:T(8,128)(2,1)} %get-tuple-element.224.logits_ref, f32[576,768]{1,0:T(8,128)} %get-tuple-element.180.mid_ref, ...), custom_call_target="tpu_custom_call" | custom-call | flops 1 | bytes 1 | tf_op jit(solution)/shard_map/middle_back/pallas_call | solution.py:474
  316.1 14.3 %attention_backward.1.grad_ref = bf16[576,2304]{1,0:T(8,128)(2,1)} custom-call(bf16[576,2304]{1,0:T(8,128)(2,1)} %get-tuple-element.176.qkv_ref, bf16[576,768]{1,0:T(8,128)(2,1)} %get-tuple-element.177.attended_ref.out_ref, f32[1,6,2,576]{3,2,1,0:T(2,128)} %get-tuple-element.220.log_ref, bf16[576,768]{1,0:T(8,128)(2,1)} %get-tuple-element.237.grad_ref), custom_call_target="tpu_custom_call" | custom-call | flops 1 | bytes 1 | tf_op jit(solution)/shard_map/attention_backward/pallas_call | solution.py:147
  330.4 7.9 %qkv_grads.1 = (bf16[2,2,4,24,2304]{4,3,2,1,0:T(8,128)(2,1)}, bf16[2,2,4,24,2304]{4,3,2,1,0:T(8,128)(2,1)}) custom-call(s32[1]{0:T(128)} %bitcast.4.me_ref, bf16[576,768]{1,0:T(8,128)(2,1)} %get-tuple-element.219.act_ref, bf16[576,2304]{1,0:T(8,128)(2,1)} %attention_backward.1.grad_ref), custom_call_target="tpu_custom_call" | custom-call | flops 1 | bytes 1 | tf_op jit(solution)/shard_map/qkv_grads/pallas_call | solution.py:543
  338.8 15.1 %collective-permute-done.27.refs_0_ = bf16[1,48,3072]{2,1,0:T(8,128)(2,1)S(1)} collective-permute-done((bf16[1,48,3072]{2,1,0:T(8,128)(2,1)}, bf16[1,48,3072]{2,1,0:T(8,128)(2,1)S(1)}, u32[]{:S(2)}, u32[]{:S(2)}) %collective-permute-start.27) | collective-permute-done | bytes 294944 | tf_op jit(solution)/shard_map/ppermute | solution.py:827
  362.8 8.1 %token_grads.1 = f32[576,768]{1,0:T(8,128)} custom-call(bf16[576,2304]{1,0:T(8,128)(2,1)} %attention_backward.1.grad_ref, bf16[768,3200]{1,0:T(8,128)(2,1)} %bitcast.30, bf16[576,768]{1,0:T(8,128)(2,1)} %tokens_ref.5, f32[576,768]{1,0:T(8,128)} %get-tuple-element.264.grad_mid_ref, bf16[128,768]{1,0:T(8,128)(2,1)} %get-tuple-element.178.table_ref), custom_call_target="tpu_custom_call" | custom-call | flops 1 | bytes 1 | tf_op jit(solution)/shard_map/token_grads/pallas_call | solution.py:564
  376.4 13.3 %collective-permute-done.30.refs_3_ = bf16[96,3200]{1,0:T(8,128)(2,1)} collective-permute-done((bf16[96,3200]{1,0:T(8,128)(2,1)}, bf16[96,3200]{1,0:T(8,128)(2,1)}, u32[]{:S(2)}, u32[]{:S(2)}) %collective-permute-start.30) | collective-permute-done | bytes 614432 | tf_op jit(solution)/shard_map/ppermute | solution.py:847
  (202 shorter events, 178.4 us)
Async XLA Ops:
  25.2 18.3 %collective-permute-start.4 = (bf16[4,24,3200]{2,1,0:T(8,128)(2,1)}, bf16[4,24,3200]{2,1,0:T(8,128)(2,1)S(1)}, u32[]{:S(2)}, u32[]{:S(2)}) collective-permute-start(bf16[4,24,3200]{2,1,0:T(8,128)(2,1)} %pack.3.refs_1_), channel_id=1, source_target_pairs={{0,2},{2,0},{1,3},{3,1},{4,6},{6,4},{5,7},{7,5},{8,10},{10,8},{9,1... | collective-permute-start | bytes 1843208 | tf_op jit(solution)/shard_map/ppermute | solution.py:827
  43.5 32.9 %all-to-all-start = ((bf16[4,48,3072]{2,1,0:T(8,128)(2,1)}), bf16[4,48,3072]{2,1,0:T(8,128)(2,1)S(1)}, u32[]{:S(2)}, u32[]{:S(2)}) async-start(bf16[4,48,3072]{2,1,0:T(8,128)(2,1)} %param.17), calls=%async_computation | async-start | bytes 2359296 | tf_op jit(solution)/shard_map/all_to_all | solution.py:830
  47.1 29.3 %collective-permute-start.9 = (bf16[4,24,3200]{2,1,0:T(8,128)(2,1)S(1)}, bf16[4,24,3200]{2,1,0:T(8,128)(2,1)}, u32[]{:S(2)}, u32[]{:S(2)}) collective-permute-start(bf16[4,24,3200]{2,1,0:T(8,128)(2,1)S(1)} %collective-permute-done.4.refs_3_), channel_id=1, source_target_pairs={{0,16},{16,0},{1,17},{17,1},{2,18},{18,2},{3,19},{19,3},{4,20},{20... | collective-permute-start | bytes 1843208 | tf_op jit(solution)/shard_map/ppermute | solution.py:827
  47.7 27.9 %collective-permute-start.10 = (bf16[2,48,3072]{2,1,0:T(8,128)(2,1)}, bf16[2,48,3072]{2,1,0:T(8,128)(2,1)S(1)}, u32[]{:S(2)}, u32[]{:S(2)}) collective-permute-start(bf16[2,48,3072]{2,1,0:T(8,128)(2,1)} %slice.35), channel_id=1, source_target_pairs={{0,8},{8,0},{1,9},{9,1},{2,10},{10,2},{3,11},{11,3},{4,12},{12,4},... | collective-permute-start | bytes 1769480 | tf_op jit(solution)/shard_map/ppermute | solution.py:827
  77.4 23.4 %all-to-all-start.1 = ((bf16[4,192,768]{2,1,0:T(8,128)(2,1)}), bf16[4,192,768]{2,1,0:T(8,128)(2,1)S(1)}, u32[]{:S(2)}, u32[]{:S(2)}) async-start(bf16[4,192,768]{2,1,0:T(8,128)(2,1)} %param.18), calls=%async_computation.1 | async-start | bytes 2359296 | tf_op jit(solution)/shard_map/all_to_all | solution.py:830
  82.1 18.7 %collective-permute-start.12 = (bf16[1,48,3072]{2,1,0:T(8,128)(2,1)}, bf16[1,48,3072]{2,1,0:T(8,128)(2,1)}, u32[]{:S(2)}, u32[]{:S(2)}) collective-permute-start(bf16[1,48,3072]{2,1,0:T(8,128)(2,1)} %get-tuple-element.174), channel_id=1, source_target_pairs={{0,8},{8,0},{1,9},{9,1},{2,10},{10,2},{3,11},{11,3},{4,12},{12,4},... | collective-permute-start | bytes 884744 | tf_op jit(solution)/shard_map/ppermute | solution.py:827
  103.2 33.8 %all-to-all-start.2 = ((bf16[4,48,3072]{2,1,0:T(8,128)(2,1)}), bf16[4,48,3072]{2,1,0:T(8,128)(2,1)S(1)}, u32[]{:S(2)}, u32[]{:S(2)}) async-start(bf16[4,48,3072]{2,1,0:T(8,128)(2,1)} %pad_maximum_fusion), calls=%async_computation.2 | async-start | bytes 2359296 | tf_op jit(solution)/shard_map/all_to_all | solution.py:830
  108.1 28.9 %collective-permute-start.13 = (bf16[2,192,768]{2,1,0:T(8,128)(2,1)}, bf16[2,192,768]{2,1,0:T(8,128)(2,1)S(1)}, u32[]{:S(2)}, u32[]{:S(2)}) collective-permute-start(bf16[2,192,768]{2,1,0:T(8,128)(2,1)} %slice.37), channel_id=1, source_target_pairs={{0,8},{8,0},{1,9},{9,1},{2,10},{10,2},{3,11},{11,3},{4,12},{12,4},... | collective-permute-start | bytes 1769480 | tf_op jit(solution)/shard_map/ppermute | solution.py:827
  138.2 34.1 %all-to-all-start.3 = ((bf16[8,152,768]{2,1,0:T(8,128)(2,1)}), bf16[8,152,768]{2,1,0:T(8,128)(2,1)S(1)}, u32[]{:S(2)}, u32[]{:S(2)}) async-start(bf16[8,152,768]{2,1,0:T(8,128)(2,1)} %get-tuple-element.188), calls=%async_computation.3 | async-start | bytes 3735552 | tf_op jit(solution)/shard_map/all_to_all | solution.py:830
  143.4 24.9 %collective-permute-start.16 = (bf16[1,192,768]{2,1,0:T(8,128)(2,1)}, bf16[1,192,768]{2,1,0:T(8,128)(2,1)S(1)}, u32[]{:S(2)}, u32[]{:S(2)}) collective-permute-start(bf16[1,192,768]{2,1,0:T(8,128)(2,1)} %slice.38), channel_id=1, source_target_pairs={{0,8},{8,0},{1,9},{9,1},{2,10},{10,2},{3,11},{11,3},{4,12},{12,4},... | collective-permute-start | bytes 884744 | tf_op jit(solution)/shard_map/ppermute | solution.py:827
  173.6 47.3 %all-to-all-start.4 = ((bf16[8,152,768]{2,1,0:T(8,128)(2,1)}), bf16[8,152,768]{2,1,0:T(8,128)(2,1)S(1)}, u32[]{:S(2)}, u32[]{:S(2)}) async-start(bf16[8,152,768]{2,1,0:T(8,128)(2,1)} %slot_grads.1), calls=%async_computation.4 | async-start | bytes 3735552 | tf_op jit(solution)/shard_map/all_to_all | solution.py:830
  177.2 27.8 %collective-permute-start.18 = (bf16[4,192,768]{2,1,0:T(8,128)(2,1)S(1)}, bf16[4,192,768]{2,1,0:T(8,128)(2,1)}, u32[]{:S(2)}, u32[]{:S(2)}) collective-permute-start(bf16[4,192,768]{2,1,0:T(8,128)(2,1)S(1)} %all-to-all-done.1.refs_1_), channel_id=1, source_target_pairs={{0,1},{1,0},{2,3},{3,2},{4,5},{5,4},{6,7},{7,6},{8,9},{9,8},{10,11... | collective-permute-start | bytes 3538952 | tf_op jit(solution)/shard_map/ppermute | solution.py:827
  178.0 25.1 %collective-permute-start.17 = (bf16[1,192,768]{2,1,0:T(8,128)(2,1)}, bf16[1,192,768]{2,1,0:T(8,128)(2,1)}, u32[]{:S(2)}, u32[]{:S(2)}) collective-permute-start(bf16[1,192,768]{2,1,0:T(8,128)(2,1)} %slice.39), channel_id=1, source_target_pairs={{0,8},{8,0},{1,9},{9,1},{2,10},{10,2},{3,11},{11,3},{4,12},{12,4},... | collective-permute-start | bytes 884744 | tf_op jit(solution)/shard_map/ppermute | solution.py:827
  178.0 25.1 %collective-permute-start.19 = (bf16[2,192,768]{2,1,0:T(8,128)(2,1)}, bf16[2,192,768]{2,1,0:T(8,128)(2,1)}, u32[]{:S(2)}, u32[]{:S(2)}) collective-permute-start(bf16[2,192,768]{2,1,0:T(8,128)(2,1)} %copy-done.14), channel_id=1, source_target_pairs={{0,1},{1,0},{2,3},{3,2},{4,5},{5,4},{6,7},{7,6},{8,9},{9,8},{10,11... | collective-permute-start | bytes 1769480 | tf_op jit(solution)/shard_map/ppermute | solution.py:827
  178.5 24.6 %collective-permute-start.20 = (bf16[1,192,768]{2,1,0:T(8,128)(2,1)S(1)}, bf16[1,192,768]{2,1,0:T(8,128)(2,1)}, u32[]{:S(2)}, u32[]{:S(2)}) collective-permute-start(bf16[1,192,768]{2,1,0:T(8,128)(2,1)S(1)} %collective-permute-done.16.refs_4_), channel_id=1, source_target_pairs={{0,1},{1,0},{2,3},{3,2},{4,5},{5,4},{6,7},{7,6},{8,9},{9,8},{10,11... | collective-permute-start | bytes 884744 | tf_op jit(solution)/shard_map/ppermute | solution.py:827
  222.1 35.3 %all-to-all-start.5 = ((bf16[8,152,768]{2,1,0:T(8,128)(2,1)}), bf16[8,152,768]{2,1,0:T(8,128)(2,1)}, u32[]{:S(2)}, u32[]{:S(2)}) async-start(bf16[8,152,768]{2,1,0:T(8,128)(2,1)} %bitcast.40), calls=%async_computation.5 | async-start | bytes 3735552 | tf_op jit(solution)/shard_map/all_to_all | solution.py:830
  257.5 41.0 %all-to-all-start.6 = ((bf16[8,152,768]{2,1,0:T(8,128)(2,1)}), bf16[8,152,768]{2,1,0:T(8,128)(2,1)S(1)}, u32[]{:S(2)}, u32[]{:S(2)}) async-start(bf16[8,152,768]{2,1,0:T(8,128)(2,1)} %bitcast.41), calls=%async_computation.6 | async-start | bytes 3735552 | tf_op jit(solution)/shard_map/all_to_all | solution.py:830
  274.0 37.5 %collective-permute-start.23 = (bf16[2,4,48,3072]{3,2,1,0:T(8,128)(2,1)}, bf16[2,4,48,3072]{3,2,1,0:T(8,128)(2,1)}, u32[]{:S(2)}, u32[]{:S(2)}) collective-permute-start(bf16[2,4,48,3072]{3,2,1,0:T(8,128)(2,1)} %get-tuple-element.231), channel_id=1, source_target_pairs={{0,1},{1,0},{2,3},{3,2},{4,5},{5,4},{6,7},{7,6},{8,9},{9,8},{10,11... | collective-permute-start | bytes 7077896 | tf_op jit(solution)/shard_map/ppermute | solution.py:827
  278.8 59.4 %collective-permute-start.24 = (bf16[4,192,768]{2,1,0:T(8,128)(2,1)}, bf16[4,192,768]{2,1,0:T(8,128)(2,1)S(1)}, u32[]{:S(2)}, u32[]{:S(2)}) collective-permute-start(bf16[4,192,768]{2,1,0:T(8,128)(2,1)} %get-tuple-element.241), channel_id=1, source_target_pairs={{0,8},{8,0},{1,9},{9,1},{2,10},{10,2},{3,11},{11,3},{4,12},{12,4},... | collective-permute-start | bytes 3538952 | tf_op jit(solution)/shard_map/ppermute | solution.py:827
  359.2 38.7 %collective-permute-start.31 = (bf16[3,48,3072]{2,1,0:T(8,128)(2,1)}, bf16[3,48,3072]{2,1,0:T(8,128)(2,1)S(1)}, u32[]{:S(2)}, u32[]{:S(2)}) collective-permute-start(bf16[3,48,3072]{2,1,0:T(8,128)(2,1)} %get-tuple-element.285), channel_id=1, source_target_pairs={{0,8},{8,0},{1,9},{9,1},{2,10},{10,2},{3,11},{11,3},{4,12},{12,4},... | collective-permute-start | bytes 2654216 | tf_op jit(solution)/shard_map/ppermute | solution.py:827
  360.3 29.4 %collective-permute-start.30 = (bf16[96,3200]{1,0:T(8,128)(2,1)}, bf16[96,3200]{1,0:T(8,128)(2,1)}, u32[]{:S(2)}, u32[]{:S(2)}) collective-permute-start(bf16[96,3200]{1,0:T(8,128)(2,1)} %get-tuple-element.262), channel_id=1, source_target_pairs={{0,18},{2,16},{16,2},{18,0},{1,19},{3,17},{17,3},{19,1},{4,22},{6,... | collective-permute-start | bytes 1843208 | tf_op jit(solution)/shard_map/ppermute | solution.py:847
  406.4 18.0 %collective-permute-start.37 = (bf16[48,3072]{1,0:T(8,128)(2,1)}, bf16[48,3072]{1,0:T(8,128)(2,1)S(1)}, u32[]{:S(2)}, u32[]{:S(2)}) collective-permute-start(bf16[48,3072]{1,0:T(8,128)(2,1)} %get-tuple-element.304), channel_id=1, source_target_pairs={{0,6},{2,4},{4,2},{6,0},{1,7},{3,5},{5,3},{7,1},{8,14},{10,12},{12... | collective-permute-start | bytes 884744 | tf_op jit(solution)/shard_map/ppermute | solution.py:847
  413.5 17.3 %collective-permute-start.39 = (bf16[192,768]{1,0:T(8,128)(2,1)S(1)}, bf16[192,768]{1,0:T(8,128)(2,1)S(1)}, u32[]{:S(2)}, u32[]{:S(2)}) collective-permute-start(bf16[192,768]{1,0:T(8,128)(2,1)S(1)} %copy-done.33), channel_id=1, source_target_pairs={{0,4},{2,6},{4,0},{6,2},{1,5},{3,7},{5,1},{7,3},{8,12},{10,14},{12... | collective-permute-start | bytes 884744 | tf_op jit(solution)/shard_map/ppermute | solution.py:847
  418.0 18.4 %collective-permute-start.40 = (bf16[192,768]{1,0:T(8,128)(2,1)S(1)}, bf16[192,768]{1,0:T(8,128)(2,1)S(1)}, u32[]{:S(2)}, u32[]{:S(2)}) collective-permute-start(bf16[192,768]{1,0:T(8,128)(2,1)S(1)} %copy-done.32), channel_id=1, source_target_pairs={{0,6},{2,4},{4,2},{6,0},{1,7},{3,5},{5,3},{7,1},{8,14},{10,12},{12... | collective-permute-start | bytes 884744 | tf_op jit(solution)/shard_map/ppermute | solution.py:847
  (59 other events, 747.4 us)
